TPU v7x, 32 devices: a whole 2x2x4 slice. The times are simulated.
32 devices in a mesh: gx: 8 (over y, x, core), pa: 4 (over z).
Axes of the slice: x: 2, y: 2, z: 4, core: 2. Of those that a mesh axis runs over, the one named last changes fastest.
Arguments:
- block_inverses: float32 [32, 32, 128, 128], P('gx', 'pa'), parts along dimension 1, may hold values from -0.25 to 1.07, as said below
- residual: float32 [32, 32, 128], P('gx', 'pa'), parts along dimension 1, may hold values from -0.3 to 0.3
- material: int32 [32, 32, 128], P('gx', 'pa'), parts along dimension 1, may hold values from 0 to 3
- fin_mask: int32 [32, 32, 128], P('gx', 'pa'), parts along dimension 1, may hold values 0 or 1
- phase_mask: int32 [32, 32, 128], P('gx', 'pa'), parts along dimension 1, may hold values 0 or 1
- k_table: float32 [4], replicated, may hold values from 0.95 to 1.05
Outputs:
- correction: float32 [32, 32, 128], P('gx', 'pa'), parts along dimension 1
- enthalpy_step: float32 [32, 32, 128], P('gx', 'pa'), parts along dimension 1
There are 4 independent parts, one for each index of `pa`. A program takes and returns all parts, laid end to end along the dimension named above; an argument that names none is the same for every part. Nothing has to cross between parts.
Inputs may be any that keep to these rules, and one draw needn't show every extreme that they name: Each block block_inverses[i, t] is a symmetric matrix.
All inputs are finite; a program needn't handle non-finite values. No bound on the sum of `fin_mask` or of `phase_mask` on one device may be relied on, other than what follows from the above.
Results may differ from a plain program's by a relative error of at most 0.0003.
Values sent between devices are 32-bit elements; how exact they have to be, the bound alone decides.
No kernel may reach another device: no remote copies, remote signals or barrier semaphores. Data moves between devices by JAX's collectives and lax.ppermute only.
A program may use at most 128 MiB of HBM per device.

v0:
```python
import jax
import jax.numpy as jnp
from jax import lax
from jax.sharding import PartitionSpec as P


def passed_along(block, axis, distance):
    devices = range(lax.axis_size(axis))
    route = [(i - distance, i) for i in devices if i - distance in devices]
    return lax.ppermute(block, axis, route)


def apply_block(pivot_entries, vector):
    return jnp.einsum("tab,tb->ta", pivot_entries, vector, precision=lax.Precision.HIGHEST)


def apply_transposed(pivot_entries, vector):
    return jnp.einsum("tba,tb->ta", pivot_entries, vector, precision=lax.Precision.HIGHEST)


def forward_pass(block_inverses, residual, face_cond, entering):
    state_vec = entering
    results = []
    for line_position in range(block_inverses.shape[0]):
        state_vec = apply_block(
            block_inverses[line_position],
            residual[line_position] + face_cond[line_position] * state_vec,
        )
        results.append(state_vec)
    return jnp.stack(results)


def backward_pass(block_inverses, forward_vals, face_cond, arriving):
    carried = arriving
    results = [None] * block_inverses.shape[0]
    for line_position in reversed(range(block_inverses.shape[0])):
        solved = forward_vals[line_position] + apply_block(block_inverses[line_position], carried)
        results[line_position] = solved
        carried = face_cond[line_position] * solved
    return (jnp.stack(results), carried)


def on_device(block_inverses, residual, material, fin_mask, phase_mask, k_table):
    block_count, tile_count, cell_count = residual.shape
    material_codes = jnp.arange(k_table.shape[0], dtype=jnp.int32)
    conduct = jnp.sum(
        jnp.where(material[..., None] == material_codes, k_table, jnp.zeros_like(k_table)), axis=-1
    )
    before = passed_along(conduct[block_count - 1], "gx", 1)
    earlier = jnp.concatenate([before[None], conduct[: block_count - 1]], axis=0)
    face_cond = (
        2.0 * conduct * earlier / (conduct + earlier) * (0.9 + 0.1 * fin_mask.astype(jnp.float32))
    )
    zero_vector = jnp.zeros((tile_count, cell_count), jnp.float32)
    scaled_rows = block_inverses * face_cond[:, :, None, :]
    matrix_product = scaled_rows[0]
    for line_position in range(1, block_count):
        matrix_product = jnp.einsum(
            "hzp,hpn->hzn",
            scaled_rows[line_position],
            matrix_product,
            precision=lax.Precision.HIGHEST,
        )
    local_vals = forward_pass(block_inverses, residual, face_cond, zero_vector)
    tail_vec = local_vals[block_count - 1]
    all_maps, all_tails = (
        lax.all_gather(matrix_product[None], "gx", axis=0, tiled=True),
        lax.all_gather(tail_vec[None], "gx", axis=0, tiled=True),
    )
    own_index = lax.axis_index("gx")
    processor_total = all_maps.shape[0]

    def fold_forward(line_position, state_vec):
        moved = apply_block(all_maps[line_position], state_vec) + all_tails[line_position]
        return jnp.where(line_position < own_index, moved, state_vec)

    entering = lax.fori_loop(0, processor_total, fold_forward, zero_vector, unroll=8)
    forward_vals = forward_pass(block_inverses, residual, face_cond, entering)
    _, leaving = backward_pass(block_inverses, forward_vals, face_cond, zero_vector)
    all_leaving = lax.all_gather(leaving[None], "gx", axis=0, tiled=True)

    def backward_accumulate(offset, state_vec):
        line_position = processor_total - 1 - offset
        moved = apply_transposed(all_maps[line_position], state_vec) + all_leaving[line_position]
        return jnp.where(line_position > own_index, moved, state_vec)

    arriving = lax.fori_loop(0, processor_total, backward_accumulate, zero_vector, unroll=8)
    correction, _ = backward_pass(block_inverses, forward_vals, face_cond, arriving)
    enthalpy_step = correction * (1.0 + 2.0 * phase_mask.astype(jnp.float32))
    return (correction, enthalpy_step)


def solution(mesh):
    return jax.shard_map(
        on_device,
        mesh=mesh,
        in_specs=(
            P("gx", "pa", None, None),
            P("gx", "pa", None),
            P("gx", "pa", None),
            P("gx", "pa", None),
            P("gx", "pa", None),
            P(),
        ),
        out_specs=(P("gx", "pa", None), P("gx", "pa", None)),
        check_vma=False,
    )
```

profile of v0, /device:TPU:0, one launch (start us, length us, event | category | flops | bytes accessed | tf_op | source)
XLA Modules:
  0.0 100.5 jit_solution(474527091113292094)
XLA Ops:
  7.2 0.8 select_reduce_fusion
  8.0 2.3 %collective-permute-start = (f32[8,128]{1,0:T(8,128)S(1)}, f32[8,128]{1,0:T(8,128)S(1)}, u32[]{:S(2)}, u32[]{:S(2)}) collective-permute-start(f32[8,128]{1,0:T(8,128)S(1)} %slice_bitcast_fusion.12), channel_id=1, source_target_pairs={{0,4},{4,8},{8,12},{12,16},{16,20},{20,24},{24,28},{1,5},{5,9},{9,... | collective-permute-start | bytes 12296 | tf_op jit(solution)/shard_map/ppermute | solution.py:10
  10.4 0.8 collective-permute-done
  11.9 1.9 %broadcast_multiply_fusion = f32[4,8,128,128]{3,2,1,0:T(8,128)S(1)} fusion(f32[4,8,128,128]{3,2,1,0:T(8,128)} %param.6, f32[4,8,128]{2,1,0:T(8,128)S(1)} %add_multiply_fusion.1), kind=kLoop, calls=%fused_computation | loop fusion | flops 524288 | bytes 4210688 | tf_op jit(solution)/shard_map/mul | solution.py:55
  15.2 1.5 %fusion.2 = f32[8,128,128]{2,1,0:T(8,128)} fusion(f32[8,128,128]{2,1,0:T(8,128)S(1)} %fusion.1, f32[4,8,128,128]{3,2,1,0:T(8,128)S(1)} %broadcast_multiply_fusion), kind=kOutput, calls=%fused_computation.7 | convolution fusion | flops 201326592 | bytes 1572864 | tf_op jit(solution)/shard_map/hzp,hpn->hzn/dot_general | solution.py:58
  16.8 0.9 fusion.5
  17.7 0.9 fusion.33
  18.6 0.9 fusion.25
  19.6 1.0 fusion.17
  20.5 0.9 fusion.9
  21.5 13.4 %all-gather.1 = f32[64,128]{1,0:T(8,128)S(1)} all-gather(f32[8,128]{1,0:T(8,128)S(1)} %bitcast.349), channel_id=3, replica_groups=mesh['gx'=8,'pa'=4] {'gx'}, dimensions={0}, use_global_device_ids=true | all-gather | bytes 36864 | tf_op jit(solution)/shard_map/all_gather | solution.py:68
  34.8 23.2 %all-gather.5.cloned.1.call-done = f32[64,128,128]{2,1,0:T(8,128)} async-done(((f32[8,128,128]{2,1,0:T(8,128)}), f32[64,128,128]{2,1,0:T(8,128)}) %all-gather.5.cloned.1.call-update) | async-done | bytes 4194320 | tf_op jit(solution)/shard_map/all_gather | solution.py:67
  58.0 2.1 %fusion.72 = f32[8,1,128]{2,1,0:T(1,128)S(1)} fusion(f32[64,128,128]{2,1,0:T(8,128)} %all-gather.5.cloned.1.call-done, f32[8,128,1]{1,2,0:T(1,128)S(1)} %bitcast.312), kind=kOutput, calls=%fused_computation.119 | convolution fusion | flops 1572864 | bytes 4202496 | tf_op jit(solution)/shard_map/eval_jaxpr/tab,tb->ta/dot_general | solution.py:14
  60.1 2.0 %fusion.73 = f32[8,1,128]{2,1,0:T(1,128)S(1)} fusion(f32[64,128,128]{2,1,0:T(8,128)} %all-gather.5.cloned.1.call-done, f32[8,128,1]{1,2,0:T(1,128)S(1)} %bitcast.326), kind=kOutput, calls=%fused_computation.120 | convolution fusion | flops 1572864 | bytes 4202496 | tf_op jit(solution)/shard_map/eval_jaxpr/tab,tb->ta/dot_general | solution.py:14
  62.1 2.0 %fusion.74 = f32[8,1,128]{2,1,0:T(1,128)S(1)} fusion(f32[64,128,128]{2,1,0:T(8,128)} %all-gather.5.cloned.1.call-done, f32[8,128,1]{1,2,0:T(1,128)S(1)} %bitcast.329), kind=kOutput, calls=%fused_computation.121 | convolution fusion | flops 1572864 | bytes 4202496 | tf_op jit(solution)/shard_map/eval_jaxpr/tab,tb->ta/dot_general | solution.py:14
  64.1 0.9 fusion.75
  65.0 0.9 fusion.76
  66.0 0.9 fusion.77
  66.9 0.9 fusion.78
  67.9 0.9 fusion.79
  68.8 0.9 fusion.31
  69.7 0.9 fusion.23
  70.7 0.9 fusion.15
  71.6 0.9 fusion.7
  72.6 0.9 fusion.13
  73.5 0.9 fusion.21
  74.5 0.9 fusion.29
  75.4 9.2 %all-gather.2 = f32[64,128]{1,0:T(8,128)S(1)} all-gather(f32[8,128]{1,0:T(8,128)S(1)} %add_multiply_fusion.2), channel_id=4, replica_groups=mesh['gx'=8,'pa'=4] {'gx'}, dimensions={0}, use_global_device_ids=true | all-gather | bytes 36864 | tf_op jit(solution)/shard_map/all_gather | solution.py:80
  89.2 0.9 fusion.3
  90.2 0.9 fusion.11
  91.1 0.9 fusion.19
  92.0 0.9 fusion.27
  (56 shorter events, 7.5 us)
Async XLA Ops:
  7.2 50.9 %all-gather.5.cloned.1.call-start = ((), (), s32[]{:S(2)}) async-start(), calls=%async_computation | async-start | bytes 4718592 | tf_op jit(solution)/shard_map/all_gather | solution.py:67
  8.0 3.2 %collective-permute-start = (f32[8,128]{1,0:T(8,128)S(1)}, f32[8,128]{1,0:T(8,128)S(1)}, u32[]{:S(2)}, u32[]{:S(2)}) collective-permute-start(f32[8,128]{1,0:T(8,128)S(1)} %slice_bitcast_fusion.12), channel_id=1, source_target_pairs={{0,4},{4,8},{8,12},{12,16},{16,20},{20,24},{24,28},{1,5},{5,9},{9,... | collective-permute-start | bytes 12296 | tf_op jit(solution)/shard_map/ppermute | solution.py:10
  11.9 4.8 %copy-start.1 = (f32[4,8,128,128]{3,2,1,0:T(8,128)S(1)}, f32[4,8,128,128]{3,2,1,0:T(8,128)}, u32[]{:S(2)}) copy-start(f32[4,8,128,128]{3,2,1,0:T(8,128)} %param.6) | copy-start | bytes 6291460
  11.9 5.8 %copy-start.2 = (f32[4,8,128]{2,1,0:T(8,128)S(1)}, f32[4,8,128]{2,1,0:T(8,128)}, u32[]{:S(2)}) copy-start(f32[4,8,128]{2,1,0:T(8,128)} %param.7) | copy-start | bytes 49156
  58.0 6.1 %copy-start = (f32[64,128,128]{2,1,0:T(8,128)S(1)}, f32[64,128,128]{2,1,0:T(8,128)}, u32[]{:S(2)}) copy-start(f32[64,128,128]{2,1,0:T(8,128)} %all-gather.5.cloned.1.call-done) | copy-start | bytes 12582916
  86.9 6.1 %copy-start.3 = (s32[4,8,128]{2,1,0:T(8,128)S(1)}, s32[4,8,128]{2,1,0:T(8,128)}, u32[]{:S(2)}) copy-start(s32[4,8,128]{2,1,0:T(8,128)} %param.10) | copy-start | bytes 49156
Sparse Core Ops, SparseCore 0:
  16.8 41.1 all-gather.4
where the time goes:
time: 101 us; the launch traced here: 100 us
  matrix products  32.9 us (33%)
  waiting for transfers between devices  24 us (24%)
  blocking collectives  22.6 us (22%)
  between operations  14.2 us (14%)
  other arithmetic  4.31 us (4%)
  starting transfers between devices  2.38 us (2%)
    dot_general x24, matrix products, apply_block(): jnp.einsum('tab,tb->ta', pivot_entries, vector, precision=lax.Precision.H...  25.7 us
    all_gather x1, waiting for transfers between devices, on_device(): lax.all_gather(matrix_product[None], 'gx', axis=0, tiled=True)  23.2 us
    all_gather x1, blocking collectives, on_device(): lax.all_gather(tail_vec[None], 'gx', axis=0, tiled=True)  13.4 us
    all_gather x1, blocking collectives, on_device(): all_leaving = lax.all_gather(leaving[None], 'gx', axis=0, tiled=True)  9.25 us
    dot_general x8, matrix products, apply_transposed(): jnp.einsum('tba,tb->ta', pivot_entries, vector, precision=lax.Precision.H...  4.48 us
    dot_general x3, matrix products, on_device(): jnp.einsum('hzp,hpn->hzn', scaled_rows[line_position], matrix_product, pr...  2.81 us
    ppermute x1, starting transfers between devices, passed_along(): return lax.ppermute(block, axis, route)  2.35 us
  transfers between devices with their start and end apart: 2, of which 2 were waited for; matrix products, arithmetic and copies ran while one was open for 5% of the time, Pallas kernels for 0%

commit v1 on v0

v1 whole, which is shorter than its diff:
```python
import functools

import jax
import jax.numpy as jnp
from jax import lax
from jax.experimental import pallas as pl
from jax.experimental.pallas import tpu as pltpu
from jax.sharding import PartitionSpec as P

BF16 = jnp.bfloat16
F32 = jnp.float32
ROWS = 8
AXIS = "gx"


def split(x):
    high = x.astype(BF16)
    return high, (x - high.astype(F32)).astype(BF16)


def mul(left, right):
    lh, ll = split(left)
    rh, rl = split(right)
    lhs = jnp.concatenate([lh, ll], axis=1)
    rhs = jnp.concatenate(
        [jnp.concatenate([rh, rl], axis=1), jnp.concatenate([rh, jnp.zeros_like(rl)], axis=1)], axis=0
    )
    both = jnp.dot(lhs, rhs, preferred_element_type=F32)
    width = right.shape[1]
    return both[:, :width] + both[:, width:]


def mul_t(left, right):
    lh, ll = split(left)
    rh, rl = split(right)
    lhs = jnp.concatenate([lh, ll], axis=1)
    rhs = jnp.concatenate(
        [jnp.concatenate([rh, rh], axis=1), jnp.concatenate([rl, jnp.zeros_like(rl)], axis=1)], axis=0
    )
    both = lax.dot_general(lhs, rhs, (((1,), (1,)), ((), ())), preferred_element_type=F32)
    width = right.shape[0]
    return both[:, :width] + both[:, width:]


def face(conduct, earlier, fin_factor):
    return 2.0 * conduct * earlier / (conduct + earlier) * fin_factor


def conductivity(material, k_ref):
    total = jnp.zeros(material.shape, F32)
    for code in range(k_ref.shape[0]):
        total = total + jnp.where(material == code, k_ref[code], 0.0)
    return total


def fin_factor(fin):
    return 0.9 + 0.1 * fin.astype(F32)


def eye_mask(size):
    return lax.broadcasted_iota(jnp.int32, (size, size), 0) == lax.broadcasted_iota(
        jnp.int32, (size, size), 1
    )


def times(matrix, row, eye):
    column = jnp.sum(matrix * row, axis=1, keepdims=True)
    return jnp.sum(jnp.where(eye, column, 0.0), axis=0, keepdims=True)


def times_t(matrix, row, eye):
    column = jnp.sum(jnp.where(eye, row, 0.0), axis=1, keepdims=True)
    return jnp.sum(matrix * column, axis=0, keepdims=True)


def stack_rows(rows, cells):
    at = lax.broadcasted_iota(jnp.int32, (ROWS, cells), 0)
    out = jnp.zeros((ROWS, cells), F32)
    for place, row in enumerate(rows):
        out = jnp.where(at == place, jnp.broadcast_to(row, (ROWS, cells)), out)
    return out


def products(wide, source, faces, g_of, out_ref, ends):
    cells = wide[0].shape[1]
    tiles = range(len(wide))
    total = list(wide)
    for i in range(1, len(source)):
        for j in tiles:
            scaled = wide[j] * faces[i][j : j + 1]
            sh, sl = split(scaled[:cells])
            vh, vl = split(scaled[cells:] + stack_rows([source[i][j : j + 1]], cells))
            gh, gl = split(g_of(i, j))
            zero = jnp.zeros_like(gl)
            both = jnp.dot(
                jnp.concatenate([jnp.concatenate([sh, sl], axis=1), jnp.concatenate([vh, vl], axis=1)], axis=0),
                jnp.concatenate([jnp.concatenate([gh, gl], axis=1), jnp.concatenate([gh, zero], axis=1)], axis=0),
                preferred_element_type=F32,
            )
            wide[j] = both[:, :cells] + both[:, cells:]
            wh, wl = split(wide[j])
            both = lax.dot_general(
                jnp.concatenate([wh, wl], axis=1),
                jnp.concatenate([jnp.concatenate([sh, sh], axis=1), jnp.concatenate([sl, zero], axis=1)], axis=0),
                (((1,), (1,)), ((), ())),
                preferred_element_type=F32,
            )
            total[j] = total[j] + (both[:, :cells] + both[:, cells:])
    for j in tiles:
        out_ref[j, 0:cells] = wide[j][:cells]
        out_ref[j, cells : 2 * cells] = total[j][:cells]
        out_ref[j, 2 * cells :] = stack_rows(
            [wide[j][cells : cells + 1], total[j][cells : cells + 1]] + [end[j : j + 1] for end in ends], cells
        )


def first_kernel(k_hbm, mat_hbm, fin_hbm, res_hbm, g_hbm, out_ref, coef_ref, g_ref, k_ref, ints, sems):
    blocks, tiles, cells = res_hbm.shape
    half = tiles // 2
    lower = lax.axis_index(AXIS) % 2 == 1
    base = jnp.where(lower, 0, half)
    small = [
        pltpu.make_async_copy(k_hbm, k_ref, sems.at[0]),
        pltpu.make_async_copy(mat_hbm, ints.at[0], sems.at[1]),
        pltpu.make_async_copy(fin_hbm, ints.at[1], sems.at[2]),
        pltpu.make_async_copy(res_hbm, coef_ref.at[pl.ds(0, blocks)], sems.at[3]),
    ]
    places = [base + j for j in range(half)] + [half - base + j for j in range(half)]
    large = [
        pltpu.make_async_copy(g_hbm.at[:, at], g_ref.at[:, at], sems.at[4 + n])
        for n, at in enumerate(places)
    ]
    for copy in small + large:
        copy.start()
    for copy in small:
        copy.wait()
    conduct = [conductivity(ints[0, i], k_ref) for i in range(blocks)]
    factor = [fin_factor(ints[1, i]) for i in range(blocks)]
    faces = [None] + [face(conduct[i], conduct[i - 1], factor[i]) for i in range(1, blocks)]
    ends = [conduct[0], conduct[-1], factor[0]]
    for n, row in enumerate(faces[1:] + ends):
        coef_ref[blocks + n] = row

    def pick(x):
        return jnp.where(lower, x[:half], x[half:])

    source = [pick(coef_ref[i]) for i in range(blocks)]
    eye = eye_mask(cells)
    wide = []
    for j in range(half):
        large[j].wait()
        g0 = g_ref[0, base + j]
        wide.append(jnp.concatenate([g0, stack_rows([times(g0, source[0][j : j + 1], eye)], cells)], axis=0))
    products(
        wide, source, [None] + [pick(f) for f in faces[1:]], lambda i, j: g_ref[i, base + j], out_ref,
        [pick(end) for end in ends],
    )
    for copy in large[half:]:
        copy.wait()


def second_kernel(coef_ref, g_ref, out_ref):
    blocks, tiles, cells = g_ref.shape[:3]
    half = tiles // 2
    upper = lax.axis_index(AXIS) % 2 == 1
    base = jnp.where(upper, half, 0)

    def pick(n):
        return jnp.where(upper, coef_ref[n, half:], coef_ref[n, :half])

    source = [pick(i) for i in range(blocks)]
    faces = [None] + [pick(blocks + i) for i in range(blocks - 1)]
    eye = eye_mask(cells)
    wide = []
    for j in range(half):
        g0 = g_ref[0, base + j]
        wide.append(jnp.concatenate([g0, stack_rows([times(g0, source[0][j : j + 1], eye)], cells)], axis=0))
    products(
        wide, source, faces, lambda i, j: g_ref[i, base + j], out_ref,
        [pick(2 * blocks - 1 + n) for n in range(3)],
    )


def response_kernel(coef_ref, keep_ref, got_ref, give_ref, gain_ref, g_ref, out_ref, const_ref):
    blocks, tiles, cells = g_ref.shape[:3]
    half = tiles // 2
    is_second = lax.axis_index(AXIS) % 2 == 1
    base = jnp.where(is_second, half, 0)
    eye = jnp.where(eye_mask(cells), 1.0, 0.0)

    def reorder(x):
        return jnp.where(is_second, jnp.concatenate([x[half:], x[:half]], axis=0), x)

    source = [reorder(coef_ref[i]) for i in range(blocks)]
    faces = [None] + [reorder(coef_ref[blocks + i]) for i in range(blocks - 1)]
    nothing = jnp.zeros((cells, cells), F32)
    for group in range(2):
        own_ref, other_ref = (keep_ref, got_ref) if group == 0 else (give_ref, gain_ref)
        start = base if group == 0 else half - base
        lead, tail, values = {}, {}, {}
        for j in range(half):
            own, other = own_ref[j], other_ref[j]
            first = jnp.where(is_second, other, own)
            last = jnp.where(is_second, own, other)
            va, vb = first[2 * cells :], last[2 * cells :]
            between = face(vb[2:3], va[3:4], vb[4:5])
            scaled = jnp.concatenate([first[:cells], stack_rows([va[0:1]], cells)], axis=0) * between
            back = mul(scaled, last[cells : 2 * cells])
            back_const = back[cells:] + stack_rows([vb[1:2]], cells)
            tail[j] = jnp.concatenate(
                [
                    jnp.where(is_second, 0.0, back[:cells] * between),
                    jnp.where(is_second, eye, last[:cells].T * between),
                    jnp.where(is_second, 0.0, back_const * between),
                ],
                axis=0,
            )
            lead[j] = jnp.concatenate(
                [
                    jnp.where(is_second, scaled[:cells], eye),
                    jnp.where(is_second, scaled[cells:], 0.0)
                    + stack_rows([source[0][group * half + j : group * half + j + 1]], cells),
                ],
                axis=0,
            )
        for i in range(blocks):
            for j in range(half):
                values[i, j] = mul(lead[j], g_ref[i, start + j])
                if i < blocks - 1:
                    at = group * half + j
                    scaled = values[i, j] * faces[i + 1][at : at + 1]
                    below = scaled[cells:] + stack_rows([source[i + 1][at : at + 1]], cells)
                    lead[j] = jnp.concatenate([scaled[:cells], below], axis=0)
        for i in reversed(range(blocks)):
            for j in range(half):
                moved = mul(tail[j], g_ref[i, start + j])
                add = jnp.concatenate([values[i, j][:cells], nothing, values[i, j][cells:]], axis=0)
                solved = moved + add
                out_ref[i, start + j] = solved[: 2 * cells]
                const_ref[i, start + j] = solved[2 * cells :]
                if i:
                    at = group * half + j
                    tail[j] = solved * faces[i][at : at + 1]


def merge_kernel(keep_ref, got_ref, *out_refs):
    half, height, cells = keep_ref.shape
    here = lax.axis_index(AXIS)
    is_second = here % 2 == 1
    chip = (here % (2 * half)) // 2
    for d in range(half):
        tile = chip ^ d
        keep, got = keep_ref[tile], got_ref[tile]
        first = jnp.where(is_second, got, keep)
        second = jnp.where(is_second, keep, got)
        va, vb = first[2 * cells :], second[2 * cells :]
        between = face(vb[2:3], va[3:4], vb[4:5])
        scaled = jnp.concatenate([first[:cells], stack_rows([va[0:1]], cells)], axis=0) * between
        moved = mul(scaled, second[:cells])
        squared = mul(scaled, second[cells : 2 * cells])
        lower = squared[cells:] + stack_rows([vb[1:2]], cells)
        squared = jnp.concatenate([squared[:cells], lower], axis=0)
        total = mul_t(squared, scaled[:cells])
        out_ref = out_refs[d]
        out_ref[0:cells] = moved[:cells]
        out_ref[cells : 2 * cells] = first[cells : 2 * cells] + total[:cells]
        out_ref[2 * cells :] = stack_rows(
            [
                moved[cells : cells + 1] + vb[0:1],
                total[cells : cells + 1] + va[1:2],
                va[2:3],
                vb[3:4],
                va[4:5],
            ],
            cells,
        )


def chain_kernel(with_edge, *refs):
    refs, nodes = refs[:-1], refs[-1]
    if with_edge:
        edge_ref, refs = refs[0], refs[1:]
    count, height, cells = nodes.shape
    refs, out_refs, ends = refs[:count], refs[count:-1], refs[-1]
    chip = (lax.axis_index(AXIS) % (2 * count)) // 2
    for d in range(count):
        nodes[chip ^ d] = refs[d][...]
    eye = eye_mask(cells)
    vectors = [nodes[k, 2 * cells :] for k in range(count)]
    faces = [None] + [
        face(vectors[k][2:3], vectors[k - 1][3:4], vectors[k][4:5]) for k in range(1, count)
    ]
    entering, arriving = [None] * count, [None] * count
    leaving = vectors[0][0:1]
    if with_edge:
        entering[0], arriving[-1] = edge_ref[0:1], edge_ref[1:2]
        leaving = leaving + times_t(nodes[0, 0:cells], entering[0], eye)
    for k in range(1, count):
        entering[k] = faces[k] * leaving
        if k < count - 1:
            leaving = vectors[k][0:1] + times_t(nodes[k, 0:cells], entering[k], eye)
    heads = [None] + [
        vectors[k][1:2] + times(nodes[k, cells : 2 * cells], entering[k], eye) for k in range(1, count)
    ]
    for k in reversed(range(1, count)):
        head = heads[k]
        if arriving[k] is not None:
            head = head + times(nodes[k, 0:cells], arriving[k], eye)
        arriving[k - 1] = faces[k] * head
    zero = jnp.zeros((1, cells), F32)
    for k in range(count):
        ends[k] = stack_rows(
            [zero if entering[k] is None else entering[k], zero if arriving[k] is None else arriving[k]],
            cells,
        )
    for d in range(count):
        out_refs[d][...] = ends[chip ^ d]


def order_kernel(*refs):
    out_ref = refs[-1]
    count = out_ref.shape[0]
    chip = (lax.axis_index(AXIS) % (2 * count)) // 2
    for d in range(count):
        out_ref[chip ^ d] = refs[d][...]


def finish_kernel(mine_ref, theirs_ref, phase_ref, out_ref, const_ref, corr_ref, step_ref, ends_ref):
    blocks, tiles, cells = corr_ref.shape
    half = tiles // 2
    is_second = lax.axis_index(AXIS) % 2 == 1
    ends_ref[:half] = jnp.where(is_second, theirs_ref[...], mine_ref[...])
    ends_ref[half:] = jnp.where(is_second, mine_ref[...], theirs_ref[...])
    eye = eye_mask(cells)
    for j in range(tiles):
        up = jnp.sum(jnp.where(eye, ends_ref[j, 0:1], 0.0), axis=1, keepdims=True)
        down = jnp.sum(jnp.where(eye, ends_ref[j, 1:2], 0.0), axis=1, keepdims=True)
        for i in range(blocks):
            both = out_ref[i, j, 0:cells] * up + out_ref[i, j, cells : 2 * cells] * down
            solved = const_ref[i, j, 0:1] + jnp.sum(both, axis=0, keepdims=True)
            corr_ref[i, j : j + 1] = solved
            step_ref[i, j : j + 1] = solved * (1.0 + 2.0 * phase_ref[i, j : j + 1].astype(F32))


VMEM = pl.BlockSpec(memory_space=pltpu.VMEM)
HBM = pl.BlockSpec(memory_space=pltpu.HBM)
LIMIT = pltpu.CompilerParams(vmem_limit_bytes=16 << 20)


def cost(flops, moved):
    return pl.CostEstimate(flops=flops, bytes_accessed=moved, transcendentals=0)


def send(x, distance):
    return lax.ppermute(x, AXIS, [(i, i ^ distance) for i in range(lax.axis_size(AXIS))])


def exact(left, right):
    return jnp.dot(left, right, precision=lax.Precision.HIGHEST)


def outer_edge(nodes, devices):
    cells = nodes[0].shape[-1]

    def parts(node):
        return node[:cells], node[cells : 2 * cells], node[2 * cells :]

    def join(first, second):
        (ma, qa, va), (mb, qb, vb) = parts(first), parts(second)
        between = face(vb[2], va[3], vb[4])
        scaled, shift = ma * between, va[0] * between
        q = qa + exact(exact(scaled, qb), scaled.T)
        tail = exact(shift, mb) + vb[0]
        lead = va[1] + exact(scaled, exact(qb, shift) + vb[1])
        rest = jnp.zeros((ROWS - 5, cells), F32)
        rows = jnp.stack([tail, lead, va[2], vb[3], va[4]])
        return jnp.concatenate([exact(scaled, mb), q, rows, rest], axis=0)

    groups = lax.axis_size(AXIS) // devices
    whole = functools.reduce(join, [nodes[k] for k in range(nodes.shape[0])])
    members = [[g * devices + q for g in range(groups)] for q in range(devices)]
    every = lax.all_gather(whole, AXIS, axis=0, axis_index_groups=members)
    split_up = [parts(every[g]) for g in range(groups)]
    faces = [face(b[2][2], a[2][3], b[2][4]) for a, b in zip(split_up[:-1], split_up[1:])]
    entering = [jnp.zeros((cells,), F32)]
    for g in range(groups - 1):
        m, _, v = split_up[g]
        entering.append(faces[g] * (exact(entering[g], m) + v[0]))
    arriving = [jnp.zeros((cells,), F32)]
    for g in reversed(range(1, groups)):
        m, q, v = split_up[g]
        arriving.append(faces[g - 1] * (exact(m, arriving[-1]) + exact(q, entering[g]) + v[1]))
    arriving.reverse()
    own = lax.axis_index(AXIS) // devices
    both = jnp.stack([jnp.stack(entering)[own], jnp.stack(arriving)[own]])
    return jnp.concatenate([both, jnp.zeros((ROWS - 2, cells), F32)], axis=0)


def on_device(block_inverses, residual, material, fin_mask, phase_mask, k_table):
    blocks, tiles, cells = residual.shape
    half = tiles // 2
    height = 2 * cells + ROWS
    map_bytes = 4 * height * cells

    map_shape = (half, height, cells)
    work = cost(24 * half * blocks * cells**3, 8 * half * blocks * cells**2)
    given = [pltpu.with_memory_space_constraint(x, pltpu.HBM) for x in (k_table, material, fin_mask, residual, block_inverses)]
    give, coef, inverses = pl.pallas_call(
        first_kernel,
        out_shape=(
            pltpu.VMEM(map_shape, F32),
            pltpu.VMEM((2 * blocks + 2, tiles, cells), F32),
            pltpu.VMEM(block_inverses.shape, F32),
        ),
        in_specs=[HBM] * 5,
        out_specs=(VMEM,) * 3,
        scratch_shapes=[
            pltpu.SMEM(k_table.shape, F32),
            pltpu.VMEM((2, blocks, tiles, cells), jnp.int32),
            pltpu.SemaphoreType.DMA((4 + tiles,)),
        ],
        compiler_params=LIMIT,
        cost_estimate=work,
    )(*given)
    got = send(give, 1)
    keep = pl.pallas_call(
        second_kernel,
        out_shape=jax.ShapeDtypeStruct(map_shape, F32),
        in_specs=[VMEM, VMEM],
        out_specs=VMEM,
        compiler_params=LIMIT,
        cost_estimate=work,
    )(coef, inverses)
    gain = send(keep, 1)
    responses, constants = pl.pallas_call(
        response_kernel,
        out_shape=(
            jax.ShapeDtypeStruct((blocks, tiles, 2 * cells, cells), F32),
            jax.ShapeDtypeStruct((blocks, tiles, ROWS, cells), F32),
        ),
        in_specs=[VMEM] * 6,
        out_specs=(VMEM, VMEM),
        compiler_params=LIMIT,
        cost_estimate=cost(48 * tiles * blocks * cells**3, 16 * tiles * blocks * cells**2),
    )(coef, keep, got, give, gain, inverses)
    node = jax.ShapeDtypeStruct((height, cells), F32)
    joined = pl.pallas_call(
        merge_kernel,
        out_shape=(node,) * half,
        in_specs=[VMEM, VMEM],
        out_specs=(VMEM,) * half,
        compiler_params=LIMIT,
        cost_estimate=cost(24 * half * cells**3, 3 * half * map_bytes),
    )(keep, got)
    arrived = [joined[0]] + [send(joined[d], 2 * d) for d in range(1, half)]
    grouped = lax.axis_size(AXIS) > tiles
    edge = []
    if grouped:
        chip = (lax.axis_index(AXIS) % tiles) // 2
        ordered = jnp.stack(arrived)[jnp.arange(half) ^ chip]
        edge = [outer_edge(ordered, tiles)]
    end = jax.ShapeDtypeStruct((ROWS, cells), F32)
    ends = pl.pallas_call(
        functools.partial(chain_kernel, grouped),
        out_shape=(end,) * half,
        in_specs=[VMEM] * (half + len(edge)),
        out_specs=(VMEM,) * half,
        scratch_shapes=[pltpu.VMEM((half, ROWS, cells), F32), pltpu.VMEM((half, height, cells), F32)],
        compiler_params=LIMIT,
        cost_estimate=cost(8 * half * cells**2, half * map_bytes),
    )(*edge, *arrived)
    ends = [ends[0]] + [send(ends[d], 2 * d) for d in range(1, half)]
    mine = pl.pallas_call(
        order_kernel,
        out_shape=jax.ShapeDtypeStruct((half, ROWS, cells), F32),
        in_specs=[VMEM] * half,
        out_specs=VMEM,
        compiler_params=LIMIT,
        cost_estimate=cost(0, 8 * half * ROWS * cells),
    )(*ends)
    theirs = send(mine, 1)
    shape = jax.ShapeDtypeStruct((blocks, tiles, cells), F32)
    return pl.pallas_call(
        finish_kernel,
        out_shape=(shape, shape),
        in_specs=[VMEM] * 5,
        out_specs=(VMEM, VMEM),
        scratch_shapes=[pltpu.VMEM((tiles, ROWS, cells), F32)],
        compiler_params=LIMIT,
        cost_estimate=cost(4 * blocks * tiles * cells**2, 8 * blocks * tiles * cells**2),
    )(mine, theirs, phase_mask, responses, constants)


def solution(mesh):
    return jax.shard_map(
        on_device,
        mesh=mesh,
        in_specs=(
            P("gx", "pa", None, None),
            P("gx", "pa", None),
            P("gx", "pa", None),
            P("gx", "pa", None),
            P("gx", "pa", None),
            P(),
        ),
        out_specs=(P("gx", "pa", None), P("gx", "pa", None)),
        check_vma=False,
    )
```

time: 101 us -> 28.5 us (0.28)
  matrix products: 32.9 us -> 0 us
  blocking collectives: 22.6 us -> 0 us
  waiting for transfers between devices: 24 us -> 9.93 us
  between operations: 14.2 us -> 0.7 us
  Pallas kernels: 0 us -> 8.93 us
  starting transfers between devices: 2.38 us -> 8.73 us
  other arithmetic: 4.31 us -> 0 us
    dot_general x35 -> x0, matrix products: 32.9 us -> none  [the longest x24 25.7 us: apply_block(): jnp.einsum('tab,tb->ta', pivot_entries, vector, precision=lax.Precision.H...]
    all_gather x1 -> x0, waiting for transfers between devices: 23.2 us -> none  [on_device(): lax.all_gather(matrix_product[None], 'gx', axis=0, tiled=True)]
    all_gather x2 -> x0, blocking collectives: 22.6 us -> none  [the longest x1 13.4 us: on_device(): lax.all_gather(tail_vec[None], 'gx', axis=0, tiled=True)]
    ppermute x1 -> x9, waiting for transfers between devices: 0.79 us -> 9.93 us  [send(): lax.ppermute(x, AXIS, [(i, i ^ distance) for i in range(lax.axis_size(AXI...]
    pallas_call x0 -> x7, Pallas kernels: none -> 8.93 us  [the longest x1 2.68 us: on_device(): pl.pallas_call(first_kernel, out_shape=(pltpu.VMEM(map_shape, F32), pltpu...]
    ppermute x1 -> x9, starting transfers between devices: 2.35 us -> 8.73 us  [send(): lax.ppermute(x, AXIS, [(i, i ^ distance) for i in range(lax.axis_size(AXI...]
    mul x10 -> x0, other arithmetic: 3.32 us -> none  [the longest x1 1.91 us: on_device(): scaled_rows = block_inverses * face_cond[:, :, None, :]]
  transfers between devices with their start and end apart: 2 -> 9, of which waited for: 2 -> 6; matrix products, arithmetic and copies ran while one was open for 5% -> 0% of each run, Pallas kernels for 0% -> 18%
where the time goes in v1:
time: 28.5 us; the launch traced here: 28.3 us
  waiting for transfers between devices  9.93 us (35%)
  Pallas kernels  8.93 us (31%)
  starting transfers between devices  8.73 us (31%)
  between operations  0.7 us (2%)
    ppermute x9, waiting for transfers between devices, send(): lax.ppermute(x, AXIS, [(i, i ^ distance) for i in range(lax.axis_size(AXI...  9.93 us
    ppermute x9, starting transfers between devices, send(): lax.ppermute(x, AXIS, [(i, i ^ distance) for i in range(lax.axis_size(AXI...  8.73 us
    pallas_call x1, Pallas kernels, on_device(): pl.pallas_call(first_kernel, out_shape=(pltpu.VMEM(map_shape, F32), pltpu...  2.68 us
    pallas_call x1, Pallas kernels, on_device(): pl.pallas_call(response_kernel, out_shape=(jax.ShapeDtypeStruct((blocks,...  2.6 us
    pallas_call x1, Pallas kernels, on_device(): pl.pallas_call(second_kernel, out_shape=jax.ShapeDtypeStruct(map_shape, F...  1.28 us
    pallas_call x1, Pallas kernels, on_device(): pl.pallas_call(finish_kernel, out_shape=(shape, shape), in_specs=[VMEM] *...  1.14 us
    pallas_call x1, Pallas kernels, on_device(): pl.pallas_call(functools.partial(chain_kernel, grouped), out_shape=(end,)...  0.63 us
    pallas_call x1, Pallas kernels, on_device(): pl.pallas_call(merge_kernel, out_shape=(node,) * half, in_specs=[VMEM, VM...  0.59 us
  transfers between devices with their start and end apart: 9, of which 6 were waited for; matrix products, arithmetic and copies ran while one was open for 0% of the time, Pallas kernels for 18%

profile of v1, /device:TPU:0, one launch (start us, length us, event | category | flops | bytes accessed | tf_op | source)
XLA Modules:
  0.0 28.3 jit_solution(13560654655783287408)
XLA Ops:
  0.6 2.7 %shard_map.77 = (f32[4,264,128]{2,1,0:T(8,128)S(1)}, f32[10,8,128]{2,1,0:T(8,128)S(1)}, f32[4,8,128,128]{3,2,1,0:T(8,128)S(1)}) custom-call(f32[4]{0:T(128)} %k_hbm.1, s32[4,8,128]{2,1,0:T(8,128)} %mat_hbm.1, s32[4,8,128]{2,1,0:T(8,128)} %fin_hbm.1, f32[4,8,128]{2,1,0:T(8,128)} %res_hbm.1, f32[4,8,128,128]{3,2,1,0:T(8,128)} %g_hbm.1), custom_call_target="tpu_custom_call" | custom-call | flops 805306368 | bytes 2097152 | tf_op jit(solution)/shard_map/pallas_call | solution.py:408
  3.3 0.5 %collective-permute-start = (f32[4,264,128]{2,1,0:T(8,128)S(1)}, f32[4,264,128]{2,1,0:T(8,128)S(1)}, u32[]{:S(2)}, u32[]{:S(2)}) collective-permute-start(f32[4,264,128]{2,1,0:T(8,128)S(1)} %get-tuple-element.17.give_ref), channel_id=1, source_target_pairs={{0,4},{4,0},{8,12},{12,8},{16,20},{20,16},{24,28},{28,24},{1,5},{5... | collective-permute-start | bytes 1622024 | tf_op jit(solution)/shard_map/ppermute | solution.py:355
  3.8 1.3 %shard_map.78.keep_ref = f32[4,264,128]{2,1,0:T(8,128)S(1)} custom-call(f32[10,8,128]{2,1,0:T(8,128)S(1)} %get-tuple-element.15.coef_ref, f32[4,8,128,128]{3,2,1,0:T(8,128)S(1)} %get-tuple-element.16.g_ref), custom_call_target="tpu_custom_call" | custom-call | flops 805306368 | bytes 2097152 | tf_op jit(solution)/shard_map/pallas_call | solution.py:426
  5.1 0.1 collective-permute-start.8
  5.3 0.1 collective-permute-done.got_ref
  5.4 0.6 %shard_map.79 = (f32[264,128]{1,0:T(8,128)S(1)}, f32[264,128]{1,0:T(8,128)S(1)}, f32[264,128]{1,0:T(8,128)S(1)}, f32[264,128]{1,0:T(8,128)S(1)}) custom-call(f32[4,264,128]{2,1,0:T(8,128)S(1)} %shard_map.78.keep_ref, f32[4,264,128]{2,1,0:T(8,128)S(1)} %collective-permute-done.got_ref), custom_call_target="tpu_custom_call" | custom-call | flops 201326592 | bytes 1622016 | tf_op jit(solution)/shard_map/pallas_call | solution.py:447
  6.0 2.9 %collective-permute-start.1 = (f32[264,128]{1,0:T(8,128)S(1)}, f32[264,128]{1,0:T(8,128)S(1)}, u32[]{:S(2)}, u32[]{:S(2)}) collective-permute-start(f32[264,128]{1,0:T(8,128)S(1)} %get-tuple-element.19), channel_id=1, source_target_pairs={{0,8},{4,12},{8,0},{12,4},{16,24},{20,28},{24,16},{28,20},{1,9},{5... | collective-permute-start | bytes 405512 | tf_op jit(solution)/shard_map/ppermute | solution.py:355
  8.9 1.5 %collective-permute-start.2 = (f32[264,128]{1,0:T(8,128)S(1)}, f32[264,128]{1,0:T(8,128)S(1)}, u32[]{:S(2)}, u32[]{:S(2)}) collective-permute-start(f32[264,128]{1,0:T(8,128)S(1)} %get-tuple-element.20), channel_id=1, source_target_pairs={{0,16},{4,20},{8,24},{12,28},{16,0},{20,4},{24,8},{28,12},{1,17},{... | collective-permute-start | bytes 405512 | tf_op jit(solution)/shard_map/ppermute | solution.py:355
  10.4 0.0 collective-permute-start.3
  10.5 2.5 %collective-permute-done.1.refs_1_ = f32[264,128]{1,0:T(8,128)S(1)} collective-permute-done((f32[264,128]{1,0:T(8,128)S(1)}, f32[264,128]{1,0:T(8,128)S(1)}, u32[]{:S(2)}, u32[]{:S(2)}) %collective-permute-start.1) | collective-permute-done | bytes 135200 | tf_op jit(solution)/shard_map/ppermute | solution.py:355
  13.0 4.2 %collective-permute-done.2.refs_2_ = f32[264,128]{1,0:T(8,128)S(1)} collective-permute-done((f32[264,128]{1,0:T(8,128)S(1)}, f32[264,128]{1,0:T(8,128)S(1)}, u32[]{:S(2)}, u32[]{:S(2)}) %collective-permute-start.2) | collective-permute-done | bytes 135200 | tf_op jit(solution)/shard_map/ppermute | solution.py:355
  17.2 0.0 collective-permute-done.3.refs_3_
  17.2 0.6 %shard_map.80 = (f32[8,128]{1,0:T(8,128)S(1)}, f32[8,128]{1,0:T(8,128)S(1)}, f32[8,128]{1,0:T(8,128)S(1)}, f32[8,128]{1,0:T(8,128)S(1)}) custom-call(f32[264,128]{1,0:T(8,128)S(1)} %get-tuple-element.18.refs_0_, f32[264,128]{1,0:T(8,128)S(1)} %collective-permute-done.1.refs_1_, f32[264,128]{1,0:T(8,128)S(1)} %collective-permute-done.2.refs_2_, ...), custom_call_target="tpu_custom_call" | custom-call | flops 524288 | bytes 540672 | tf_op jit(solution)/shard_map/pallas_call | solution.py:463
  17.8 1.3 %collective-permute-start.4 = (f32[8,128]{1,0:T(8,128)S(1)}, f32[8,128]{1,0:T(8,128)S(1)}, u32[]{:S(2)}, u32[]{:S(2)}) collective-permute-start(f32[8,128]{1,0:T(8,128)S(1)} %get-tuple-element.23), channel_id=1, source_target_pairs={{0,8},{4,12},{8,0},{12,4},{16,24},{20,28},{24,16},{28,20},{1,9},{5... | collective-permute-start | bytes 12296 | tf_op jit(solution)/shard_map/ppermute | solution.py:355
  19.1 0.8 %collective-permute-start.5 = (f32[8,128]{1,0:T(8,128)S(1)}, f32[8,128]{1,0:T(8,128)S(1)}, u32[]{:S(2)}, u32[]{:S(2)}) collective-permute-start(f32[8,128]{1,0:T(8,128)S(1)} %get-tuple-element.24), channel_id=1, source_target_pairs={{0,16},{4,20},{8,24},{12,28},{16,0},{20,4},{24,8},{28,12},{1,17},{... | collective-permute-start | bytes 12296 | tf_op jit(solution)/shard_map/ppermute | solution.py:355
  19.9 1.4 %collective-permute-start.6 = (f32[8,128]{1,0:T(8,128)S(1)}, f32[8,128]{1,0:T(8,128)S(1)}, u32[]{:S(2)}, u32[]{:S(2)}) collective-permute-start(f32[8,128]{1,0:T(8,128)S(1)} %get-tuple-element.25), channel_id=1, source_target_pairs={{0,24},{4,28},{8,16},{12,20},{16,8},{20,12},{24,0},{28,4},{1,25},{... | collective-permute-start | bytes 12296 | tf_op jit(solution)/shard_map/ppermute | solution.py:355
  21.4 0.1 collective-permute-done.4.refs_1_
  21.5 1.2 %collective-permute-done.5.refs_2_ = f32[8,128]{1,0:T(8,128)S(1)} collective-permute-done((f32[8,128]{1,0:T(8,128)S(1)}, f32[8,128]{1,0:T(8,128)S(1)}, u32[]{:S(2)}, u32[]{:S(2)}) %collective-permute-start.5) | collective-permute-done | bytes 4128 | tf_op jit(solution)/shard_map/ppermute | solution.py:355
  22.7 1.7 %collective-permute-done.6.refs_3_ = f32[8,128]{1,0:T(8,128)S(1)} collective-permute-done((f32[8,128]{1,0:T(8,128)S(1)}, f32[8,128]{1,0:T(8,128)S(1)}, u32[]{:S(2)}, u32[]{:S(2)}) %collective-permute-start.6) | collective-permute-done | bytes 4128 | tf_op jit(solution)/shard_map/ppermute | solution.py:355
  24.4 0.0 copy-start
  24.4 0.1 collective-permute-start.7
  24.5 0.0 collective-permute-done.8.gain_ref
  24.5 2.6 %shard_map.82 = (f32[4,8,256,128]{3,2,1,0:T(8,128)S(1)}, f32[4,8,8,128]{3,2,1,0:T(8,128)S(1)}) custom-call(f32[10,8,128]{2,1,0:T(8,128)S(1)} %get-tuple-element.15.coef_ref, f32[4,264,128]{2,1,0:T(8,128)S(1)} %shard_map.78.keep_ref, f32[4,264,128]{2,1,0:T(8,128)S(1)} %collective-permute-done.got_ref, f32[4,264,128]{2,1,0:T(8,128)S(1)} %get-tuple-element.17.give_ref, ...), custom_call_target="tpu_custom_call" | custom-call | flops 3221225472 | bytes 8388608 | tf_op jit(solution)/shard_map/pallas_call | solution.py:435
  27.1 0.0 collective-permute-done.7.theirs_ref
  27.1 0.0 copy-done
  27.1 1.1 %shard_map.83 = (f32[4,8,128]{2,1,0:T(8,128)}, f32[4,8,128]{2,1,0:T(8,128)}) custom-call(f32[4,8,128]{2,1,0:T(8,128)S(1)} %shard_map.81.mine_ref, f32[4,8,128]{2,1,0:T(8,128)S(1)} %collective-permute-done.7.theirs_ref, s32[4,8,128]{2,1,0:T(8,128)S(1)} %copy-done, f32[4,8,256,128]{3,2,1,0:T(8,128)S(1)} %get-tuple-element.26.out_ref, ...), custom_call_target="tpu_custom_call" | custom-call | flops 2097152 | bytes 4194304 | tf_op jit(solution)/shard_map/pallas_call | solution.py:483
  (1 shorter events, 0.0 us)
Async XLA Ops:
  3.3 2.1 %collective-permute-start = (f32[4,264,128]{2,1,0:T(8,128)S(1)}, f32[4,264,128]{2,1,0:T(8,128)S(1)}, u32[]{:S(2)}, u32[]{:S(2)}) collective-permute-start(f32[4,264,128]{2,1,0:T(8,128)S(1)} %get-tuple-element.17.give_ref), channel_id=1, source_target_pairs={{0,4},{4,0},{8,12},{12,8},{16,20},{20,16},{24,28},{28,24},{1,5},{5... | collective-permute-start | bytes 1622024 | tf_op jit(solution)/shard_map/ppermute | solution.py:355
  5.1 19.4 %collective-permute-start.8 = (f32[4,264,128]{2,1,0:T(8,128)S(1)}, f32[4,264,128]{2,1,0:T(8,128)S(1)}, u32[]{:S(2)}, u32[]{:S(2)}) collective-permute-start(f32[4,264,128]{2,1,0:T(8,128)S(1)} %shard_map.78.keep_ref), channel_id=1, source_target_pairs={{0,4},{4,0},{8,12},{12,8},{16,20},{20,16},{24,28},{28,24},{1,5},{5... | collective-permute-start | bytes 1622024 | tf_op jit(solution)/shard_map/ppermute | solution.py:355
  6.0 7.0 %collective-permute-start.1 = (f32[264,128]{1,0:T(8,128)S(1)}, f32[264,128]{1,0:T(8,128)S(1)}, u32[]{:S(2)}, u32[]{:S(2)}) collective-permute-start(f32[264,128]{1,0:T(8,128)S(1)} %get-tuple-element.19), channel_id=1, source_target_pairs={{0,8},{4,12},{8,0},{12,4},{16,24},{20,28},{24,16},{28,20},{1,9},{5... | collective-permute-start | bytes 405512 | tf_op jit(solution)/shard_map/ppermute | solution.py:355
  8.9 8.2 %collective-permute-start.2 = (f32[264,128]{1,0:T(8,128)S(1)}, f32[264,128]{1,0:T(8,128)S(1)}, u32[]{:S(2)}, u32[]{:S(2)}) collective-permute-start(f32[264,128]{1,0:T(8,128)S(1)} %get-tuple-element.20), channel_id=1, source_target_pairs={{0,16},{4,20},{8,24},{12,28},{16,0},{20,4},{24,8},{28,12},{1,17},{... | collective-permute-start | bytes 405512 | tf_op jit(solution)/shard_map/ppermute | solution.py:355
  10.4 6.7 %collective-permute-start.3 = (f32[264,128]{1,0:T(8,128)S(1)}, f32[264,128]{1,0:T(8,128)S(1)}, u32[]{:S(2)}, u32[]{:S(2)}) collective-permute-start(f32[264,128]{1,0:T(8,128)S(1)} %get-tuple-element.21), channel_id=1, source_target_pairs={{0,24},{4,28},{8,16},{12,20},{16,8},{20,12},{24,0},{28,4},{1,25},{... | collective-permute-start | bytes 405512 | tf_op jit(solution)/shard_map/ppermute | solution.py:355
  17.8 3.7 %collective-permute-start.4 = (f32[8,128]{1,0:T(8,128)S(1)}, f32[8,128]{1,0:T(8,128)S(1)}, u32[]{:S(2)}, u32[]{:S(2)}) collective-permute-start(f32[8,128]{1,0:T(8,128)S(1)} %get-tuple-element.23), channel_id=1, source_target_pairs={{0,8},{4,12},{8,0},{12,4},{16,24},{20,28},{24,16},{28,20},{1,9},{5... | collective-permute-start | bytes 12296 | tf_op jit(solution)/shard_map/ppermute | solution.py:355
  19.1 3.6 %collective-permute-start.5 = (f32[8,128]{1,0:T(8,128)S(1)}, f32[8,128]{1,0:T(8,128)S(1)}, u32[]{:S(2)}, u32[]{:S(2)}) collective-permute-start(f32[8,128]{1,0:T(8,128)S(1)} %get-tuple-element.24), channel_id=1, source_target_pairs={{0,16},{4,20},{8,24},{12,28},{16,0},{20,4},{24,8},{28,12},{1,17},{... | collective-permute-start | bytes 12296 | tf_op jit(solution)/shard_map/ppermute | solution.py:355
  19.9 4.5 %collective-permute-start.6 = (f32[8,128]{1,0:T(8,128)S(1)}, f32[8,128]{1,0:T(8,128)S(1)}, u32[]{:S(2)}, u32[]{:S(2)}) collective-permute-start(f32[8,128]{1,0:T(8,128)S(1)} %get-tuple-element.25), channel_id=1, source_target_pairs={{0,24},{4,28},{8,16},{12,20},{16,8},{20,12},{24,0},{28,4},{1,25},{... | collective-permute-start | bytes 12296 | tf_op jit(solution)/shard_map/ppermute | solution.py:355
  24.4 2.7 %copy-start = (s32[4,8,128]{2,1,0:T(8,128)S(1)}, s32[4,8,128]{2,1,0:T(8,128)}, u32[]{:S(2)}) copy-start(s32[4,8,128]{2,1,0:T(8,128)} %phase_ref.1) | copy-start | bytes 49156
  24.4 2.7 %collective-permute-start.7 = (f32[4,8,128]{2,1,0:T(8,128)S(1)}, f32[4,8,128]{2,1,0:T(8,128)S(1)}, u32[]{:S(2)}, u32[]{:S(2)}) collective-permute-start(f32[4,8,128]{2,1,0:T(8,128)S(1)} %shard_map.81.mine_ref), channel_id=1, source_target_pairs={{0,4},{4,0},{8,12},{12,8},{16,20},{20,16},{24,28},{28,24},{1,5},{5... | collective-permute-start | bytes 49160 | tf_op jit(solution)/shard_map/ppermute | solution.py:355

commit v2 on v1

--- a/solution.py
+++ b/solution.py
@@ -277,11 +277,11 @@
 
 
 def chain_kernel(with_edge, *refs):
-    refs, nodes = refs[:-1], refs[-1]
+    refs, nodes = refs[1:-1], refs[-1]
     if with_edge:
         edge_ref, refs = refs[0], refs[1:]
     count, height, cells = nodes.shape
-    refs, out_refs, ends = refs[:count], refs[count:-1], refs[-1]
+    refs, out_refs, ends = refs[count - 1 :: -1], refs[count:-1], refs[-1]
     chip = (lax.axis_index(AXIS) % (2 * count)) // 2
     for d in range(count):
         nodes[chip ^ d] = refs[d][...]
@@ -322,7 +322,7 @@
     count = out_ref.shape[0]
     chip = (lax.axis_index(AXIS) % (2 * count)) // 2
     for d in range(count):
-        out_ref[chip ^ d] = refs[d][...]
+        out_ref[chip ^ d] = refs[count - 1 - d][...]
 
 
 def finish_kernel(mine_ref, theirs_ref, phase_ref, out_ref, const_ref, corr_ref, step_ref, ends_ref):
@@ -353,6 +353,13 @@
 
 def send(x, distance):
     return lax.ppermute(x, AXIS, [(i, i ^ distance) for i in range(lax.axis_size(AXIS))])
+
+
+def send_all(parts):
+    arrived = {0: parts[0]}
+    for d in reversed(range(1, len(parts))):
+        arrived[d] = send(parts[d], 2 * d)
+    return [arrived[d] for d in range(len(parts))]
 
 
 def exact(left, right):
@@ -452,7 +459,7 @@
         compiler_params=LIMIT,
         cost_estimate=cost(24 * half * cells**3, 3 * half * map_bytes),
     )(keep, got)
-    arrived = [joined[0]] + [send(joined[d], 2 * d) for d in range(1, half)]
+    arrived = send_all(joined)
     grouped = lax.axis_size(AXIS) > tiles
     edge = []
     if grouped:
@@ -463,13 +470,13 @@
     ends = pl.pallas_call(
         functools.partial(chain_kernel, grouped),
         out_shape=(end,) * half,
-        in_specs=[VMEM] * (half + len(edge)),
+        in_specs=[pl.BlockSpec(memory_space=pl.ANY)] + [VMEM] * (half + len(edge)),
         out_specs=(VMEM,) * half,
         scratch_shapes=[pltpu.VMEM((half, ROWS, cells), F32), pltpu.VMEM((half, height, cells), F32)],
         compiler_params=LIMIT,
         cost_estimate=cost(8 * half * cells**2, half * map_bytes),
-    )(*edge, *arrived)
-    ends = [ends[0]] + [send(ends[d], 2 * d) for d in range(1, half)]
+    )(constants, *edge, *arrived[::-1])
+    ends = send_all(ends)
     mine = pl.pallas_call(
         order_kernel,
         out_shape=jax.ShapeDtypeStruct((half, ROWS, cells), F32),
@@ -477,7 +484,7 @@
         out_specs=VMEM,
         compiler_params=LIMIT,
         cost_estimate=cost(0, 8 * half * ROWS * cells),
-    )(*ends)
+    )(*ends[::-1])
     theirs = send(mine, 1)
     shape = jax.ShapeDtypeStruct((blocks, tiles, cells), F32)
     return pl.pallas_call(

time: 28.5 us -> 26.7 us (0.937)
  waiting for transfers between devices: 9.93 us -> 8.22 us
    ppermute x9, waiting for transfers between devices: 9.93 us -> 8.22 us  [send(): lax.ppermute(x, AXIS, [(i, i ^ distance) for i in range(lax.axis_size(AXI...]
  transfers between devices with their start and end apart: 9 -> 9, of which waited for: 6 -> 8; matrix products, arithmetic and copies ran while one was open for 0% -> 0% of each run, Pallas kernels for 18% -> 17%
where the time goes in v2:
time: 26.7 us; the launch traced here: 26.5 us
  Pallas kernels  8.93 us (33%)
  starting transfers between devices  8.73 us (33%)
  waiting for transfers between devices  8.22 us (31%)
  between operations  0.68 us (3%)
    ppermute x9, starting transfers between devices, send(): lax.ppermute(x, AXIS, [(i, i ^ distance) for i in range(lax.axis_size(AXI...  8.73 us
    ppermute x9, waiting for transfers between devices, send(): lax.ppermute(x, AXIS, [(i, i ^ distance) for i in range(lax.axis_size(AXI...  8.22 us
    pallas_call x1, Pallas kernels, on_device(): pl.pallas_call(first_kernel, out_shape=(pltpu.VMEM(map_shape, F32), pltpu...  2.69 us
    pallas_call x1, Pallas kernels, on_device(): pl.pallas_call(response_kernel, out_shape=(jax.ShapeDtypeStruct((blocks,...  2.6 us
    pallas_call x1, Pallas kernels, on_device(): pl.pallas_call(second_kernel, out_shape=jax.ShapeDtypeStruct(map_shape, F...  1.28 us
    pallas_call x1, Pallas kernels, on_device(): pl.pallas_call(finish_kernel, out_shape=(shape, shape), in_specs=[VMEM] *...  1.14 us
    pallas_call x1, Pallas kernels, on_device(): pl.pallas_call(functools.partial(chain_kernel, grouped), out_shape=(end,)...  0.63 us
    pallas_call x1, Pallas kernels, on_device(): pl.pallas_call(merge_kernel, out_shape=(node,) * half, in_specs=[VMEM, VM...  0.59 us
  transfers between devices with their start and end apart: 9, of which 8 were waited for; matrix products, arithmetic and copies ran while one was open for 0% of the time, Pallas kernels for 17%

profile of v2, /device:TPU:0, one launch (start us, length us, event | category | flops | bytes accessed | tf_op | source)
XLA Modules:
  0.0 26.5 jit_solution(15721264714078257584)
XLA Ops:
  0.6 2.7 %shard_map.77 = (f32[4,264,128]{2,1,0:T(8,128)S(1)}, f32[10,8,128]{2,1,0:T(8,128)S(1)}, f32[4,8,128,128]{3,2,1,0:T(8,128)S(1)}) custom-call(f32[4]{0:T(128)} %k_hbm.1, s32[4,8,128]{2,1,0:T(8,128)} %mat_hbm.1, s32[4,8,128]{2,1,0:T(8,128)} %fin_hbm.1, f32[4,8,128]{2,1,0:T(8,128)} %res_hbm.1, f32[4,8,128,128]{3,2,1,0:T(8,128)} %g_hbm.1), custom_call_target="tpu_custom_call" | custom-call | flops 805306368 | bytes 2097152 | tf_op jit(solution)/shard_map/pallas_call | solution.py:415
  3.3 0.5 %collective-permute-start = (f32[4,264,128]{2,1,0:T(8,128)S(1)}, f32[4,264,128]{2,1,0:T(8,128)S(1)}, u32[]{:S(2)}, u32[]{:S(2)}) collective-permute-start(f32[4,264,128]{2,1,0:T(8,128)S(1)} %get-tuple-element.17.give_ref), channel_id=1, source_target_pairs={{0,4},{4,0},{8,12},{12,8},{16,20},{20,16},{24,28},{28,24},{1,5},{5... | collective-permute-start | bytes 1622024 | tf_op jit(solution)/shard_map/ppermute | solution.py:355
  3.8 1.3 %shard_map.78.keep_ref = f32[4,264,128]{2,1,0:T(8,128)S(1)} custom-call(f32[10,8,128]{2,1,0:T(8,128)S(1)} %get-tuple-element.15.coef_ref, f32[4,8,128,128]{3,2,1,0:T(8,128)S(1)} %get-tuple-element.16.g_ref), custom_call_target="tpu_custom_call" | custom-call | flops 805306368 | bytes 2097152 | tf_op jit(solution)/shard_map/pallas_call | solution.py:433
  5.1 0.1 collective-permute-start.1
  5.3 0.1 collective-permute-done.got_ref
  5.4 0.6 %shard_map.80 = (f32[264,128]{1,0:T(8,128)S(1)}, f32[264,128]{1,0:T(8,128)S(1)}, f32[264,128]{1,0:T(8,128)S(1)}, f32[264,128]{1,0:T(8,128)S(1)}) custom-call(f32[4,264,128]{2,1,0:T(8,128)S(1)} %shard_map.78.keep_ref, f32[4,264,128]{2,1,0:T(8,128)S(1)} %collective-permute-done.got_ref), custom_call_target="tpu_custom_call" | custom-call | flops 201326592 | bytes 1622016 | tf_op jit(solution)/shard_map/pallas_call | solution.py:454
  6.0 3.9 %collective-permute-start.2 = (f32[264,128]{1,0:T(8,128)S(1)}, f32[264,128]{1,0:T(8,128)S(1)}, u32[]{:S(2)}, u32[]{:S(2)}) collective-permute-start(f32[264,128]{1,0:T(8,128)S(1)} %get-tuple-element.19), channel_id=1, source_target_pairs={{0,24},{4,28},{8,16},{12,20},{16,8},{20,12},{24,0},{28,4},{1,25},{... | collective-permute-start | bytes 405512 | tf_op jit(solution)/shard_map/ppermute | solution.py:355
  9.9 0.5 %collective-permute-start.3 = (f32[264,128]{1,0:T(8,128)S(1)}, f32[264,128]{1,0:T(8,128)S(1)}, u32[]{:S(2)}, u32[]{:S(2)}) collective-permute-start(f32[264,128]{1,0:T(8,128)S(1)} %get-tuple-element.20), channel_id=1, source_target_pairs={{0,16},{4,20},{8,24},{12,28},{16,0},{20,4},{24,8},{28,12},{1,17},{... | collective-permute-start | bytes 405512 | tf_op jit(solution)/shard_map/ppermute | solution.py:355
  10.4 0.0 copy-start
  10.4 0.1 collective-permute-start.4
  10.5 0.0 collective-permute-done.1.gain_ref
  10.5 2.6 %shard_map.79 = (f32[4,8,256,128]{3,2,1,0:T(8,128)S(1)}, f32[4,8,8,128]{3,2,1,0:T(8,128)S(1)}) custom-call(f32[10,8,128]{2,1,0:T(8,128)S(1)} %get-tuple-element.15.coef_ref, f32[4,264,128]{2,1,0:T(8,128)S(1)} %shard_map.78.keep_ref, f32[4,264,128]{2,1,0:T(8,128)S(1)} %collective-permute-done.got_ref, f32[4,264,128]{2,1,0:T(8,128)S(1)} %get-tuple-element.17.give_ref, ...), custom_call_target="tpu_custom_call" | custom-call | flops 3221225472 | bytes 8388608 | tf_op jit(solution)/shard_map/pallas_call | solution.py:442
  13.1 0.8 %collective-permute-done.2.refs_1_ = f32[264,128]{1,0:T(8,128)S(1)} collective-permute-done((f32[264,128]{1,0:T(8,128)S(1)}, f32[264,128]{1,0:T(8,128)S(1)}, u32[]{:S(2)}, u32[]{:S(2)}) %collective-permute-start.2) | collective-permute-done | bytes 135200 | tf_op jit(solution)/shard_map/ppermute | solution.py:355
  14.0 2.7 %collective-permute-done.3.refs_2_ = f32[264,128]{1,0:T(8,128)S(1)} collective-permute-done((f32[264,128]{1,0:T(8,128)S(1)}, f32[264,128]{1,0:T(8,128)S(1)}, u32[]{:S(2)}, u32[]{:S(2)}) %collective-permute-start.3) | collective-permute-done | bytes 135200 | tf_op jit(solution)/shard_map/ppermute | solution.py:355
  16.7 0.3 %collective-permute-done.4.refs_3_ = f32[264,128]{1,0:T(8,128)S(1)} collective-permute-done((f32[264,128]{1,0:T(8,128)S(1)}, f32[264,128]{1,0:T(8,128)S(1)}, u32[]{:S(2)}, u32[]{:S(2)}) %collective-permute-start.4) | collective-permute-done | bytes 135200 | tf_op jit(solution)/shard_map/ppermute | solution.py:355
  17.0 0.6 %shard_map.81 = (f32[8,128]{1,0:T(8,128)S(1)}, f32[8,128]{1,0:T(8,128)S(1)}, f32[8,128]{1,0:T(8,128)S(1)}, f32[8,128]{1,0:T(8,128)S(1)}) custom-call(f32[4,8,8,128]{3,2,1,0:T(8,128)S(1)} %get-tuple-element.18.refs_0_.const_ref, f32[264,128]{1,0:T(8,128)S(1)} %collective-permute-done.2.refs_1_, f32[264,128]{1,0:T(8,128)S(1)} %collective-permute-done.3.refs_2_, ...), custom_call_target="tpu_custom_call" | custom-call | flops 524288 | bytes 540672 | tf_op jit(solution)/shard_map/pallas_call | solution.py:470
  17.6 1.6 %collective-permute-start.5 = (f32[8,128]{1,0:T(8,128)S(1)}, f32[8,128]{1,0:T(8,128)S(1)}, u32[]{:S(2)}, u32[]{:S(2)}) collective-permute-start(f32[8,128]{1,0:T(8,128)S(1)} %get-tuple-element.23), channel_id=1, source_target_pairs={{0,24},{4,28},{8,16},{12,20},{16,8},{20,12},{24,0},{28,4},{1,25},{... | collective-permute-start | bytes 12296 | tf_op jit(solution)/shard_map/ppermute | solution.py:355
  19.2 1.4 %collective-permute-start.6 = (f32[8,128]{1,0:T(8,128)S(1)}, f32[8,128]{1,0:T(8,128)S(1)}, u32[]{:S(2)}, u32[]{:S(2)}) collective-permute-start(f32[8,128]{1,0:T(8,128)S(1)} %get-tuple-element.24), channel_id=1, source_target_pairs={{0,16},{4,20},{8,24},{12,28},{16,0},{20,4},{24,8},{28,12},{1,17},{... | collective-permute-start | bytes 12296 | tf_op jit(solution)/shard_map/ppermute | solution.py:355
  20.6 0.5 %collective-permute-start.7 = (f32[8,128]{1,0:T(8,128)S(1)}, f32[8,128]{1,0:T(8,128)S(1)}, u32[]{:S(2)}, u32[]{:S(2)}) collective-permute-start(f32[8,128]{1,0:T(8,128)S(1)} %get-tuple-element.25), channel_id=1, source_target_pairs={{0,8},{4,12},{8,0},{12,4},{16,24},{20,28},{24,16},{28,20},{1,9},{5... | collective-permute-start | bytes 12296 | tf_op jit(solution)/shard_map/ppermute | solution.py:355
  21.1 1.0 %collective-permute-done.5.refs_0_ = f32[8,128]{1,0:T(8,128)S(1)} collective-permute-done((f32[8,128]{1,0:T(8,128)S(1)}, f32[8,128]{1,0:T(8,128)S(1)}, u32[]{:S(2)}, u32[]{:S(2)}) %collective-permute-start.5) | collective-permute-done | bytes 4128 | tf_op jit(solution)/shard_map/ppermute | solution.py:355
  22.2 0.6 %collective-permute-done.6.refs_1_ = f32[8,128]{1,0:T(8,128)S(1)} collective-permute-done((f32[8,128]{1,0:T(8,128)S(1)}, f32[8,128]{1,0:T(8,128)S(1)}, u32[]{:S(2)}, u32[]{:S(2)}) %collective-permute-start.6) | collective-permute-done | bytes 4128 | tf_op jit(solution)/shard_map/ppermute | solution.py:355
  22.8 1.4 %collective-permute-done.7.refs_2_ = f32[8,128]{1,0:T(8,128)S(1)} collective-permute-done((f32[8,128]{1,0:T(8,128)S(1)}, f32[8,128]{1,0:T(8,128)S(1)}, u32[]{:S(2)}, u32[]{:S(2)}) %collective-permute-start.7) | collective-permute-done | bytes 4128 | tf_op jit(solution)/shard_map/ppermute | solution.py:355
  24.2 0.0 collective-permute-start.8
  24.2 1.2 %collective-permute-done.8.theirs_ref = f32[4,8,128]{2,1,0:T(8,128)S(1)} collective-permute-done((f32[4,8,128]{2,1,0:T(8,128)S(1)}, f32[4,8,128]{2,1,0:T(8,128)S(1)}, u32[]{:S(2)}, u32[]{:S(2)}) %collective-permute-start.8) | collective-permute-done | bytes 16416 | tf_op jit(solution)/shard_map/ppermute | solution.py:355
  25.4 0.0 copy-done
  25.4 1.1 %shard_map.83 = (f32[4,8,128]{2,1,0:T(8,128)}, f32[4,8,128]{2,1,0:T(8,128)}) custom-call(f32[4,8,128]{2,1,0:T(8,128)S(1)} %shard_map.82.mine_ref, f32[4,8,128]{2,1,0:T(8,128)S(1)} %collective-permute-done.8.theirs_ref, s32[4,8,128]{2,1,0:T(8,128)S(1)} %copy-done, f32[4,8,256,128]{3,2,1,0:T(8,128)S(1)} %get-tuple-element.27.out_ref, ...), custom_call_target="tpu_custom_call" | custom-call | flops 2097152 | bytes 4194304 | tf_op jit(solution)/shard_map/pallas_call | solution.py:490
  (1 shorter events, 0.0 us)
Async XLA Ops:
  3.3 2.1 %collective-permute-start = (f32[4,264,128]{2,1,0:T(8,128)S(1)}, f32[4,264,128]{2,1,0:T(8,128)S(1)}, u32[]{:S(2)}, u32[]{:S(2)}) collective-permute-start(f32[4,264,128]{2,1,0:T(8,128)S(1)} %get-tuple-element.17.give_ref), channel_id=1, source_target_pairs={{0,4},{4,0},{8,12},{12,8},{16,20},{20,16},{24,28},{28,24},{1,5},{5... | collective-permute-start | bytes 1622024 | tf_op jit(solution)/shard_map/ppermute | solution.py:355
  5.1 5.4 %collective-permute-start.1 = (f32[4,264,128]{2,1,0:T(8,128)S(1)}, f32[4,264,128]{2,1,0:T(8,128)S(1)}, u32[]{:S(2)}, u32[]{:S(2)}) collective-permute-start(f32[4,264,128]{2,1,0:T(8,128)S(1)} %shard_map.78.keep_ref), channel_id=1, source_target_pairs={{0,4},{4,0},{8,12},{12,8},{16,20},{20,16},{24,28},{28,24},{1,5},{5... | collective-permute-start | bytes 1622024 | tf_op jit(solution)/shard_map/ppermute | solution.py:355
  6.0 8.0 %collective-permute-start.2 = (f32[264,128]{1,0:T(8,128)S(1)}, f32[264,128]{1,0:T(8,128)S(1)}, u32[]{:S(2)}, u32[]{:S(2)}) collective-permute-start(f32[264,128]{1,0:T(8,128)S(1)} %get-tuple-element.19), channel_id=1, source_target_pairs={{0,24},{4,28},{8,16},{12,20},{16,8},{20,12},{24,0},{28,4},{1,25},{... | collective-permute-start | bytes 405512 | tf_op jit(solution)/shard_map/ppermute | solution.py:355
  9.9 6.8 %collective-permute-start.3 = (f32[264,128]{1,0:T(8,128)S(1)}, f32[264,128]{1,0:T(8,128)S(1)}, u32[]{:S(2)}, u32[]{:S(2)}) collective-permute-start(f32[264,128]{1,0:T(8,128)S(1)} %get-tuple-element.20), channel_id=1, source_target_pairs={{0,16},{4,20},{8,24},{12,28},{16,0},{20,4},{24,8},{28,12},{1,17},{... | collective-permute-start | bytes 405512 | tf_op jit(solution)/shard_map/ppermute | solution.py:355
  10.4 15.0 %copy-start = (s32[4,8,128]{2,1,0:T(8,128)S(1)}, s32[4,8,128]{2,1,0:T(8,128)}, u32[]{:S(2)}) copy-start(s32[4,8,128]{2,1,0:T(8,128)} %phase_ref.1) | copy-start | bytes 49156
  10.4 6.6 %collective-permute-start.4 = (f32[264,128]{1,0:T(8,128)S(1)}, f32[264,128]{1,0:T(8,128)S(1)}, u32[]{:S(2)}, u32[]{:S(2)}) collective-permute-start(f32[264,128]{1,0:T(8,128)S(1)} %get-tuple-element.21), channel_id=1, source_target_pairs={{0,8},{4,12},{8,0},{12,4},{16,24},{20,28},{24,16},{28,20},{1,9},{5... | collective-permute-start | bytes 405512 | tf_op jit(solution)/shard_map/ppermute | solution.py:355
  17.6 4.6 %collective-permute-start.5 = (f32[8,128]{1,0:T(8,128)S(1)}, f32[8,128]{1,0:T(8,128)S(1)}, u32[]{:S(2)}, u32[]{:S(2)}) collective-permute-start(f32[8,128]{1,0:T(8,128)S(1)} %get-tuple-element.23), channel_id=1, source_target_pairs={{0,24},{4,28},{8,16},{12,20},{16,8},{20,12},{24,0},{28,4},{1,25},{... | collective-permute-start | bytes 12296 | tf_op jit(solution)/shard_map/ppermute | solution.py:355
  19.2 3.6 %collective-permute-start.6 = (f32[8,128]{1,0:T(8,128)S(1)}, f32[8,128]{1,0:T(8,128)S(1)}, u32[]{:S(2)}, u32[]{:S(2)}) collective-permute-start(f32[8,128]{1,0:T(8,128)S(1)} %get-tuple-element.24), channel_id=1, source_target_pairs={{0,16},{4,20},{8,24},{12,28},{16,0},{20,4},{24,8},{28,12},{1,17},{... | collective-permute-start | bytes 12296 | tf_op jit(solution)/shard_map/ppermute | solution.py:355
  20.6 3.6 %collective-permute-start.7 = (f32[8,128]{1,0:T(8,128)S(1)}, f32[8,128]{1,0:T(8,128)S(1)}, u32[]{:S(2)}, u32[]{:S(2)}) collective-permute-start(f32[8,128]{1,0:T(8,128)S(1)} %get-tuple-element.25), channel_id=1, source_target_pairs={{0,8},{4,12},{8,0},{12,4},{16,24},{20,28},{24,16},{28,20},{1,9},{5... | collective-permute-start | bytes 12296 | tf_op jit(solution)/shard_map/ppermute | solution.py:355
  24.2 1.2 %collective-permute-start.8 = (f32[4,8,128]{2,1,0:T(8,128)S(1)}, f32[4,8,128]{2,1,0:T(8,128)S(1)}, u32[]{:S(2)}, u32[]{:S(2)}) collective-permute-start(f32[4,8,128]{2,1,0:T(8,128)S(1)} %shard_map.82.mine_ref), channel_id=1, source_target_pairs={{0,4},{4,0},{8,12},{12,8},{16,20},{20,16},{24,28},{28,24},{1,5},{5... | collective-permute-start | bytes 49160 | tf_op jit(solution)/shard_map/ppermute | solution.py:355

commit v3 on v2

--- a/solution.py
+++ b/solution.py
@@ -71,6 +71,29 @@
 def times_t(matrix, row, eye):
     column = jnp.sum(jnp.where(eye, row, 0.0), axis=1, keepdims=True)
     return jnp.sum(matrix * column, axis=0, keepdims=True)
+
+
+def halves(cells):
+    shape = (cells // 2, cells)
+    return lax.broadcasted_iota(jnp.int32, shape, 0), lax.broadcasted_iota(jnp.int32, shape, 1)
+
+
+def pack(square):
+    middle = square.shape[0] // 2
+    row, lane = halves(square.shape[1])
+    top, bottom = square[:middle], pltpu.roll(square[middle:], middle, 1)
+    return jnp.where(
+        (lane >= middle) | (lane < row), top, jnp.where(lane == row, 0.5 * top, bottom)
+    )
+
+
+def unpack(packed, half_diagonal, roll):
+    middle, cells = packed.shape
+    row, lane = halves(cells)
+    top = jnp.where((lane >= middle) | (lane <= row), packed, 0.0)
+    bottom = jnp.where(lane - middle > row, roll(packed, middle, 1), 0.0)
+    bottom = jnp.where(lane - middle == row, half_diagonal, bottom)
+    return jnp.concatenate([top, bottom], axis=0)
 
 
 def stack_rows(rows, cells):
@@ -248,6 +271,7 @@
     here = lax.axis_index(AXIS)
     is_second = here % 2 == 1
     chip = (here % (2 * half)) // 2
+    eye = eye_mask(cells)
     for d in range(half):
         tile = chip ^ d
         keep, got = keep_ref[tile], got_ref[tile]
@@ -261,16 +285,18 @@
         lower = squared[cells:] + stack_rows([vb[1:2]], cells)
         squared = jnp.concatenate([squared[:cells], lower], axis=0)
         total = mul_t(squared, scaled[:cells])
+        square = first[cells : 2 * cells] + total[:cells]
         out_ref = out_refs[d]
         out_ref[0:cells] = moved[:cells]
-        out_ref[cells : 2 * cells] = first[cells : 2 * cells] + total[:cells]
-        out_ref[2 * cells :] = stack_rows(
+        out_ref[cells:-ROWS] = pack(square)
+        out_ref[-ROWS:] = stack_rows(
             [
                 moved[cells : cells + 1] + vb[0:1],
                 total[cells : cells + 1] + va[1:2],
                 va[2:3],
                 vb[3:4],
                 va[4:5],
+                0.5 * jnp.sum(jnp.where(eye, square, 0.0), axis=0, keepdims=True),
             ],
             cells,
         )
@@ -286,7 +312,10 @@
     for d in range(count):
         nodes[chip ^ d] = refs[d][...]
     eye = eye_mask(cells)
-    vectors = [nodes[k, 2 * cells :] for k in range(count)]
+    vectors = [nodes[k, height - ROWS :] for k in range(count)]
+    squares = [None] + [
+        unpack(nodes[k, cells : height - ROWS], vectors[k][5:6], pltpu.roll) for k in range(1, count)
+    ]
     faces = [None] + [
         face(vectors[k][2:3], vectors[k - 1][3:4], vectors[k][4:5]) for k in range(1, count)
     ]
@@ -300,7 +329,8 @@
         if k < count - 1:
             leaving = vectors[k][0:1] + times_t(nodes[k, 0:cells], entering[k], eye)
     heads = [None] + [
-        vectors[k][1:2] + times(nodes[k, cells : 2 * cells], entering[k], eye) for k in range(1, count)
+        vectors[k][1:2] + times(squares[k], entering[k], eye) + times_t(squares[k], entering[k], eye)
+        for k in range(1, count)
     ]
     for k in reversed(range(1, count)):
         head = heads[k]
@@ -372,6 +402,10 @@
     def parts(node):
         return node[:cells], node[cells : 2 * cells], node[2 * cells :]
 
+    def widen(node):
+        part = unpack(node[cells:-ROWS], node[-3:-2], jnp.roll)
+        return jnp.concatenate([node[:cells], part + part.T, node[-ROWS:]], axis=0)
+
     def join(first, second):
         (ma, qa, va), (mb, qb, vb) = parts(first), parts(second)
         between = face(vb[2], va[3], vb[4])
@@ -384,7 +418,7 @@
         return jnp.concatenate([exact(scaled, mb), q, rows, rest], axis=0)
 
     groups = lax.axis_size(AXIS) // devices
-    whole = functools.reduce(join, [nodes[k] for k in range(nodes.shape[0])])
+    whole = functools.reduce(join, [widen(nodes[k]) for k in range(nodes.shape[0])])
     members = [[g * devices + q for g in range(groups)] for q in range(devices)]
     every = lax.all_gather(whole, AXIS, axis=0, axis_index_groups=members)
     split_up = [parts(every[g]) for g in range(groups)]
@@ -450,7 +484,8 @@
         compiler_params=LIMIT,
         cost_estimate=cost(48 * tiles * blocks * cells**3, 16 * tiles * blocks * cells**2),
     )(coef, keep, got, give, gain, inverses)
-    node = jax.ShapeDtypeStruct((height, cells), F32)
+    short = cells + cells // 2 + ROWS
+    node = jax.ShapeDtypeStruct((short, cells), F32)
     joined = pl.pallas_call(
         merge_kernel,
         out_shape=(node,) * half,
@@ -472,7 +507,7 @@
         out_shape=(end,) * half,
         in_specs=[pl.BlockSpec(memory_space=pl.ANY)] + [VMEM] * (half + len(edge)),
         out_specs=(VMEM,) * half,
-        scratch_shapes=[pltpu.VMEM((half, ROWS, cells), F32), pltpu.VMEM((half, height, cells), F32)],
+        scratch_shapes=[pltpu.VMEM((half, ROWS, cells), F32), pltpu.VMEM((half, short, cells), F32)],
         compiler_params=LIMIT,
         cost_estimate=cost(8 * half * cells**2, half * map_bytes),
     )(constants, *edge, *arrived[::-1])

time: 26.7 us -> 25.3 us (0.948)
  waiting for transfers between devices: 8.22 us -> 6.83 us
    ppermute x9, waiting for transfers between devices: 8.22 us -> 6.83 us  [send(): lax.ppermute(x, AXIS, [(i, i ^ distance) for i in range(lax.axis_size(AXI...]
  transfers between devices with their start and end apart: 9 -> 9, of which waited for: 8 -> 7; matrix products, arithmetic and copies ran while one was open for 0% -> 0% of each run, Pallas kernels for 17% -> 18%
where the time goes in v3:
time: 25.3 us; the launch traced here: 25.2 us
  Pallas kernels  8.97 us (35%)
  starting transfers between devices  8.72 us (34%)
  waiting for transfers between devices  6.83 us (27%)
  between operations  0.67 us (3%)
    ppermute x9, starting transfers between devices, send(): lax.ppermute(x, AXIS, [(i, i ^ distance) for i in range(lax.axis_size(AXI...  8.72 us
    ppermute x9, waiting for transfers between devices, send(): lax.ppermute(x, AXIS, [(i, i ^ distance) for i in range(lax.axis_size(AXI...  6.83 us
    pallas_call x1, Pallas kernels, on_device(): pl.pallas_call(first_kernel, out_shape=(pltpu.VMEM(map_shape, F32), pltpu...  2.68 us
    pallas_call x1, Pallas kernels, on_device(): pl.pallas_call(response_kernel, out_shape=(jax.ShapeDtypeStruct((blocks,...  2.59 us
    pallas_call x1, Pallas kernels, on_device(): pl.pallas_call(second_kernel, out_shape=jax.ShapeDtypeStruct(map_shape, F...  1.28 us
    pallas_call x1, Pallas kernels, on_device(): pl.pallas_call(finish_kernel, out_shape=(shape, shape), in_specs=[VMEM] *...  1.13 us
    pallas_call x1, Pallas kernels, on_device(): pl.pallas_call(merge_kernel, out_shape=(node,) * half, in_specs=[VMEM, VM...  0.66 us
    pallas_call x1, Pallas kernels, on_device(): pl.pallas_call(functools.partial(chain_kernel, grouped), out_shape=(end,)...  0.63 us
  transfers between devices with their start and end apart: 9, of which 7 were waited for; matrix products, arithmetic and copies ran while one was open for 0% of the time, Pallas kernels for 18%

profile of v3, /device:TPU:0, one launch (start us, length us, event | category | flops | bytes accessed | tf_op | source)
XLA Modules:
  0.0 25.2 jit_solution(2493074997180287496)
XLA Ops:
  0.6 2.7 %shard_map.77 = (f32[4,264,128]{2,1,0:T(8,128)S(1)}, f32[10,8,128]{2,1,0:T(8,128)S(1)}, f32[4,8,128,128]{3,2,1,0:T(8,128)S(1)}) custom-call(f32[4]{0:T(128)} %k_hbm.1, s32[4,8,128]{2,1,0:T(8,128)} %mat_hbm.1, s32[4,8,128]{2,1,0:T(8,128)} %fin_hbm.1, f32[4,8,128]{2,1,0:T(8,128)} %res_hbm.1, f32[4,8,128,128]{3,2,1,0:T(8,128)} %g_hbm.1), custom_call_target="tpu_custom_call" | custom-call | flops 805306368 | bytes 2097152 | tf_op jit(solution)/shard_map/pallas_call | solution.py:449
  3.3 0.5 %collective-permute-start = (f32[4,264,128]{2,1,0:T(8,128)S(1)}, f32[4,264,128]{2,1,0:T(8,128)S(1)}, u32[]{:S(2)}, u32[]{:S(2)}) collective-permute-start(f32[4,264,128]{2,1,0:T(8,128)S(1)} %get-tuple-element.17.give_ref), channel_id=1, source_target_pairs={{0,4},{4,0},{8,12},{12,8},{16,20},{20,16},{24,28},{28,24},{1,5},{5... | collective-permute-start | bytes 1622024 | tf_op jit(solution)/shard_map/ppermute | solution.py:385
  3.8 1.3 %shard_map.78.keep_ref = f32[4,264,128]{2,1,0:T(8,128)S(1)} custom-call(f32[10,8,128]{2,1,0:T(8,128)S(1)} %get-tuple-element.15.coef_ref, f32[4,8,128,128]{3,2,1,0:T(8,128)S(1)} %get-tuple-element.16.g_ref), custom_call_target="tpu_custom_call" | custom-call | flops 805306368 | bytes 2097152 | tf_op jit(solution)/shard_map/pallas_call | solution.py:467
  5.1 0.1 collective-permute-start.1
  5.3 0.1 collective-permute-done.got_ref
  5.4 0.7 %shard_map.80 = (f32[200,128]{1,0:T(8,128)S(1)}, f32[200,128]{1,0:T(8,128)S(1)}, f32[200,128]{1,0:T(8,128)S(1)}, f32[200,128]{1,0:T(8,128)S(1)}) custom-call(f32[4,264,128]{2,1,0:T(8,128)S(1)} %shard_map.78.keep_ref, f32[4,264,128]{2,1,0:T(8,128)S(1)} %collective-permute-done.got_ref), custom_call_target="tpu_custom_call" | custom-call | flops 201326592 | bytes 1622016 | tf_op jit(solution)/shard_map/pallas_call | solution.py:489
  6.1 3.9 %collective-permute-start.2 = (f32[200,128]{1,0:T(8,128)S(1)}, f32[200,128]{1,0:T(8,128)S(1)}, u32[]{:S(2)}, u32[]{:S(2)}) collective-permute-start(f32[200,128]{1,0:T(8,128)S(1)} %get-tuple-element.19), channel_id=1, source_target_pairs={{0,24},{4,28},{8,16},{12,20},{16,8},{20,12},{24,0},{28,4},{1,25},{... | collective-permute-start | bytes 307208 | tf_op jit(solution)/shard_map/ppermute | solution.py:385
  9.9 0.5 %collective-permute-start.3 = (f32[200,128]{1,0:T(8,128)S(1)}, f32[200,128]{1,0:T(8,128)S(1)}, u32[]{:S(2)}, u32[]{:S(2)}) collective-permute-start(f32[200,128]{1,0:T(8,128)S(1)} %get-tuple-element.20), channel_id=1, source_target_pairs={{0,16},{4,20},{8,24},{12,28},{16,0},{20,4},{24,8},{28,12},{1,17},{... | collective-permute-start | bytes 307208 | tf_op jit(solution)/shard_map/ppermute | solution.py:385
  10.4 0.0 copy-start
  10.4 0.1 collective-permute-start.4
  10.6 0.0 collective-permute-done.1.gain_ref
  10.6 2.6 %shard_map.79 = (f32[4,8,256,128]{3,2,1,0:T(8,128)S(1)}, f32[4,8,8,128]{3,2,1,0:T(8,128)S(1)}) custom-call(f32[10,8,128]{2,1,0:T(8,128)S(1)} %get-tuple-element.15.coef_ref, f32[4,264,128]{2,1,0:T(8,128)S(1)} %shard_map.78.keep_ref, f32[4,264,128]{2,1,0:T(8,128)S(1)} %collective-permute-done.got_ref, f32[4,264,128]{2,1,0:T(8,128)S(1)} %get-tuple-element.17.give_ref, ...), custom_call_target="tpu_custom_call" | custom-call | flops 3221225472 | bytes 8388608 | tf_op jit(solution)/shard_map/pallas_call | solution.py:476
  13.2 0.0 collective-permute-done.2.refs_1_
  13.2 2.1 %collective-permute-done.3.refs_2_ = f32[200,128]{1,0:T(8,128)S(1)} collective-permute-done((f32[200,128]{1,0:T(8,128)S(1)}, f32[200,128]{1,0:T(8,128)S(1)}, u32[]{:S(2)}, u32[]{:S(2)}) %collective-permute-start.3) | collective-permute-done | bytes 102432 | tf_op jit(solution)/shard_map/ppermute | solution.py:385
  15.3 0.2 collective-permute-done.4.refs_3_
  15.6 0.6 %shard_map.81 = (f32[8,128]{1,0:T(8,128)S(1)}, f32[8,128]{1,0:T(8,128)S(1)}, f32[8,128]{1,0:T(8,128)S(1)}, f32[8,128]{1,0:T(8,128)S(1)}) custom-call(f32[4,8,8,128]{3,2,1,0:T(8,128)S(1)} %get-tuple-element.18.refs_0_.const_ref, f32[200,128]{1,0:T(8,128)S(1)} %collective-permute-done.2.refs_1_, f32[200,128]{1,0:T(8,128)S(1)} %collective-permute-done.3.refs_2_, ...), custom_call_target="tpu_custom_call" | custom-call | flops 524288 | bytes 540672 | tf_op jit(solution)/shard_map/pallas_call | solution.py:505
  16.2 1.6 %collective-permute-start.5 = (f32[8,128]{1,0:T(8,128)S(1)}, f32[8,128]{1,0:T(8,128)S(1)}, u32[]{:S(2)}, u32[]{:S(2)}) collective-permute-start(f32[8,128]{1,0:T(8,128)S(1)} %get-tuple-element.23), channel_id=1, source_target_pairs={{0,24},{4,28},{8,16},{12,20},{16,8},{20,12},{24,0},{28,4},{1,25},{... | collective-permute-start | bytes 12296 | tf_op jit(solution)/shard_map/ppermute | solution.py:385
  17.8 1.4 %collective-permute-start.6 = (f32[8,128]{1,0:T(8,128)S(1)}, f32[8,128]{1,0:T(8,128)S(1)}, u32[]{:S(2)}, u32[]{:S(2)}) collective-permute-start(f32[8,128]{1,0:T(8,128)S(1)} %get-tuple-element.24), channel_id=1, source_target_pairs={{0,16},{4,20},{8,24},{12,28},{16,0},{20,4},{24,8},{28,12},{1,17},{... | collective-permute-start | bytes 12296 | tf_op jit(solution)/shard_map/ppermute | solution.py:385
  19.3 0.5 %collective-permute-start.7 = (f32[8,128]{1,0:T(8,128)S(1)}, f32[8,128]{1,0:T(8,128)S(1)}, u32[]{:S(2)}, u32[]{:S(2)}) collective-permute-start(f32[8,128]{1,0:T(8,128)S(1)} %get-tuple-element.25), channel_id=1, source_target_pairs={{0,8},{4,12},{8,0},{12,4},{16,24},{20,28},{24,16},{28,20},{1,9},{5... | collective-permute-start | bytes 12296 | tf_op jit(solution)/shard_map/ppermute | solution.py:385
  19.7 1.0 %collective-permute-done.5.refs_0_ = f32[8,128]{1,0:T(8,128)S(1)} collective-permute-done((f32[8,128]{1,0:T(8,128)S(1)}, f32[8,128]{1,0:T(8,128)S(1)}, u32[]{:S(2)}, u32[]{:S(2)}) %collective-permute-start.5) | collective-permute-done | bytes 4128 | tf_op jit(solution)/shard_map/ppermute | solution.py:385
  20.8 0.7 %collective-permute-done.6.refs_1_ = f32[8,128]{1,0:T(8,128)S(1)} collective-permute-done((f32[8,128]{1,0:T(8,128)S(1)}, f32[8,128]{1,0:T(8,128)S(1)}, u32[]{:S(2)}, u32[]{:S(2)}) %collective-permute-start.6) | collective-permute-done | bytes 4128 | tf_op jit(solution)/shard_map/ppermute | solution.py:385
  21.4 1.4 %collective-permute-done.7.refs_2_ = f32[8,128]{1,0:T(8,128)S(1)} collective-permute-done((f32[8,128]{1,0:T(8,128)S(1)}, f32[8,128]{1,0:T(8,128)S(1)}, u32[]{:S(2)}, u32[]{:S(2)}) %collective-permute-start.7) | collective-permute-done | bytes 4128 | tf_op jit(solution)/shard_map/ppermute | solution.py:385
  22.9 0.0 collective-permute-start.8
  22.9 1.2 %collective-permute-done.8.theirs_ref = f32[4,8,128]{2,1,0:T(8,128)S(1)} collective-permute-done((f32[4,8,128]{2,1,0:T(8,128)S(1)}, f32[4,8,128]{2,1,0:T(8,128)S(1)}, u32[]{:S(2)}, u32[]{:S(2)}) %collective-permute-start.8) | collective-permute-done | bytes 16416 | tf_op jit(solution)/shard_map/ppermute | solution.py:385
  24.1 0.0 copy-done
  24.1 1.1 %shard_map.83 = (f32[4,8,128]{2,1,0:T(8,128)}, f32[4,8,128]{2,1,0:T(8,128)}) custom-call(f32[4,8,128]{2,1,0:T(8,128)S(1)} %shard_map.82.mine_ref, f32[4,8,128]{2,1,0:T(8,128)S(1)} %collective-permute-done.8.theirs_ref, s32[4,8,128]{2,1,0:T(8,128)S(1)} %copy-done, f32[4,8,256,128]{3,2,1,0:T(8,128)S(1)} %get-tuple-element.27.out_ref, ...), custom_call_target="tpu_custom_call" | custom-call | flops 2097152 | bytes 4194304 | tf_op jit(solution)/shard_map/pallas_call | solution.py:525
  (1 shorter events, 0.0 us)
Async XLA Ops:
  3.3 2.1 %collective-permute-start = (f32[4,264,128]{2,1,0:T(8,128)S(1)}, f32[4,264,128]{2,1,0:T(8,128)S(1)}, u32[]{:S(2)}, u32[]{:S(2)}) collective-permute-start(f32[4,264,128]{2,1,0:T(8,128)S(1)} %get-tuple-element.17.give_ref), channel_id=1, source_target_pairs={{0,4},{4,0},{8,12},{12,8},{16,20},{20,16},{24,28},{28,24},{1,5},{5... | collective-permute-start | bytes 1622024 | tf_op jit(solution)/shard_map/ppermute | solution.py:385
  5.1 5.5 %collective-permute-start.1 = (f32[4,264,128]{2,1,0:T(8,128)S(1)}, f32[4,264,128]{2,1,0:T(8,128)S(1)}, u32[]{:S(2)}, u32[]{:S(2)}) collective-permute-start(f32[4,264,128]{2,1,0:T(8,128)S(1)} %shard_map.78.keep_ref), channel_id=1, source_target_pairs={{0,4},{4,0},{8,12},{12,8},{16,20},{20,16},{24,28},{28,24},{1,5},{5... | collective-permute-start | bytes 1622024 | tf_op jit(solution)/shard_map/ppermute | solution.py:385
  6.1 7.2 %collective-permute-start.2 = (f32[200,128]{1,0:T(8,128)S(1)}, f32[200,128]{1,0:T(8,128)S(1)}, u32[]{:S(2)}, u32[]{:S(2)}) collective-permute-start(f32[200,128]{1,0:T(8,128)S(1)} %get-tuple-element.19), channel_id=1, source_target_pairs={{0,24},{4,28},{8,16},{12,20},{16,8},{20,12},{24,0},{28,4},{1,25},{... | collective-permute-start | bytes 307208 | tf_op jit(solution)/shard_map/ppermute | solution.py:385
  9.9 5.4 %collective-permute-start.3 = (f32[200,128]{1,0:T(8,128)S(1)}, f32[200,128]{1,0:T(8,128)S(1)}, u32[]{:S(2)}, u32[]{:S(2)}) collective-permute-start(f32[200,128]{1,0:T(8,128)S(1)} %get-tuple-element.20), channel_id=1, source_target_pairs={{0,16},{4,20},{8,24},{12,28},{16,0},{20,4},{24,8},{28,12},{1,17},{... | collective-permute-start | bytes 307208 | tf_op jit(solution)/shard_map/ppermute | solution.py:385
  10.4 13.6 %copy-start = (s32[4,8,128]{2,1,0:T(8,128)S(1)}, s32[4,8,128]{2,1,0:T(8,128)}, u32[]{:S(2)}) copy-start(s32[4,8,128]{2,1,0:T(8,128)} %phase_ref.1) | copy-start | bytes 49156
  10.4 5.1 %collective-permute-start.4 = (f32[200,128]{1,0:T(8,128)S(1)}, f32[200,128]{1,0:T(8,128)S(1)}, u32[]{:S(2)}, u32[]{:S(2)}) collective-permute-start(f32[200,128]{1,0:T(8,128)S(1)} %get-tuple-element.21), channel_id=1, source_target_pairs={{0,8},{4,12},{8,0},{12,4},{16,24},{20,28},{24,16},{28,20},{1,9},{5... | collective-permute-start | bytes 307208 | tf_op jit(solution)/shard_map/ppermute | solution.py:385
  16.2 4.6 %collective-permute-start.5 = (f32[8,128]{1,0:T(8,128)S(1)}, f32[8,128]{1,0:T(8,128)S(1)}, u32[]{:S(2)}, u32[]{:S(2)}) collective-permute-start(f32[8,128]{1,0:T(8,128)S(1)} %get-tuple-element.23), channel_id=1, source_target_pairs={{0,24},{4,28},{8,16},{12,20},{16,8},{20,12},{24,0},{28,4},{1,25},{... | collective-permute-start | bytes 12296 | tf_op jit(solution)/shard_map/ppermute | solution.py:385
  17.8 3.6 %collective-permute-start.6 = (f32[8,128]{1,0:T(8,128)S(1)}, f32[8,128]{1,0:T(8,128)S(1)}, u32[]{:S(2)}, u32[]{:S(2)}) collective-permute-start(f32[8,128]{1,0:T(8,128)S(1)} %get-tuple-element.24), channel_id=1, source_target_pairs={{0,16},{4,20},{8,24},{12,28},{16,0},{20,4},{24,8},{28,12},{1,17},{... | collective-permute-start | bytes 12296 | tf_op jit(solution)/shard_map/ppermute | solution.py:385
  19.3 3.6 %collective-permute-start.7 = (f32[8,128]{1,0:T(8,128)S(1)}, f32[8,128]{1,0:T(8,128)S(1)}, u32[]{:S(2)}, u32[]{:S(2)}) collective-permute-start(f32[8,128]{1,0:T(8,128)S(1)} %get-tuple-element.25), channel_id=1, source_target_pairs={{0,8},{4,12},{8,0},{12,4},{16,24},{20,28},{24,16},{28,20},{1,9},{5... | collective-permute-start | bytes 12296 | tf_op jit(solution)/shard_map/ppermute | solution.py:385
  22.9 1.2 %collective-permute-start.8 = (f32[4,8,128]{2,1,0:T(8,128)S(1)}, f32[4,8,128]{2,1,0:T(8,128)S(1)}, u32[]{:S(2)}, u32[]{:S(2)}) collective-permute-start(f32[4,8,128]{2,1,0:T(8,128)S(1)} %shard_map.82.mine_ref), channel_id=1, source_target_pairs={{0,4},{4,0},{8,12},{12,8},{16,20},{20,16},{24,28},{28,24},{1,5},{5... | collective-permute-start | bytes 49160 | tf_op jit(solution)/shard_map/ppermute | solution.py:385

commit v4 on v3

--- a/solution.py
+++ b/solution.py
@@ -122,10 +122,10 @@
             )
             wide[j] = both[:, :cells] + both[:, cells:]
             wh, wl = split(wide[j])
-            both = lax.dot_general(
+            th, tl = split(scaled[:cells].T)
+            both = jnp.dot(
                 jnp.concatenate([wh, wl], axis=1),
-                jnp.concatenate([jnp.concatenate([sh, sh], axis=1), jnp.concatenate([sl, zero], axis=1)], axis=0),
-                (((1,), (1,)), ((), ())),
+                jnp.concatenate([jnp.concatenate([th, tl], axis=1), jnp.concatenate([th, zero], axis=1)], axis=0),
                 preferred_element_type=F32,
             )
             total[j] = total[j] + (both[:, :cells] + both[:, cells:])
@@ -272,26 +272,31 @@
     is_second = here % 2 == 1
     chip = (here % (2 * half)) // 2
     eye = eye_mask(cells)
-    for d in range(half):
-        tile = chip ^ d
-        keep, got = keep_ref[tile], got_ref[tile]
-        first = jnp.where(is_second, got, keep)
-        second = jnp.where(is_second, keep, got)
-        va, vb = first[2 * cells :], second[2 * cells :]
+    order = list(reversed(range(half)))
+    first, last, scaled, between, moved, squared = {}, {}, {}, {}, {}, {}
+    for d in order:
+        keep, got = keep_ref[chip ^ d], got_ref[chip ^ d]
+        first[d] = jnp.where(is_second, got, keep)
+        last[d] = jnp.where(is_second, keep, got)
+        va, vb = first[d][2 * cells :], last[d][2 * cells :]
         between = face(vb[2:3], va[3:4], vb[4:5])
-        scaled = jnp.concatenate([first[:cells], stack_rows([va[0:1]], cells)], axis=0) * between
-        moved = mul(scaled, second[:cells])
-        squared = mul(scaled, second[cells : 2 * cells])
-        lower = squared[cells:] + stack_rows([vb[1:2]], cells)
-        squared = jnp.concatenate([squared[:cells], lower], axis=0)
-        total = mul_t(squared, scaled[:cells])
-        square = first[cells : 2 * cells] + total[:cells]
+        scaled[d] = jnp.concatenate([first[d][:cells], stack_rows([va[0:1]], cells)], axis=0) * between
+    for d in order:
+        moved[d] = mul(scaled[d], last[d][:cells])
+    for d in order:
+        squared[d] = mul(scaled[d], last[d][cells : 2 * cells])
+        lower = squared[d][cells:] + stack_rows([last[d][2 * cells + 1 : 2 * cells + 2]], cells)
+        squared[d] = jnp.concatenate([squared[d][:cells], lower], axis=0)
+    for d in order:
+        total = mul(squared[d], scaled[d][:cells].T)
+        va, vb = first[d][2 * cells :], last[d][2 * cells :]
+        square = first[d][cells : 2 * cells] + total[:cells]
         out_ref = out_refs[d]
-        out_ref[0:cells] = moved[:cells]
+        out_ref[0:cells] = moved[d][:cells]
         out_ref[cells:-ROWS] = pack(square)
         out_ref[-ROWS:] = stack_rows(
             [
-                moved[cells : cells + 1] + vb[0:1],
+                moved[d][cells : cells + 1] + vb[0:1],
                 total[cells : cells + 1] + va[1:2],
                 va[2:3],
                 vb[3:4],

time: 25.3 us -> 24.8 us (0.980)
  Pallas kernels: 8.97 us -> 7.88 us
  waiting for transfers between devices: 6.83 us -> 7.33 us
    ppermute x9, waiting for transfers between devices: 6.83 us -> 7.33 us  [send(): lax.ppermute(x, AXIS, [(i, i ^ distance) for i in range(lax.axis_size(AXI...]
    pallas_call x1, Pallas kernels: 2.68 us -> 2.18 us  [on_device(): pl.pallas_call(first_kernel, out_shape=(pltpu.VMEM(map_shape, F32), pltpu...]
    pallas_call x1, Pallas kernels: 1.28 us -> 0.79 us  [on_device(): pl.pallas_call(second_kernel, out_shape=jax.ShapeDtypeStruct(map_shape, F...]
  transfers between devices with their start and end apart: 9 -> 9, of which waited for: 7 -> 8; matrix products, arithmetic and copies ran while one was open for 0% -> 0% of each run, Pallas kernels for 18% -> 16%
where the time goes in v4:
time: 24.8 us; the launch traced here: 24.6 us
  starting transfers between devices  8.72 us (35%)
  Pallas kernels  7.88 us (32%)
  waiting for transfers between devices  7.33 us (30%)
  between operations  0.67 us (3%)
    ppermute x9, starting transfers between devices, send(): lax.ppermute(x, AXIS, [(i, i ^ distance) for i in range(lax.axis_size(AXI...  8.72 us
    ppermute x9, waiting for transfers between devices, send(): lax.ppermute(x, AXIS, [(i, i ^ distance) for i in range(lax.axis_size(AXI...  7.33 us
    pallas_call x1, Pallas kernels, on_device(): pl.pallas_call(response_kernel, out_shape=(jax.ShapeDtypeStruct((blocks,...  2.58 us
    pallas_call x1, Pallas kernels, on_device(): pl.pallas_call(first_kernel, out_shape=(pltpu.VMEM(map_shape, F32), pltpu...  2.18 us
    pallas_call x1, Pallas kernels, on_device(): pl.pallas_call(finish_kernel, out_shape=(shape, shape), in_specs=[VMEM] *...  1.13 us
    pallas_call x1, Pallas kernels, on_device(): pl.pallas_call(second_kernel, out_shape=jax.ShapeDtypeStruct(map_shape, F...  0.79 us
    pallas_call x1, Pallas kernels, on_device(): pl.pallas_call(functools.partial(chain_kernel, grouped), out_shape=(end,)...  0.63 us
    pallas_call x1, Pallas kernels, on_device(): pl.pallas_call(merge_kernel, out_shape=(node,) * half, in_specs=[VMEM, VM...  0.57 us
  transfers between devices with their start and end apart: 9, of which 8 were waited for; matrix products, arithmetic and copies ran while one was open for 0% of the time, Pallas kernels for 16%

profile of v4, /device:TPU:0, one launch (start us, length us, event | category | flops | bytes accessed | tf_op | source)
XLA Modules:
  0.0 24.6 jit_solution(9177063474421622893)
XLA Ops:
  0.6 2.2 %shard_map.77 = (f32[4,264,128]{2,1,0:T(8,128)S(1)}, f32[10,8,128]{2,1,0:T(8,128)S(1)}, f32[4,8,128,128]{3,2,1,0:T(8,128)S(1)}) custom-call(f32[4]{0:T(128)} %k_hbm.1, s32[4,8,128]{2,1,0:T(8,128)} %mat_hbm.1, s32[4,8,128]{2,1,0:T(8,128)} %fin_hbm.1, f32[4,8,128]{2,1,0:T(8,128)} %res_hbm.1, f32[4,8,128,128]{3,2,1,0:T(8,128)} %g_hbm.1), custom_call_target="tpu_custom_call" | custom-call | flops 805306368 | bytes 2097152 | tf_op jit(solution)/shard_map/pallas_call | solution.py:454
  2.8 0.5 %collective-permute-start = (f32[4,264,128]{2,1,0:T(8,128)S(1)}, f32[4,264,128]{2,1,0:T(8,128)S(1)}, u32[]{:S(2)}, u32[]{:S(2)}) collective-permute-start(f32[4,264,128]{2,1,0:T(8,128)S(1)} %get-tuple-element.17.give_ref), channel_id=1, source_target_pairs={{0,4},{4,0},{8,12},{12,8},{16,20},{20,16},{24,28},{28,24},{1,5},{5... | collective-permute-start | bytes 1622024 | tf_op jit(solution)/shard_map/ppermute | solution.py:390
  3.3 0.8 %shard_map.78.keep_ref = f32[4,264,128]{2,1,0:T(8,128)S(1)} custom-call(f32[10,8,128]{2,1,0:T(8,128)S(1)} %get-tuple-element.15.coef_ref, f32[4,8,128,128]{3,2,1,0:T(8,128)S(1)} %get-tuple-element.16.g_ref), custom_call_target="tpu_custom_call" | custom-call | flops 805306368 | bytes 2097152 | tf_op jit(solution)/shard_map/pallas_call | solution.py:472
  4.1 0.1 collective-permute-start.1
  4.3 0.6 %collective-permute-done.got_ref = f32[4,264,128]{2,1,0:T(8,128)S(1)} collective-permute-done((f32[4,264,128]{2,1,0:T(8,128)S(1)}, f32[4,264,128]{2,1,0:T(8,128)S(1)}, u32[]{:S(2)}, u32[]{:S(2)}) %collective-permute-start) | collective-permute-done | bytes 540704 | tf_op jit(solution)/shard_map/ppermute | solution.py:390
  4.9 0.6 %shard_map.80 = (f32[200,128]{1,0:T(8,128)S(1)}, f32[200,128]{1,0:T(8,128)S(1)}, f32[200,128]{1,0:T(8,128)S(1)}, f32[200,128]{1,0:T(8,128)S(1)}) custom-call(f32[4,264,128]{2,1,0:T(8,128)S(1)} %shard_map.78.keep_ref, f32[4,264,128]{2,1,0:T(8,128)S(1)} %collective-permute-done.got_ref), custom_call_target="tpu_custom_call" | custom-call | flops 201326592 | bytes 1622016 | tf_op jit(solution)/shard_map/pallas_call | solution.py:494
  5.5 3.9 %collective-permute-start.2 = (f32[200,128]{1,0:T(8,128)S(1)}, f32[200,128]{1,0:T(8,128)S(1)}, u32[]{:S(2)}, u32[]{:S(2)}) collective-permute-start(f32[200,128]{1,0:T(8,128)S(1)} %get-tuple-element.19), channel_id=1, source_target_pairs={{0,24},{4,28},{8,16},{12,20},{16,8},{20,12},{24,0},{28,4},{1,25},{... | collective-permute-start | bytes 307208 | tf_op jit(solution)/shard_map/ppermute | solution.py:390
  9.4 0.5 %collective-permute-start.3 = (f32[200,128]{1,0:T(8,128)S(1)}, f32[200,128]{1,0:T(8,128)S(1)}, u32[]{:S(2)}, u32[]{:S(2)}) collective-permute-start(f32[200,128]{1,0:T(8,128)S(1)} %get-tuple-element.20), channel_id=1, source_target_pairs={{0,16},{4,20},{8,24},{12,28},{16,0},{20,4},{24,8},{28,12},{1,17},{... | collective-permute-start | bytes 307208 | tf_op jit(solution)/shard_map/ppermute | solution.py:390
  9.9 0.0 copy-start
  9.9 0.1 collective-permute-start.4
  10.0 0.0 collective-permute-done.1.gain_ref
  10.0 2.6 %shard_map.79 = (f32[4,8,256,128]{3,2,1,0:T(8,128)S(1)}, f32[4,8,8,128]{3,2,1,0:T(8,128)S(1)}) custom-call(f32[10,8,128]{2,1,0:T(8,128)S(1)} %get-tuple-element.15.coef_ref, f32[4,264,128]{2,1,0:T(8,128)S(1)} %shard_map.78.keep_ref, f32[4,264,128]{2,1,0:T(8,128)S(1)} %collective-permute-done.got_ref, f32[4,264,128]{2,1,0:T(8,128)S(1)} %get-tuple-element.17.give_ref, ...), custom_call_target="tpu_custom_call" | custom-call | flops 3221225472 | bytes 8388608 | tf_op jit(solution)/shard_map/pallas_call | solution.py:481
  12.6 0.1 collective-permute-done.2.refs_1_
  12.6 2.1 %collective-permute-done.3.refs_2_ = f32[200,128]{1,0:T(8,128)S(1)} collective-permute-done((f32[200,128]{1,0:T(8,128)S(1)}, f32[200,128]{1,0:T(8,128)S(1)}, u32[]{:S(2)}, u32[]{:S(2)}) %collective-permute-start.3) | collective-permute-done | bytes 102432 | tf_op jit(solution)/shard_map/ppermute | solution.py:390
  14.7 0.2 collective-permute-done.4.refs_3_
  15.0 0.6 %shard_map.81 = (f32[8,128]{1,0:T(8,128)S(1)}, f32[8,128]{1,0:T(8,128)S(1)}, f32[8,128]{1,0:T(8,128)S(1)}, f32[8,128]{1,0:T(8,128)S(1)}) custom-call(f32[4,8,8,128]{3,2,1,0:T(8,128)S(1)} %get-tuple-element.18.refs_0_.const_ref, f32[200,128]{1,0:T(8,128)S(1)} %collective-permute-done.2.refs_1_, f32[200,128]{1,0:T(8,128)S(1)} %collective-permute-done.3.refs_2_, ...), custom_call_target="tpu_custom_call" | custom-call | flops 524288 | bytes 540672 | tf_op jit(solution)/shard_map/pallas_call | solution.py:510
  15.6 1.6 %collective-permute-start.5 = (f32[8,128]{1,0:T(8,128)S(1)}, f32[8,128]{1,0:T(8,128)S(1)}, u32[]{:S(2)}, u32[]{:S(2)}) collective-permute-start(f32[8,128]{1,0:T(8,128)S(1)} %get-tuple-element.23), channel_id=1, source_target_pairs={{0,24},{4,28},{8,16},{12,20},{16,8},{20,12},{24,0},{28,4},{1,25},{... | collective-permute-start | bytes 12296 | tf_op jit(solution)/shard_map/ppermute | solution.py:390
  17.3 1.4 %collective-permute-start.6 = (f32[8,128]{1,0:T(8,128)S(1)}, f32[8,128]{1,0:T(8,128)S(1)}, u32[]{:S(2)}, u32[]{:S(2)}) collective-permute-start(f32[8,128]{1,0:T(8,128)S(1)} %get-tuple-element.24), channel_id=1, source_target_pairs={{0,16},{4,20},{8,24},{12,28},{16,0},{20,4},{24,8},{28,12},{1,17},{... | collective-permute-start | bytes 12296 | tf_op jit(solution)/shard_map/ppermute | solution.py:390
  18.7 0.5 %collective-permute-start.7 = (f32[8,128]{1,0:T(8,128)S(1)}, f32[8,128]{1,0:T(8,128)S(1)}, u32[]{:S(2)}, u32[]{:S(2)}) collective-permute-start(f32[8,128]{1,0:T(8,128)S(1)} %get-tuple-element.25), channel_id=1, source_target_pairs={{0,8},{4,12},{8,0},{12,4},{16,24},{20,28},{24,16},{28,20},{1,9},{5... | collective-permute-start | bytes 12296 | tf_op jit(solution)/shard_map/ppermute | solution.py:390
  19.2 1.0 %collective-permute-done.5.refs_0_ = f32[8,128]{1,0:T(8,128)S(1)} collective-permute-done((f32[8,128]{1,0:T(8,128)S(1)}, f32[8,128]{1,0:T(8,128)S(1)}, u32[]{:S(2)}, u32[]{:S(2)}) %collective-permute-start.5) | collective-permute-done | bytes 4128 | tf_op jit(solution)/shard_map/ppermute | solution.py:390
  20.2 0.7 %collective-permute-done.6.refs_1_ = f32[8,128]{1,0:T(8,128)S(1)} collective-permute-done((f32[8,128]{1,0:T(8,128)S(1)}, f32[8,128]{1,0:T(8,128)S(1)}, u32[]{:S(2)}, u32[]{:S(2)}) %collective-permute-start.6) | collective-permute-done | bytes 4128 | tf_op jit(solution)/shard_map/ppermute | solution.py:390
  20.9 1.4 %collective-permute-done.7.refs_2_ = f32[8,128]{1,0:T(8,128)S(1)} collective-permute-done((f32[8,128]{1,0:T(8,128)S(1)}, f32[8,128]{1,0:T(8,128)S(1)}, u32[]{:S(2)}, u32[]{:S(2)}) %collective-permute-start.7) | collective-permute-done | bytes 4128 | tf_op jit(solution)/shard_map/ppermute | solution.py:390
  22.3 0.0 collective-permute-start.8
  22.3 1.2 %collective-permute-done.8.theirs_ref = f32[4,8,128]{2,1,0:T(8,128)S(1)} collective-permute-done((f32[4,8,128]{2,1,0:T(8,128)S(1)}, f32[4,8,128]{2,1,0:T(8,128)S(1)}, u32[]{:S(2)}, u32[]{:S(2)}) %collective-permute-start.8) | collective-permute-done | bytes 16416 | tf_op jit(solution)/shard_map/ppermute | solution.py:390
  23.5 0.0 copy-done
  23.5 1.1 %shard_map.83 = (f32[4,8,128]{2,1,0:T(8,128)}, f32[4,8,128]{2,1,0:T(8,128)}) custom-call(f32[4,8,128]{2,1,0:T(8,128)S(1)} %shard_map.82.mine_ref, f32[4,8,128]{2,1,0:T(8,128)S(1)} %collective-permute-done.8.theirs_ref, s32[4,8,128]{2,1,0:T(8,128)S(1)} %copy-done, f32[4,8,256,128]{3,2,1,0:T(8,128)S(1)} %get-tuple-element.27.out_ref, ...), custom_call_target="tpu_custom_call" | custom-call | flops 2097152 | bytes 4194304 | tf_op jit(solution)/shard_map/pallas_call | solution.py:530
  (1 shorter events, 0.0 us)
Async XLA Ops:
  2.8 2.1 %collective-permute-start = (f32[4,264,128]{2,1,0:T(8,128)S(1)}, f32[4,264,128]{2,1,0:T(8,128)S(1)}, u32[]{:S(2)}, u32[]{:S(2)}) collective-permute-start(f32[4,264,128]{2,1,0:T(8,128)S(1)} %get-tuple-element.17.give_ref), channel_id=1, source_target_pairs={{0,4},{4,0},{8,12},{12,8},{16,20},{20,16},{24,28},{28,24},{1,5},{5... | collective-permute-start | bytes 1622024 | tf_op jit(solution)/shard_map/ppermute | solution.py:390
  4.1 5.9 %collective-permute-start.1 = (f32[4,264,128]{2,1,0:T(8,128)S(1)}, f32[4,264,128]{2,1,0:T(8,128)S(1)}, u32[]{:S(2)}, u32[]{:S(2)}) collective-permute-start(f32[4,264,128]{2,1,0:T(8,128)S(1)} %shard_map.78.keep_ref), channel_id=1, source_target_pairs={{0,4},{4,0},{8,12},{12,8},{16,20},{20,16},{24,28},{28,24},{1,5},{5... | collective-permute-start | bytes 1622024 | tf_op jit(solution)/shard_map/ppermute | solution.py:390
  5.5 7.2 %collective-permute-start.2 = (f32[200,128]{1,0:T(8,128)S(1)}, f32[200,128]{1,0:T(8,128)S(1)}, u32[]{:S(2)}, u32[]{:S(2)}) collective-permute-start(f32[200,128]{1,0:T(8,128)S(1)} %get-tuple-element.19), channel_id=1, source_target_pairs={{0,24},{4,28},{8,16},{12,20},{16,8},{20,12},{24,0},{28,4},{1,25},{... | collective-permute-start | bytes 307208 | tf_op jit(solution)/shard_map/ppermute | solution.py:390
  9.4 5.4 %collective-permute-start.3 = (f32[200,128]{1,0:T(8,128)S(1)}, f32[200,128]{1,0:T(8,128)S(1)}, u32[]{:S(2)}, u32[]{:S(2)}) collective-permute-start(f32[200,128]{1,0:T(8,128)S(1)} %get-tuple-element.20), channel_id=1, source_target_pairs={{0,16},{4,20},{8,24},{12,28},{16,0},{20,4},{24,8},{28,12},{1,17},{... | collective-permute-start | bytes 307208 | tf_op jit(solution)/shard_map/ppermute | solution.py:390
  9.9 13.6 %copy-start = (s32[4,8,128]{2,1,0:T(8,128)S(1)}, s32[4,8,128]{2,1,0:T(8,128)}, u32[]{:S(2)}) copy-start(s32[4,8,128]{2,1,0:T(8,128)} %phase_ref.1) | copy-start | bytes 49156
  9.9 5.1 %collective-permute-start.4 = (f32[200,128]{1,0:T(8,128)S(1)}, f32[200,128]{1,0:T(8,128)S(1)}, u32[]{:S(2)}, u32[]{:S(2)}) collective-permute-start(f32[200,128]{1,0:T(8,128)S(1)} %get-tuple-element.21), channel_id=1, source_target_pairs={{0,8},{4,12},{8,0},{12,4},{16,24},{20,28},{24,16},{28,20},{1,9},{5... | collective-permute-start | bytes 307208 | tf_op jit(solution)/shard_map/ppermute | solution.py:390
  15.6 4.6 %collective-permute-start.5 = (f32[8,128]{1,0:T(8,128)S(1)}, f32[8,128]{1,0:T(8,128)S(1)}, u32[]{:S(2)}, u32[]{:S(2)}) collective-permute-start(f32[8,128]{1,0:T(8,128)S(1)} %get-tuple-element.23), channel_id=1, source_target_pairs={{0,24},{4,28},{8,16},{12,20},{16,8},{20,12},{24,0},{28,4},{1,25},{... | collective-permute-start | bytes 12296 | tf_op jit(solution)/shard_map/ppermute | solution.py:390
  17.3 3.6 %collective-permute-start.6 = (f32[8,128]{1,0:T(8,128)S(1)}, f32[8,128]{1,0:T(8,128)S(1)}, u32[]{:S(2)}, u32[]{:S(2)}) collective-permute-start(f32[8,128]{1,0:T(8,128)S(1)} %get-tuple-element.24), channel_id=1, source_target_pairs={{0,16},{4,20},{8,24},{12,28},{16,0},{20,4},{24,8},{28,12},{1,17},{... | collective-permute-start | bytes 12296 | tf_op jit(solution)/shard_map/ppermute | solution.py:390
  18.7 3.6 %collective-permute-start.7 = (f32[8,128]{1,0:T(8,128)S(1)}, f32[8,128]{1,0:T(8,128)S(1)}, u32[]{:S(2)}, u32[]{:S(2)}) collective-permute-start(f32[8,128]{1,0:T(8,128)S(1)} %get-tuple-element.25), channel_id=1, source_target_pairs={{0,8},{4,12},{8,0},{12,4},{16,24},{20,28},{24,16},{28,20},{1,9},{5... | collective-permute-start | bytes 12296 | tf_op jit(solution)/shard_map/ppermute | solution.py:390
  22.3 1.2 %collective-permute-start.8 = (f32[4,8,128]{2,1,0:T(8,128)S(1)}, f32[4,8,128]{2,1,0:T(8,128)S(1)}, u32[]{:S(2)}, u32[]{:S(2)}) collective-permute-start(f32[4,8,128]{2,1,0:T(8,128)S(1)} %shard_map.82.mine_ref), channel_id=1, source_target_pairs={{0,4},{4,0},{8,12},{12,8},{16,20},{20,16},{24,28},{28,24},{1,5},{5... | collective-permute-start | bytes 49160 | tf_op jit(solution)/shard_map/ppermute | solution.py:390

commit v5 on v4

--- a/solution.py
+++ b/solution.py
@@ -148,10 +148,9 @@
         pltpu.make_async_copy(fin_hbm, ints.at[1], sems.at[2]),
         pltpu.make_async_copy(res_hbm, coef_ref.at[pl.ds(0, blocks)], sems.at[3]),
     ]
-    places = [base + j for j in range(half)] + [half - base + j for j in range(half)]
     large = [
-        pltpu.make_async_copy(g_hbm.at[:, at], g_ref.at[:, at], sems.at[4 + n])
-        for n, at in enumerate(places)
+        pltpu.make_async_copy(g_hbm.at[:, pl.ds(start, half)], g_ref.at[:, pl.ds(start, half)], sems.at[4 + n])
+        for n, start in enumerate((base, half - base))
     ]
     for copy in small + large:
         copy.start()
@@ -170,16 +169,15 @@
     source = [pick(coef_ref[i]) for i in range(blocks)]
     eye = eye_mask(cells)
     wide = []
+    large[0].wait()
     for j in range(half):
-        large[j].wait()
         g0 = g_ref[0, base + j]
         wide.append(jnp.concatenate([g0, stack_rows([times(g0, source[0][j : j + 1], eye)], cells)], axis=0))
     products(
         wide, source, [None] + [pick(f) for f in faces[1:]], lambda i, j: g_ref[i, base + j], out_ref,
         [pick(end) for end in ends],
     )
-    for copy in large[half:]:
-        copy.wait()
+    large[1].wait()
 
 
 def second_kernel(coef_ref, g_ref, out_ref):
@@ -360,21 +358,42 @@
         out_ref[chip ^ d] = refs[count - 1 - d][...]
 
 
-def finish_kernel(mine_ref, theirs_ref, phase_ref, out_ref, const_ref, corr_ref, step_ref, ends_ref):
-    blocks, tiles, cells = corr_ref.shape
-    half = tiles // 2
+def finish(ends_ref, start, out_ref, const_ref, put):
+    blocks, _, _, cells = out_ref.shape
+    eye = eye_mask(cells)
+    for j in range(ends_ref.shape[0]):
+        up, down = (
+            jnp.sum(jnp.where(eye, ends_ref[j, n : n + 1], 0.0), axis=1, keepdims=True) for n in range(2)
+        )
+        for i in range(blocks):
+            both = out_ref[i, start + j, 0:cells] * up + out_ref[i, start + j, cells : 2 * cells] * down
+            put(i, j, const_ref[i, start + j, 0:1] + jnp.sum(both, axis=0, keepdims=True))
+
+
+def own_kernel(mine_ref, out_ref, const_ref, done_ref):
+    half = mine_ref.shape[0]
+
+    def put(i, j, row):
+        done_ref[i, j : j + 1] = row
+
+    finish(mine_ref, jnp.where(lax.axis_index(AXIS) % 2 == 1, half, 0), out_ref, const_ref, put)
+
+
+def finish_kernel(theirs_ref, done_ref, phase_ref, out_ref, const_ref, corr_ref, step_ref, rest_ref):
+    half = theirs_ref.shape[0]
     is_second = lax.axis_index(AXIS) % 2 == 1
-    ends_ref[:half] = jnp.where(is_second, theirs_ref[...], mine_ref[...])
-    ends_ref[half:] = jnp.where(is_second, mine_ref[...], theirs_ref[...])
-    eye = eye_mask(cells)
-    for j in range(tiles):
-        up = jnp.sum(jnp.where(eye, ends_ref[j, 0:1], 0.0), axis=1, keepdims=True)
-        down = jnp.sum(jnp.where(eye, ends_ref[j, 1:2], 0.0), axis=1, keepdims=True)
-        for i in range(blocks):
-            both = out_ref[i, j, 0:cells] * up + out_ref[i, j, cells : 2 * cells] * down
-            solved = const_ref[i, j, 0:1] + jnp.sum(both, axis=0, keepdims=True)
-            corr_ref[i, j : j + 1] = solved
-            step_ref[i, j : j + 1] = solved * (1.0 + 2.0 * phase_ref[i, j : j + 1].astype(F32))
+
+    def put(i, j, row):
+        rest_ref[i, j : j + 1] = row
+
+    finish(theirs_ref, jnp.where(is_second, 0, half), out_ref, const_ref, put)
+    for i in range(corr_ref.shape[0]):
+        own, rest = done_ref[i], rest_ref[i]
+        both = jnp.where(
+            is_second, jnp.concatenate([rest, own], axis=0), jnp.concatenate([own, rest], axis=0)
+        )
+        corr_ref[i] = both
+        step_ref[i] = both * (1.0 + 2.0 * phase_ref[i].astype(F32))
 
 
 VMEM = pl.BlockSpec(memory_space=pltpu.VMEM)
@@ -463,7 +482,7 @@
         scratch_shapes=[
             pltpu.SMEM(k_table.shape, F32),
             pltpu.VMEM((2, blocks, tiles, cells), jnp.int32),
-            pltpu.SemaphoreType.DMA((4 + tiles,)),
+            pltpu.SemaphoreType.DMA((6,)),
         ],
         compiler_params=LIMIT,
         cost_estimate=work,
@@ -526,16 +545,26 @@
         cost_estimate=cost(0, 8 * half * ROWS * cells),
     )(*ends[::-1])
     theirs = send(mine, 1)
+    half_shape = (blocks, half, cells)
+    work = cost(2 * blocks * tiles * cells**2, 4 * blocks * tiles * cells**2)
+    done = pl.pallas_call(
+        own_kernel,
+        out_shape=jax.ShapeDtypeStruct(half_shape, F32),
+        in_specs=[VMEM] * 3,
+        out_specs=VMEM,
+        compiler_params=LIMIT,
+        cost_estimate=work,
+    )(mine, responses, constants)
     shape = jax.ShapeDtypeStruct((blocks, tiles, cells), F32)
     return pl.pallas_call(
         finish_kernel,
         out_shape=(shape, shape),
         in_specs=[VMEM] * 5,
         out_specs=(VMEM, VMEM),
-        scratch_shapes=[pltpu.VMEM((tiles, ROWS, cells), F32)],
-        compiler_params=LIMIT,
-        cost_estimate=cost(4 * blocks * tiles * cells**2, 8 * blocks * tiles * cells**2),
-    )(mine, theirs, phase_mask, responses, constants)
+        scratch_shapes=[pltpu.VMEM(half_shape, F32)],
+        compiler_params=LIMIT,
+        cost_estimate=work,
+    )(theirs, done, phase_mask, responses, constants)
 
 
 def solution(mesh):

time: 24.8 us -> 24.4 us (0.984)
  waiting for transfers between devices: 7.33 us -> 7.06 us
    ppermute x9, waiting for transfers between devices: 7.33 us -> 7.06 us  [send(): lax.ppermute(x, AXIS, [(i, i ^ distance) for i in range(lax.axis_size(AXI...]
    pallas_call x0 -> x1, Pallas kernels: none -> 0.25 us  [on_device(): pl.pallas_call(own_kernel, out_shape=jax.ShapeDtypeStruct(half_shape, F32...]
    pallas_call x1, Pallas kernels: 1.13 us -> 0.88 us  [on_device(): pl.pallas_call(finish_kernel, out_shape=(shape, shape), in_specs=[VMEM] *...]
  transfers between devices with their start and end apart: 9 -> 9, of which waited for: 8 -> 8; matrix products, arithmetic and copies ran while one was open for 0% -> 0% of each run, Pallas kernels for 16% -> 17%
where the time goes in v5:
time: 24.4 us; the launch traced here: 24.3 us
  starting transfers between devices  8.72 us (36%)
  Pallas kernels  7.82 us (32%)
  waiting for transfers between devices  7.06 us (29%)
  between operations  0.69 us (3%)
    ppermute x9, starting transfers between devices, send(): lax.ppermute(x, AXIS, [(i, i ^ distance) for i in range(lax.axis_size(AXI...  8.72 us
    ppermute x9, waiting for transfers between devices, send(): lax.ppermute(x, AXIS, [(i, i ^ distance) for i in range(lax.axis_size(AXI...  7.06 us
    pallas_call x1, Pallas kernels, on_device(): pl.pallas_call(response_kernel, out_shape=(jax.ShapeDtypeStruct((blocks,...  2.58 us
    pallas_call x1, Pallas kernels, on_device(): pl.pallas_call(first_kernel, out_shape=(pltpu.VMEM(map_shape, F32), pltpu...  2.12 us
    pallas_call x1, Pallas kernels, on_device(): pl.pallas_call(finish_kernel, out_shape=(shape, shape), in_specs=[VMEM] *...  0.88 us
    pallas_call x1, Pallas kernels, on_device(): pl.pallas_call(second_kernel, out_shape=jax.ShapeDtypeStruct(map_shape, F...  0.79 us
    pallas_call x1, Pallas kernels, on_device(): pl.pallas_call(functools.partial(chain_kernel, grouped), out_shape=(end,)...  0.63 us
    pallas_call x1, Pallas kernels, on_device(): pl.pallas_call(merge_kernel, out_shape=(node,) * half, in_specs=[VMEM, VM...  0.57 us
  transfers between devices with their start and end apart: 9, of which 8 were waited for; matrix products, arithmetic and copies ran while one was open for 0% of the time, Pallas kernels for 17%

profile of v5, /device:TPU:0, one launch (start us, length us, event | category | flops | bytes accessed | tf_op | source)
XLA Modules:
  0.0 24.3 jit_solution(1773389230456314962)
XLA Ops:
  0.6 2.1 %shard_map.77 = (f32[4,264,128]{2,1,0:T(8,128)S(1)}, f32[10,8,128]{2,1,0:T(8,128)S(1)}, f32[4,8,128,128]{3,2,1,0:T(8,128)S(1)}) custom-call(f32[4]{0:T(128)} %k_hbm.1, s32[4,8,128]{2,1,0:T(8,128)} %mat_hbm.1, s32[4,8,128]{2,1,0:T(8,128)} %fin_hbm.1, f32[4,8,128]{2,1,0:T(8,128)} %res_hbm.1, f32[4,8,128,128]{3,2,1,0:T(8,128)} %g_hbm.1), custom_call_target="tpu_custom_call" | custom-call | flops 805306368 | bytes 2097152 | tf_op jit(solution)/shard_map/pallas_call | solution.py:473
  2.8 0.5 %collective-permute-start = (f32[4,264,128]{2,1,0:T(8,128)S(1)}, f32[4,264,128]{2,1,0:T(8,128)S(1)}, u32[]{:S(2)}, u32[]{:S(2)}) collective-permute-start(f32[4,264,128]{2,1,0:T(8,128)S(1)} %get-tuple-element.17.give_ref), channel_id=1, source_target_pairs={{0,4},{4,0},{8,12},{12,8},{16,20},{20,16},{24,28},{28,24},{1,5},{5... | collective-permute-start | bytes 1622024 | tf_op jit(solution)/shard_map/ppermute | solution.py:409
  3.3 0.8 %shard_map.78.keep_ref = f32[4,264,128]{2,1,0:T(8,128)S(1)} custom-call(f32[10,8,128]{2,1,0:T(8,128)S(1)} %get-tuple-element.15.coef_ref, f32[4,8,128,128]{3,2,1,0:T(8,128)S(1)} %get-tuple-element.16.g_ref), custom_call_target="tpu_custom_call" | custom-call | flops 805306368 | bytes 2097152 | tf_op jit(solution)/shard_map/pallas_call | solution.py:491
  4.1 0.1 collective-permute-start.1
  4.2 0.6 %collective-permute-done.got_ref = f32[4,264,128]{2,1,0:T(8,128)S(1)} collective-permute-done((f32[4,264,128]{2,1,0:T(8,128)S(1)}, f32[4,264,128]{2,1,0:T(8,128)S(1)}, u32[]{:S(2)}, u32[]{:S(2)}) %collective-permute-start) | collective-permute-done | bytes 540704 | tf_op jit(solution)/shard_map/ppermute | solution.py:409
  4.8 0.6 %shard_map.80 = (f32[200,128]{1,0:T(8,128)S(1)}, f32[200,128]{1,0:T(8,128)S(1)}, f32[200,128]{1,0:T(8,128)S(1)}, f32[200,128]{1,0:T(8,128)S(1)}) custom-call(f32[4,264,128]{2,1,0:T(8,128)S(1)} %shard_map.78.keep_ref, f32[4,264,128]{2,1,0:T(8,128)S(1)} %collective-permute-done.got_ref), custom_call_target="tpu_custom_call" | custom-call | flops 201326592 | bytes 1622016 | tf_op jit(solution)/shard_map/pallas_call | solution.py:513
  5.4 3.9 %collective-permute-start.2 = (f32[200,128]{1,0:T(8,128)S(1)}, f32[200,128]{1,0:T(8,128)S(1)}, u32[]{:S(2)}, u32[]{:S(2)}) collective-permute-start(f32[200,128]{1,0:T(8,128)S(1)} %get-tuple-element.19), channel_id=1, source_target_pairs={{0,24},{4,28},{8,16},{12,20},{16,8},{20,12},{24,0},{28,4},{1,25},{... | collective-permute-start | bytes 307208 | tf_op jit(solution)/shard_map/ppermute | solution.py:409
  9.3 0.5 %collective-permute-start.3 = (f32[200,128]{1,0:T(8,128)S(1)}, f32[200,128]{1,0:T(8,128)S(1)}, u32[]{:S(2)}, u32[]{:S(2)}) collective-permute-start(f32[200,128]{1,0:T(8,128)S(1)} %get-tuple-element.20), channel_id=1, source_target_pairs={{0,16},{4,20},{8,24},{12,28},{16,0},{20,4},{24,8},{28,12},{1,17},{... | collective-permute-start | bytes 307208 | tf_op jit(solution)/shard_map/ppermute | solution.py:409
  9.8 0.1 collective-permute-start.4
  9.9 0.0 collective-permute-done.1.gain_ref
  9.9 2.6 %shard_map.79 = (f32[4,8,256,128]{3,2,1,0:T(8,128)S(1)}, f32[4,8,8,128]{3,2,1,0:T(8,128)S(1)}) custom-call(f32[10,8,128]{2,1,0:T(8,128)S(1)} %get-tuple-element.15.coef_ref, f32[4,264,128]{2,1,0:T(8,128)S(1)} %shard_map.78.keep_ref, f32[4,264,128]{2,1,0:T(8,128)S(1)} %collective-permute-done.got_ref, f32[4,264,128]{2,1,0:T(8,128)S(1)} %get-tuple-element.17.give_ref, ...), custom_call_target="tpu_custom_call" | custom-call | flops 3221225472 | bytes 8388608 | tf_op jit(solution)/shard_map/pallas_call | solution.py:500
  12.5 0.1 collective-permute-done.2.refs_1_
  12.6 2.1 %collective-permute-done.3.refs_2_ = f32[200,128]{1,0:T(8,128)S(1)} collective-permute-done((f32[200,128]{1,0:T(8,128)S(1)}, f32[200,128]{1,0:T(8,128)S(1)}, u32[]{:S(2)}, u32[]{:S(2)}) %collective-permute-start.3) | collective-permute-done | bytes 102432 | tf_op jit(solution)/shard_map/ppermute | solution.py:409
  14.7 0.2 collective-permute-done.4.refs_3_
  14.9 0.6 %shard_map.81 = (f32[8,128]{1,0:T(8,128)S(1)}, f32[8,128]{1,0:T(8,128)S(1)}, f32[8,128]{1,0:T(8,128)S(1)}, f32[8,128]{1,0:T(8,128)S(1)}) custom-call(f32[4,8,8,128]{3,2,1,0:T(8,128)S(1)} %get-tuple-element.18.refs_0_.const_ref, f32[200,128]{1,0:T(8,128)S(1)} %collective-permute-done.2.refs_1_, f32[200,128]{1,0:T(8,128)S(1)} %collective-permute-done.3.refs_2_, ...), custom_call_target="tpu_custom_call" | custom-call | flops 524288 | bytes 540672 | tf_op jit(solution)/shard_map/pallas_call | solution.py:529
  15.5 1.6 %collective-permute-start.5 = (f32[8,128]{1,0:T(8,128)S(1)}, f32[8,128]{1,0:T(8,128)S(1)}, u32[]{:S(2)}, u32[]{:S(2)}) collective-permute-start(f32[8,128]{1,0:T(8,128)S(1)} %get-tuple-element.23), channel_id=1, source_target_pairs={{0,24},{4,28},{8,16},{12,20},{16,8},{20,12},{24,0},{28,4},{1,25},{... | collective-permute-start | bytes 12296 | tf_op jit(solution)/shard_map/ppermute | solution.py:409
  17.2 1.4 %collective-permute-start.6 = (f32[8,128]{1,0:T(8,128)S(1)}, f32[8,128]{1,0:T(8,128)S(1)}, u32[]{:S(2)}, u32[]{:S(2)}) collective-permute-start(f32[8,128]{1,0:T(8,128)S(1)} %get-tuple-element.24), channel_id=1, source_target_pairs={{0,16},{4,20},{8,24},{12,28},{16,0},{20,4},{24,8},{28,12},{1,17},{... | collective-permute-start | bytes 12296 | tf_op jit(solution)/shard_map/ppermute | solution.py:409
  18.6 0.5 %collective-permute-start.7 = (f32[8,128]{1,0:T(8,128)S(1)}, f32[8,128]{1,0:T(8,128)S(1)}, u32[]{:S(2)}, u32[]{:S(2)}) collective-permute-start(f32[8,128]{1,0:T(8,128)S(1)} %get-tuple-element.25), channel_id=1, source_target_pairs={{0,8},{4,12},{8,0},{12,4},{16,24},{20,28},{24,16},{28,20},{1,9},{5... | collective-permute-start | bytes 12296 | tf_op jit(solution)/shard_map/ppermute | solution.py:409
  19.1 1.0 %collective-permute-done.5.refs_0_ = f32[8,128]{1,0:T(8,128)S(1)} collective-permute-done((f32[8,128]{1,0:T(8,128)S(1)}, f32[8,128]{1,0:T(8,128)S(1)}, u32[]{:S(2)}, u32[]{:S(2)}) %collective-permute-start.5) | collective-permute-done | bytes 4128 | tf_op jit(solution)/shard_map/ppermute | solution.py:409
  20.1 0.7 %collective-permute-done.6.refs_1_ = f32[8,128]{1,0:T(8,128)S(1)} collective-permute-done((f32[8,128]{1,0:T(8,128)S(1)}, f32[8,128]{1,0:T(8,128)S(1)}, u32[]{:S(2)}, u32[]{:S(2)}) %collective-permute-start.6) | collective-permute-done | bytes 4128 | tf_op jit(solution)/shard_map/ppermute | solution.py:409
  20.8 1.4 %collective-permute-done.7.refs_2_ = f32[8,128]{1,0:T(8,128)S(1)} collective-permute-done((f32[8,128]{1,0:T(8,128)S(1)}, f32[8,128]{1,0:T(8,128)S(1)}, u32[]{:S(2)}, u32[]{:S(2)}) %collective-permute-start.7) | collective-permute-done | bytes 4128 | tf_op jit(solution)/shard_map/ppermute | solution.py:409
  22.2 0.0 collective-permute-start.8
  22.2 0.0 copy-start
  22.2 0.3 %shard_map.83.done_ref = f32[4,4,128]{2,1,0:T(4,128)S(1)} custom-call(f32[4,8,128]{2,1,0:T(8,128)S(1)} %shard_map.82.mine_ref, f32[4,8,256,128]{3,2,1,0:T(8,128)S(1)} %get-tuple-element.27.out_ref, f32[4,8,8,128]{3,2,1,0:T(8,128)S(1)} %get-tuple-element.18.refs_0_.const_ref), custom_call_target="tpu_custom_call" | custom-call | flops 1048576 | bytes 2097152 | tf_op jit(solution)/shard_map/pallas_call | solution.py:550
  22.5 0.9 %collective-permute-done.8.theirs_ref = f32[4,8,128]{2,1,0:T(8,128)S(1)} collective-permute-done((f32[4,8,128]{2,1,0:T(8,128)S(1)}, f32[4,8,128]{2,1,0:T(8,128)S(1)}, u32[]{:S(2)}, u32[]{:S(2)}) %collective-permute-start.8) | collective-permute-done | bytes 16416 | tf_op jit(solution)/shard_map/ppermute | solution.py:409
  23.4 0.0 copy-done
  23.4 0.9 %shard_map.84 = (f32[4,8,128]{2,1,0:T(8,128)}, f32[4,8,128]{2,1,0:T(8,128)}) custom-call(f32[4,8,128]{2,1,0:T(8,128)S(1)} %collective-permute-done.8.theirs_ref, f32[4,4,128]{2,1,0:T(4,128)S(1)} %shard_map.83.done_ref, s32[4,8,128]{2,1,0:T(8,128)S(1)} %copy-done, f32[4,8,256,128]{3,2,1,0:T(8,128)S(1)} %get-tuple-element.27.out_ref, ...), custom_call_target="tpu_custom_call" | custom-call | flops 1048576 | bytes 2097152 | tf_op jit(solution)/shard_map/pallas_call | solution.py:559
  (1 shorter events, 0.0 us)
Async XLA Ops:
  2.8 2.1 %collective-permute-start = (f32[4,264,128]{2,1,0:T(8,128)S(1)}, f32[4,264,128]{2,1,0:T(8,128)S(1)}, u32[]{:S(2)}, u32[]{:S(2)}) collective-permute-start(f32[4,264,128]{2,1,0:T(8,128)S(1)} %get-tuple-element.17.give_ref), channel_id=1, source_target_pairs={{0,4},{4,0},{8,12},{12,8},{16,20},{20,16},{24,28},{28,24},{1,5},{5... | collective-permute-start | bytes 1622024 | tf_op jit(solution)/shard_map/ppermute | solution.py:409
  4.1 5.9 %collective-permute-start.1 = (f32[4,264,128]{2,1,0:T(8,128)S(1)}, f32[4,264,128]{2,1,0:T(8,128)S(1)}, u32[]{:S(2)}, u32[]{:S(2)}) collective-permute-start(f32[4,264,128]{2,1,0:T(8,128)S(1)} %shard_map.78.keep_ref), channel_id=1, source_target_pairs={{0,4},{4,0},{8,12},{12,8},{16,20},{20,16},{24,28},{28,24},{1,5},{5... | collective-permute-start | bytes 1622024 | tf_op jit(solution)/shard_map/ppermute | solution.py:409
  5.4 7.2 %collective-permute-start.2 = (f32[200,128]{1,0:T(8,128)S(1)}, f32[200,128]{1,0:T(8,128)S(1)}, u32[]{:S(2)}, u32[]{:S(2)}) collective-permute-start(f32[200,128]{1,0:T(8,128)S(1)} %get-tuple-element.19), channel_id=1, source_target_pairs={{0,24},{4,28},{8,16},{12,20},{16,8},{20,12},{24,0},{28,4},{1,25},{... | collective-permute-start | bytes 307208 | tf_op jit(solution)/shard_map/ppermute | solution.py:409
  9.3 5.4 %collective-permute-start.3 = (f32[200,128]{1,0:T(8,128)S(1)}, f32[200,128]{1,0:T(8,128)S(1)}, u32[]{:S(2)}, u32[]{:S(2)}) collective-permute-start(f32[200,128]{1,0:T(8,128)S(1)} %get-tuple-element.20), channel_id=1, source_target_pairs={{0,16},{4,20},{8,24},{12,28},{16,0},{20,4},{24,8},{28,12},{1,17},{... | collective-permute-start | bytes 307208 | tf_op jit(solution)/shard_map/ppermute | solution.py:409
  9.8 5.1 %collective-permute-start.4 = (f32[200,128]{1,0:T(8,128)S(1)}, f32[200,128]{1,0:T(8,128)S(1)}, u32[]{:S(2)}, u32[]{:S(2)}) collective-permute-start(f32[200,128]{1,0:T(8,128)S(1)} %get-tuple-element.21), channel_id=1, source_target_pairs={{0,8},{4,12},{8,0},{12,4},{16,24},{20,28},{24,16},{28,20},{1,9},{5... | collective-permute-start | bytes 307208 | tf_op jit(solution)/shard_map/ppermute | solution.py:409
  15.5 4.6 %collective-permute-start.5 = (f32[8,128]{1,0:T(8,128)S(1)}, f32[8,128]{1,0:T(8,128)S(1)}, u32[]{:S(2)}, u32[]{:S(2)}) collective-permute-start(f32[8,128]{1,0:T(8,128)S(1)} %get-tuple-element.23), channel_id=1, source_target_pairs={{0,24},{4,28},{8,16},{12,20},{16,8},{20,12},{24,0},{28,4},{1,25},{... | collective-permute-start | bytes 12296 | tf_op jit(solution)/shard_map/ppermute | solution.py:409
  17.2 3.6 %collective-permute-start.6 = (f32[8,128]{1,0:T(8,128)S(1)}, f32[8,128]{1,0:T(8,128)S(1)}, u32[]{:S(2)}, u32[]{:S(2)}) collective-permute-start(f32[8,128]{1,0:T(8,128)S(1)} %get-tuple-element.24), channel_id=1, source_target_pairs={{0,16},{4,20},{8,24},{12,28},{16,0},{20,4},{24,8},{28,12},{1,17},{... | collective-permute-start | bytes 12296 | tf_op jit(solution)/shard_map/ppermute | solution.py:409
  18.6 3.6 %collective-permute-start.7 = (f32[8,128]{1,0:T(8,128)S(1)}, f32[8,128]{1,0:T(8,128)S(1)}, u32[]{:S(2)}, u32[]{:S(2)}) collective-permute-start(f32[8,128]{1,0:T(8,128)S(1)} %get-tuple-element.25), channel_id=1, source_target_pairs={{0,8},{4,12},{8,0},{12,4},{16,24},{20,28},{24,16},{28,20},{1,9},{5... | collective-permute-start | bytes 12296 | tf_op jit(solution)/shard_map/ppermute | solution.py:409
  22.2 1.2 %collective-permute-start.8 = (f32[4,8,128]{2,1,0:T(8,128)S(1)}, f32[4,8,128]{2,1,0:T(8,128)S(1)}, u32[]{:S(2)}, u32[]{:S(2)}) collective-permute-start(f32[4,8,128]{2,1,0:T(8,128)S(1)} %shard_map.82.mine_ref), channel_id=1, source_target_pairs={{0,4},{4,0},{8,12},{12,8},{16,20},{20,16},{24,28},{28,24},{1,5},{5... | collective-permute-start | bytes 49160 | tf_op jit(solution)/shard_map/ppermute | solution.py:409
  22.2 1.2 %copy-start = (s32[4,8,128]{2,1,0:T(8,128)S(1)}, s32[4,8,128]{2,1,0:T(8,128)}, u32[]{:S(2)}) copy-start(s32[4,8,128]{2,1,0:T(8,128)} %phase_ref.1) | copy-start | bytes 49156

commit v6 on v5

--- a/solution.py
+++ b/solution.py
@@ -264,13 +264,13 @@
                     tail[j] = solved * faces[i][at : at + 1]
 
 
-def merge_kernel(keep_ref, got_ref, *out_refs):
+def merge_kernel(order, keep_ref, got_ref, *rest):
     half, height, cells = keep_ref.shape
+    out_refs = rest[-len(order) :]
     here = lax.axis_index(AXIS)
     is_second = here % 2 == 1
     chip = (here % (2 * half)) // 2
     eye = eye_mask(cells)
-    order = list(reversed(range(half)))
     first, last, scaled, between, moved, squared = {}, {}, {}, {}, {}, {}
     for d in order:
         keep, got = keep_ref[chip ^ d], got_ref[chip ^ d]
@@ -289,7 +289,7 @@
         total = mul(squared[d], scaled[d][:cells].T)
         va, vb = first[d][2 * cells :], last[d][2 * cells :]
         square = first[d][cells : 2 * cells] + total[:cells]
-        out_ref = out_refs[d]
+        out_ref = out_refs[order.index(d)]
         out_ref[0:cells] = moved[d][:cells]
         out_ref[cells:-ROWS] = pack(square)
         out_ref[-ROWS:] = stack_rows(
@@ -510,14 +510,20 @@
     )(coef, keep, got, give, gain, inverses)
     short = cells + cells // 2 + ROWS
     node = jax.ShapeDtypeStruct((short, cells), F32)
-    joined = pl.pallas_call(
-        merge_kernel,
-        out_shape=(node,) * half,
-        in_specs=[VMEM, VMEM],
-        out_specs=(VMEM,) * half,
-        compiler_params=LIMIT,
-        cost_estimate=cost(24 * half * cells**3, 3 * half * map_bytes),
-    )(keep, got)
+
+    def join(order, *after):
+        return pl.pallas_call(
+            functools.partial(merge_kernel, order),
+            out_shape=(node,) * len(order),
+            in_specs=[VMEM, VMEM] + [pl.BlockSpec(memory_space=pl.ANY)] * len(after),
+            out_specs=(VMEM,) * len(order),
+            compiler_params=LIMIT,
+            cost_estimate=cost(24 * len(order) * cells**3, 3 * len(order) * map_bytes),
+        )(keep, got, *after)
+
+    near = list(reversed(range(half - 1)))
+    far = join([half - 1])
+    joined = [*far, *join(near, *far)][::-1]
     arrived = send_all(joined)
     grouped = lax.axis_size(AXIS) > tiles
     edge = []

time: 24.4 us -> 24.3 us (level)
  waiting for transfers between devices: 7.06 us -> 6.49 us
  Pallas kernels: 7.82 us -> 8.16 us
    ppermute x9, waiting for transfers between devices: 7.06 us -> 6.49 us  [send(): lax.ppermute(x, AXIS, [(i, i ^ distance) for i in range(lax.axis_size(AXI...]
    pallas_call x1 -> x2, Pallas kernels: 0.57 us -> 0.89 us  [join(): pl.pallas_call(functools.partial(merge_kernel, order), out_shape=(node,)...]
  transfers between devices with their start and end apart: 9 -> 9, of which waited for: 8 -> 7; matrix products, arithmetic and copies ran while one was open for 0% -> 0% of each run, Pallas kernels for 17% -> 19%
where the time goes in v6:
time: 24.3 us; the launch traced here: 24.1 us
  starting transfers between devices  8.76 us (36%)
  Pallas kernels  8.16 us (34%)
  waiting for transfers between devices  6.49 us (27%)
  between operations  0.7 us (3%)
    ppermute x9, starting transfers between devices, send(): lax.ppermute(x, AXIS, [(i, i ^ distance) for i in range(lax.axis_size(AXI...  8.76 us
    ppermute x9, waiting for transfers between devices, send(): lax.ppermute(x, AXIS, [(i, i ^ distance) for i in range(lax.axis_size(AXI...  6.49 us
    pallas_call x1, Pallas kernels, on_device(): pl.pallas_call(response_kernel, out_shape=(jax.ShapeDtypeStruct((blocks,...  2.6 us
    pallas_call x1, Pallas kernels, on_device(): pl.pallas_call(first_kernel, out_shape=(pltpu.VMEM(map_shape, F32), pltpu...  2.12 us
    pallas_call x2, Pallas kernels, join(): pl.pallas_call(functools.partial(merge_kernel, order), out_shape=(node,)...  0.89 us
    pallas_call x1, Pallas kernels, on_device(): pl.pallas_call(finish_kernel, out_shape=(shape, shape), in_specs=[VMEM] *...  0.88 us
    pallas_call x1, Pallas kernels, on_device(): pl.pallas_call(second_kernel, out_shape=jax.ShapeDtypeStruct(map_shape, F...  0.79 us
    pallas_call x1, Pallas kernels, on_device(): pl.pallas_call(functools.partial(chain_kernel, grouped), out_shape=(end,)...  0.63 us
  transfers between devices with their start and end apart: 9, of which 7 were waited for; matrix products, arithmetic and copies ran while one was open for 0% of the time, Pallas kernels for 19%

profile of v6, /device:TPU:0, one launch (start us, length us, event | category | flops | bytes accessed | tf_op | source)
XLA Modules:
  0.0 24.1 jit_solution(3334572161366904908)
XLA Ops:
  0.6 2.1 %shard_map.77 = (f32[4,264,128]{2,1,0:T(8,128)S(1)}, f32[10,8,128]{2,1,0:T(8,128)S(1)}, f32[4,8,128,128]{3,2,1,0:T(8,128)S(1)}) custom-call(f32[4]{0:T(128)} %k_hbm.1, s32[4,8,128]{2,1,0:T(8,128)} %mat_hbm.1, s32[4,8,128]{2,1,0:T(8,128)} %fin_hbm.1, f32[4,8,128]{2,1,0:T(8,128)} %res_hbm.1, f32[4,8,128,128]{3,2,1,0:T(8,128)} %g_hbm.1), custom_call_target="tpu_custom_call" | custom-call | flops 805306368 | bytes 2097152 | tf_op jit(solution)/shard_map/pallas_call | solution.py:473
  2.8 0.5 %collective-permute-start = (f32[4,264,128]{2,1,0:T(8,128)S(1)}, f32[4,264,128]{2,1,0:T(8,128)S(1)}, u32[]{:S(2)}, u32[]{:S(2)}) collective-permute-start(f32[4,264,128]{2,1,0:T(8,128)S(1)} %get-tuple-element.16.give_ref), channel_id=1, source_target_pairs={{0,4},{4,0},{8,12},{12,8},{16,20},{20,16},{24,28},{28,24},{1,5},{5... | collective-permute-start | bytes 1622024 | tf_op jit(solution)/shard_map/ppermute | solution.py:409
  3.3 0.8 %shard_map.78.keep_ref = f32[4,264,128]{2,1,0:T(8,128)S(1)} custom-call(f32[10,8,128]{2,1,0:T(8,128)S(1)} %get-tuple-element.14.coef_ref, f32[4,8,128,128]{3,2,1,0:T(8,128)S(1)} %get-tuple-element.15.g_ref), custom_call_target="tpu_custom_call" | custom-call | flops 805306368 | bytes 2097152 | tf_op jit(solution)/shard_map/pallas_call | solution.py:491
  4.1 0.1 collective-permute-start.1
  4.2 0.6 %collective-permute-done.got_ref = f32[4,264,128]{2,1,0:T(8,128)S(1)} collective-permute-done((f32[4,264,128]{2,1,0:T(8,128)S(1)}, f32[4,264,128]{2,1,0:T(8,128)S(1)}, u32[]{:S(2)}, u32[]{:S(2)}) %collective-permute-start) | collective-permute-done | bytes 540704 | tf_op jit(solution)/shard_map/ppermute | solution.py:409
  4.8 0.4 %shard_map.80.rest_0_ = f32[200,128]{1,0:T(8,128)S(1)} custom-call(f32[4,264,128]{2,1,0:T(8,128)S(1)} %shard_map.78.keep_ref, f32[4,264,128]{2,1,0:T(8,128)S(1)} %collective-permute-done.got_ref), custom_call_target="tpu_custom_call" | custom-call | flops 50331648 | bytes 405504 | tf_op jit(solution)/shard_map/pallas_call | solution.py:515
  5.2 3.9 %collective-permute-start.2 = (f32[200,128]{1,0:T(8,128)S(1)}, f32[200,128]{1,0:T(8,128)S(1)}, u32[]{:S(2)}, u32[]{:S(2)}) collective-permute-start(f32[200,128]{1,0:T(8,128)S(1)} %shard_map.80.rest_0_), channel_id=1, source_target_pairs={{0,24},{4,28},{8,16},{12,20},{16,8},{20,12},{24,0},{28,4},{1,25},{... | collective-permute-start | bytes 307208 | tf_op jit(solution)/shard_map/ppermute | solution.py:409
  9.1 0.5 %shard_map.81 = (f32[200,128]{1,0:T(8,128)S(1)}, f32[200,128]{1,0:T(8,128)S(1)}, f32[200,128]{1,0:T(8,128)S(1)}) custom-call(f32[4,264,128]{2,1,0:T(8,128)S(1)} %shard_map.78.keep_ref, f32[4,264,128]{2,1,0:T(8,128)S(1)} %collective-permute-done.got_ref, f32[200,128]{1,0:T(8,128)S(1)} %shard_map.80.rest_0_), custom_call_target="tpu_custom_call" | custom-call | flops 150994944 | bytes 1216512 | tf_op jit(solution)/shard_map/pallas_call | solution.py:515
  9.6 0.6 %collective-permute-start.3 = (f32[200,128]{1,0:T(8,128)S(1)}, f32[200,128]{1,0:T(8,128)S(1)}, u32[]{:S(2)}, u32[]{:S(2)}) collective-permute-start(f32[200,128]{1,0:T(8,128)S(1)} %get-tuple-element.18), channel_id=1, source_target_pairs={{0,16},{4,20},{8,24},{12,28},{16,0},{20,4},{24,8},{28,12},{1,17},{... | collective-permute-start | bytes 307208 | tf_op jit(solution)/shard_map/ppermute | solution.py:409
  10.2 0.1 collective-permute-start.4
  10.3 0.0 collective-permute-done.1.gain_ref
  10.3 2.6 %shard_map.79 = (f32[4,8,256,128]{3,2,1,0:T(8,128)S(1)}, f32[4,8,8,128]{3,2,1,0:T(8,128)S(1)}) custom-call(f32[10,8,128]{2,1,0:T(8,128)S(1)} %get-tuple-element.14.coef_ref, f32[4,264,128]{2,1,0:T(8,128)S(1)} %shard_map.78.keep_ref, f32[4,264,128]{2,1,0:T(8,128)S(1)} %collective-permute-done.got_ref, f32[4,264,128]{2,1,0:T(8,128)S(1)} %get-tuple-element.16.give_ref, ...), custom_call_target="tpu_custom_call" | custom-call | flops 3221225472 | bytes 8388608 | tf_op jit(solution)/shard_map/pallas_call | solution.py:500
  12.9 1.6 %collective-permute-done.3.refs_2_ = f32[200,128]{1,0:T(8,128)S(1)} collective-permute-done((f32[200,128]{1,0:T(8,128)S(1)}, f32[200,128]{1,0:T(8,128)S(1)}, u32[]{:S(2)}, u32[]{:S(2)}) %collective-permute-start.3) | collective-permute-done | bytes 102432 | tf_op jit(solution)/shard_map/ppermute | solution.py:409
  14.5 0.4 %collective-permute-done.4.refs_3_ = f32[200,128]{1,0:T(8,128)S(1)} collective-permute-done((f32[200,128]{1,0:T(8,128)S(1)}, f32[200,128]{1,0:T(8,128)S(1)}, u32[]{:S(2)}, u32[]{:S(2)}) %collective-permute-start.4) | collective-permute-done | bytes 102432 | tf_op jit(solution)/shard_map/ppermute | solution.py:409
  14.9 0.0 collective-permute-done.2.refs_1_
  14.9 0.6 %shard_map.82 = (f32[8,128]{1,0:T(8,128)S(1)}, f32[8,128]{1,0:T(8,128)S(1)}, f32[8,128]{1,0:T(8,128)S(1)}, f32[8,128]{1,0:T(8,128)S(1)}) custom-call(f32[4,8,8,128]{3,2,1,0:T(8,128)S(1)} %get-tuple-element.17.refs_0_.const_ref, f32[200,128]{1,0:T(8,128)S(1)} %collective-permute-done.2.refs_1_, f32[200,128]{1,0:T(8,128)S(1)} %collective-permute-done.3.refs_2_, ...), custom_call_target="tpu_custom_call" | custom-call | flops 524288 | bytes 540672 | tf_op jit(solution)/shard_map/pallas_call | solution.py:535
  15.5 2.1 %collective-permute-start.5 = (f32[8,128]{1,0:T(8,128)S(1)}, f32[8,128]{1,0:T(8,128)S(1)}, u32[]{:S(2)}, u32[]{:S(2)}) collective-permute-start(f32[8,128]{1,0:T(8,128)S(1)} %get-tuple-element.21), channel_id=1, source_target_pairs={{0,24},{4,28},{8,16},{12,20},{16,8},{20,12},{24,0},{28,4},{1,25},{... | collective-permute-start | bytes 12296 | tf_op jit(solution)/shard_map/ppermute | solution.py:409
  17.6 0.9 %collective-permute-start.6 = (f32[8,128]{1,0:T(8,128)S(1)}, f32[8,128]{1,0:T(8,128)S(1)}, u32[]{:S(2)}, u32[]{:S(2)}) collective-permute-start(f32[8,128]{1,0:T(8,128)S(1)} %get-tuple-element.22), channel_id=1, source_target_pairs={{0,16},{4,20},{8,24},{12,28},{16,0},{20,4},{24,8},{28,12},{1,17},{... | collective-permute-start | bytes 12296 | tf_op jit(solution)/shard_map/ppermute | solution.py:409
  18.4 0.6 %collective-permute-start.7 = (f32[8,128]{1,0:T(8,128)S(1)}, f32[8,128]{1,0:T(8,128)S(1)}, u32[]{:S(2)}, u32[]{:S(2)}) collective-permute-start(f32[8,128]{1,0:T(8,128)S(1)} %get-tuple-element.23), channel_id=1, source_target_pairs={{0,8},{4,12},{8,0},{12,4},{16,24},{20,28},{24,16},{28,20},{1,9},{5... | collective-permute-start | bytes 12296 | tf_op jit(solution)/shard_map/ppermute | solution.py:409
  19.0 1.0 %collective-permute-done.5.refs_0_ = f32[8,128]{1,0:T(8,128)S(1)} collective-permute-done((f32[8,128]{1,0:T(8,128)S(1)}, f32[8,128]{1,0:T(8,128)S(1)}, u32[]{:S(2)}, u32[]{:S(2)}) %collective-permute-start.5) | collective-permute-done | bytes 4128 | tf_op jit(solution)/shard_map/ppermute | solution.py:409
  20.1 1.1 %collective-permute-done.6.refs_1_ = f32[8,128]{1,0:T(8,128)S(1)} collective-permute-done((f32[8,128]{1,0:T(8,128)S(1)}, f32[8,128]{1,0:T(8,128)S(1)}, u32[]{:S(2)}, u32[]{:S(2)}) %collective-permute-start.6) | collective-permute-done | bytes 4128 | tf_op jit(solution)/shard_map/ppermute | solution.py:409
  21.2 0.9 %collective-permute-done.7.refs_2_ = f32[8,128]{1,0:T(8,128)S(1)} collective-permute-done((f32[8,128]{1,0:T(8,128)S(1)}, f32[8,128]{1,0:T(8,128)S(1)}, u32[]{:S(2)}, u32[]{:S(2)}) %collective-permute-start.7) | collective-permute-done | bytes 4128 | tf_op jit(solution)/shard_map/ppermute | solution.py:409
  22.0 0.0 collective-permute-start.8
  22.1 0.0 copy-start
  22.1 0.3 %shard_map.84.done_ref = f32[4,4,128]{2,1,0:T(4,128)S(1)} custom-call(f32[4,8,128]{2,1,0:T(8,128)S(1)} %shard_map.83.mine_ref, f32[4,8,256,128]{3,2,1,0:T(8,128)S(1)} %get-tuple-element.25.out_ref, f32[4,8,8,128]{3,2,1,0:T(8,128)S(1)} %get-tuple-element.17.refs_0_.const_ref), custom_call_target="tpu_custom_call" | custom-call | flops 1048576 | bytes 2097152 | tf_op jit(solution)/shard_map/pallas_call | solution.py:556
  22.3 0.9 %collective-permute-done.8.theirs_ref = f32[4,8,128]{2,1,0:T(8,128)S(1)} collective-permute-done((f32[4,8,128]{2,1,0:T(8,128)S(1)}, f32[4,8,128]{2,1,0:T(8,128)S(1)}, u32[]{:S(2)}, u32[]{:S(2)}) %collective-permute-start.8) | collective-permute-done | bytes 16416 | tf_op jit(solution)/shard_map/ppermute | solution.py:409
  23.2 0.0 copy-done
  23.2 0.9 %shard_map.85 = (f32[4,8,128]{2,1,0:T(8,128)}, f32[4,8,128]{2,1,0:T(8,128)}) custom-call(f32[4,8,128]{2,1,0:T(8,128)S(1)} %collective-permute-done.8.theirs_ref, f32[4,4,128]{2,1,0:T(4,128)S(1)} %shard_map.84.done_ref, s32[4,8,128]{2,1,0:T(8,128)S(1)} %copy-done, f32[4,8,256,128]{3,2,1,0:T(8,128)S(1)} %get-tuple-element.25.out_ref, ...), custom_call_target="tpu_custom_call" | custom-call | flops 1048576 | bytes 2097152 | tf_op jit(solution)/shard_map/pallas_call | solution.py:565
  (1 shorter events, 0.0 us)
Async XLA Ops:
  2.8 2.1 %collective-permute-start = (f32[4,264,128]{2,1,0:T(8,128)S(1)}, f32[4,264,128]{2,1,0:T(8,128)S(1)}, u32[]{:S(2)}, u32[]{:S(2)}) collective-permute-start(f32[4,264,128]{2,1,0:T(8,128)S(1)} %get-tuple-element.16.give_ref), channel_id=1, source_target_pairs={{0,4},{4,0},{8,12},{12,8},{16,20},{20,16},{24,28},{28,24},{1,5},{5... | collective-permute-start | bytes 1622024 | tf_op jit(solution)/shard_map/ppermute | solution.py:409
  4.1 6.2 %collective-permute-start.1 = (f32[4,264,128]{2,1,0:T(8,128)S(1)}, f32[4,264,128]{2,1,0:T(8,128)S(1)}, u32[]{:S(2)}, u32[]{:S(2)}) collective-permute-start(f32[4,264,128]{2,1,0:T(8,128)S(1)} %shard_map.78.keep_ref), channel_id=1, source_target_pairs={{0,4},{4,0},{8,12},{12,8},{16,20},{20,16},{24,28},{28,24},{1,5},{5... | collective-permute-start | bytes 1622024 | tf_op jit(solution)/shard_map/ppermute | solution.py:409
  5.2 9.6 %collective-permute-start.2 = (f32[200,128]{1,0:T(8,128)S(1)}, f32[200,128]{1,0:T(8,128)S(1)}, u32[]{:S(2)}, u32[]{:S(2)}) collective-permute-start(f32[200,128]{1,0:T(8,128)S(1)} %shard_map.80.rest_0_), channel_id=1, source_target_pairs={{0,24},{4,28},{8,16},{12,20},{16,8},{20,12},{24,0},{28,4},{1,25},{... | collective-permute-start | bytes 307208 | tf_op jit(solution)/shard_map/ppermute | solution.py:409
  9.6 4.9 %collective-permute-start.3 = (f32[200,128]{1,0:T(8,128)S(1)}, f32[200,128]{1,0:T(8,128)S(1)}, u32[]{:S(2)}, u32[]{:S(2)}) collective-permute-start(f32[200,128]{1,0:T(8,128)S(1)} %get-tuple-element.18), channel_id=1, source_target_pairs={{0,16},{4,20},{8,24},{12,28},{16,0},{20,4},{24,8},{28,12},{1,17},{... | collective-permute-start | bytes 307208 | tf_op jit(solution)/shard_map/ppermute | solution.py:409
  10.2 4.7 %collective-permute-start.4 = (f32[200,128]{1,0:T(8,128)S(1)}, f32[200,128]{1,0:T(8,128)S(1)}, u32[]{:S(2)}, u32[]{:S(2)}) collective-permute-start(f32[200,128]{1,0:T(8,128)S(1)} %get-tuple-element.19), channel_id=1, source_target_pairs={{0,8},{4,12},{8,0},{12,4},{16,24},{20,28},{24,16},{28,20},{1,9},{5... | collective-permute-start | bytes 307208 | tf_op jit(solution)/shard_map/ppermute | solution.py:409
  15.5 4.6 %collective-permute-start.5 = (f32[8,128]{1,0:T(8,128)S(1)}, f32[8,128]{1,0:T(8,128)S(1)}, u32[]{:S(2)}, u32[]{:S(2)}) collective-permute-start(f32[8,128]{1,0:T(8,128)S(1)} %get-tuple-element.21), channel_id=1, source_target_pairs={{0,24},{4,28},{8,16},{12,20},{16,8},{20,12},{24,0},{28,4},{1,25},{... | collective-permute-start | bytes 12296 | tf_op jit(solution)/shard_map/ppermute | solution.py:409
  17.6 3.6 %collective-permute-start.6 = (f32[8,128]{1,0:T(8,128)S(1)}, f32[8,128]{1,0:T(8,128)S(1)}, u32[]{:S(2)}, u32[]{:S(2)}) collective-permute-start(f32[8,128]{1,0:T(8,128)S(1)} %get-tuple-element.22), channel_id=1, source_target_pairs={{0,16},{4,20},{8,24},{12,28},{16,0},{20,4},{24,8},{28,12},{1,17},{... | collective-permute-start | bytes 12296 | tf_op jit(solution)/shard_map/ppermute | solution.py:409
  18.4 3.6 %collective-permute-start.7 = (f32[8,128]{1,0:T(8,128)S(1)}, f32[8,128]{1,0:T(8,128)S(1)}, u32[]{:S(2)}, u32[]{:S(2)}) collective-permute-start(f32[8,128]{1,0:T(8,128)S(1)} %get-tuple-element.23), channel_id=1, source_target_pairs={{0,8},{4,12},{8,0},{12,4},{16,24},{20,28},{24,16},{28,20},{1,9},{5... | collective-permute-start | bytes 12296 | tf_op jit(solution)/shard_map/ppermute | solution.py:409
  22.0 1.2 %collective-permute-start.8 = (f32[4,8,128]{2,1,0:T(8,128)S(1)}, f32[4,8,128]{2,1,0:T(8,128)S(1)}, u32[]{:S(2)}, u32[]{:S(2)}) collective-permute-start(f32[4,8,128]{2,1,0:T(8,128)S(1)} %shard_map.83.mine_ref), channel_id=1, source_target_pairs={{0,4},{4,0},{8,12},{12,8},{16,20},{20,16},{24,28},{28,24},{1,5},{5... | collective-permute-start | bytes 49160 | tf_op jit(solution)/shard_map/ppermute | solution.py:409
  22.1 1.2 %copy-start = (s32[4,8,128]{2,1,0:T(8,128)S(1)}, s32[4,8,128]{2,1,0:T(8,128)}, u32[]{:S(2)}) copy-start(s32[4,8,128]{2,1,0:T(8,128)} %phase_ref.1) | copy-start | bytes 49156

commit v7 on v6

--- a/solution.py
+++ b/solution.py
@@ -305,49 +305,61 @@
         )
 
 
-def chain_kernel(with_edge, *refs):
-    refs, nodes = refs[1:-1], refs[-1]
+def by_place(parts, chip):
+    step = 1
+    while step < len(parts):
+        swap = (chip & step) != 0
+        parts = [jnp.where(swap, parts[d ^ step], parts[d]) for d in range(len(parts))]
+        step *= 2
+    return parts
+
+
+def chain_kernel(with_edge, count, *refs):
+    refs = refs[1:]
     if with_edge:
         edge_ref, refs = refs[0], refs[1:]
-    count, height, cells = nodes.shape
-    refs, out_refs, ends = refs[count - 1 :: -1], refs[count:-1], refs[-1]
+    refs, out_refs = refs[count - 1 :: -1], refs[count:]
+    height, cells = refs[0].shape
     chip = (lax.axis_index(AXIS) % (2 * count)) // 2
-    for d in range(count):
-        nodes[chip ^ d] = refs[d][...]
     eye = eye_mask(cells)
-    vectors = [nodes[k, height - ROWS :] for k in range(count)]
-    squares = [None] + [
-        unpack(nodes[k, cells : height - ROWS], vectors[k][5:6], pltpu.roll) for k in range(1, count)
-    ]
+
+    def column(row):
+        return jnp.sum(jnp.where(eye, row, 0.0), axis=1, keepdims=True)
+
+    vectors = by_place([ref[height - ROWS :] for ref in refs], chip)
+    maps_t = by_place([ref[0:cells] for ref in refs], chip)
+    packed = by_place([ref[cells : height - ROWS] for ref in refs], chip)
     faces = [None] + [
         face(vectors[k][2:3], vectors[k - 1][3:4], vectors[k][4:5]) for k in range(1, count)
     ]
-    entering, arriving = [None] * count, [None] * count
+    zero = jnp.zeros((1, cells), F32)
+    entering, sideways, arriving = [zero] + [None] * (count - 1), [None] * count, [zero] * count
     leaving = vectors[0][0:1]
     if with_edge:
         entering[0], arriving[-1] = edge_ref[0:1], edge_ref[1:2]
-        leaving = leaving + times_t(nodes[0, 0:cells], entering[0], eye)
+        leaving = leaving + times_t(maps_t[0], entering[0], eye)
     for k in range(1, count):
         entering[k] = faces[k] * leaving
+        sideways[k] = column(entering[k])
         if k < count - 1:
-            leaving = vectors[k][0:1] + times_t(nodes[k, 0:cells], entering[k], eye)
-    heads = [None] + [
-        vectors[k][1:2] + times(squares[k], entering[k], eye) + times_t(squares[k], entering[k], eye)
-        for k in range(1, count)
-    ]
+            leaving = vectors[k][0:1] + jnp.sum(maps_t[k] * sideways[k], axis=0, keepdims=True)
+    carried = arriving[-1] if with_edge else None
     for k in reversed(range(1, count)):
-        head = heads[k]
-        if arriving[k] is not None:
-            head = head + times(nodes[k, 0:cells], arriving[k], eye)
-        arriving[k - 1] = faces[k] * head
-    zero = jnp.zeros((1, cells), F32)
-    for k in range(count):
-        ends[k] = stack_rows(
-            [zero if entering[k] is None else entering[k], zero if arriving[k] is None else arriving[k]],
-            cells,
-        )
+        part = unpack(packed[k], vectors[k][5:6], pltpu.roll)
+        square = part + part.T
+        if (count - k) % 2:
+            terms = square * entering[k]
+            if carried is not None:
+                terms = terms + maps_t[k] * carried
+            carried = column(faces[k]) * (column(vectors[k][1:2]) + jnp.sum(terms, axis=1, keepdims=True))
+            arriving[k - 1] = jnp.sum(jnp.where(eye, carried, 0.0), axis=0, keepdims=True)
+        else:
+            terms = square * sideways[k] + maps_t[k].T * carried
+            carried = faces[k] * (vectors[k][1:2] + jnp.sum(terms, axis=0, keepdims=True))
+            arriving[k - 1] = carried
+    ends = by_place([stack_rows([entering[k], arriving[k]], cells) for k in range(count)], chip)
     for d in range(count):
-        out_refs[d][...] = ends[chip ^ d]
+        out_refs[d][...] = ends[d]
 
 
 def order_kernel(*refs):
@@ -533,11 +545,10 @@
         edge = [outer_edge(ordered, tiles)]
     end = jax.ShapeDtypeStruct((ROWS, cells), F32)
     ends = pl.pallas_call(
-        functools.partial(chain_kernel, grouped),
+        functools.partial(chain_kernel, grouped, half),
         out_shape=(end,) * half,
         in_specs=[pl.BlockSpec(memory_space=pl.ANY)] + [VMEM] * (half + len(edge)),
         out_specs=(VMEM,) * half,
-        scratch_shapes=[pltpu.VMEM((half, ROWS, cells), F32), pltpu.VMEM((half, short, cells), F32)],
         compiler_params=LIMIT,
         cost_estimate=cost(8 * half * cells**2, half * map_bytes),
     )(constants, *edge, *arrived[::-1])

time: 24.3 us -> 24.2 us (level)
  no operation moved by 1% of the time
where the time goes in v7:
time: 24.2 us; the launch traced here: 24 us
  starting transfers between devices  8.76 us (36%)
  Pallas kernels  8.07 us (33%)
  waiting for transfers between devices  6.49 us (27%)
  between operations  0.7 us (3%)
    ppermute x9, starting transfers between devices, send(): lax.ppermute(x, AXIS, [(i, i ^ distance) for i in range(lax.axis_size(AXI...  8.76 us
    ppermute x9, waiting for transfers between devices, send(): lax.ppermute(x, AXIS, [(i, i ^ distance) for i in range(lax.axis_size(AXI...  6.49 us
    pallas_call x1, Pallas kernels, on_device(): pl.pallas_call(response_kernel, out_shape=(jax.ShapeDtypeStruct((blocks,...  2.6 us
    pallas_call x1, Pallas kernels, on_device(): pl.pallas_call(first_kernel, out_shape=(pltpu.VMEM(map_shape, F32), pltpu...  2.12 us
    pallas_call x2, Pallas kernels, join(): pl.pallas_call(functools.partial(merge_kernel, order), out_shape=(node,)...  0.89 us
    pallas_call x1, Pallas kernels, on_device(): pl.pallas_call(finish_kernel, out_shape=(shape, shape), in_specs=[VMEM] *...  0.88 us
    pallas_call x1, Pallas kernels, on_device(): pl.pallas_call(second_kernel, out_shape=jax.ShapeDtypeStruct(map_shape, F...  0.79 us
    pallas_call x1, Pallas kernels, on_device(): pl.pallas_call(functools.partial(chain_kernel, grouped, half), out_shape=...  0.53 us
  transfers between devices with their start and end apart: 9, of which 7 were waited for; matrix products, arithmetic and copies ran while one was open for 0% of the time, Pallas kernels for 19%

profile of v7, /device:TPU:0, one launch (start us, length us, event | category | flops | bytes accessed | tf_op | source)
XLA Modules:
  0.0 24.0 jit_solution(3531627140714611369)
XLA Ops:
  0.6 2.1 %shard_map.77 = (f32[4,264,128]{2,1,0:T(8,128)S(1)}, f32[10,8,128]{2,1,0:T(8,128)S(1)}, f32[4,8,128,128]{3,2,1,0:T(8,128)S(1)}) custom-call(f32[4]{0:T(128)} %k_hbm.1, s32[4,8,128]{2,1,0:T(8,128)} %mat_hbm.1, s32[4,8,128]{2,1,0:T(8,128)} %fin_hbm.1, f32[4,8,128]{2,1,0:T(8,128)} %res_hbm.1, f32[4,8,128,128]{3,2,1,0:T(8,128)} %g_hbm.1), custom_call_target="tpu_custom_call" | custom-call | flops 805306368 | bytes 2097152 | tf_op jit(solution)/shard_map/pallas_call | solution.py:485
  2.8 0.5 %collective-permute-start = (f32[4,264,128]{2,1,0:T(8,128)S(1)}, f32[4,264,128]{2,1,0:T(8,128)S(1)}, u32[]{:S(2)}, u32[]{:S(2)}) collective-permute-start(f32[4,264,128]{2,1,0:T(8,128)S(1)} %get-tuple-element.16.give_ref), channel_id=1, source_target_pairs={{0,4},{4,0},{8,12},{12,8},{16,20},{20,16},{24,28},{28,24},{1,5},{5... | collective-permute-start | bytes 1622024 | tf_op jit(solution)/shard_map/ppermute | solution.py:421
  3.3 0.8 %shard_map.78.keep_ref = f32[4,264,128]{2,1,0:T(8,128)S(1)} custom-call(f32[10,8,128]{2,1,0:T(8,128)S(1)} %get-tuple-element.14.coef_ref, f32[4,8,128,128]{3,2,1,0:T(8,128)S(1)} %get-tuple-element.15.g_ref), custom_call_target="tpu_custom_call" | custom-call | flops 805306368 | bytes 2097152 | tf_op jit(solution)/shard_map/pallas_call | solution.py:503
  4.1 0.1 collective-permute-start.1
  4.2 0.6 %collective-permute-done.got_ref = f32[4,264,128]{2,1,0:T(8,128)S(1)} collective-permute-done((f32[4,264,128]{2,1,0:T(8,128)S(1)}, f32[4,264,128]{2,1,0:T(8,128)S(1)}, u32[]{:S(2)}, u32[]{:S(2)}) %collective-permute-start) | collective-permute-done | bytes 540704 | tf_op jit(solution)/shard_map/ppermute | solution.py:421
  4.8 0.4 %shard_map.80.rest_0_ = f32[200,128]{1,0:T(8,128)S(1)} custom-call(f32[4,264,128]{2,1,0:T(8,128)S(1)} %shard_map.78.keep_ref, f32[4,264,128]{2,1,0:T(8,128)S(1)} %collective-permute-done.got_ref), custom_call_target="tpu_custom_call" | custom-call | flops 50331648 | bytes 405504 | tf_op jit(solution)/shard_map/pallas_call | solution.py:527
  5.2 3.9 %collective-permute-start.2 = (f32[200,128]{1,0:T(8,128)S(1)}, f32[200,128]{1,0:T(8,128)S(1)}, u32[]{:S(2)}, u32[]{:S(2)}) collective-permute-start(f32[200,128]{1,0:T(8,128)S(1)} %shard_map.80.rest_0_), channel_id=1, source_target_pairs={{0,24},{4,28},{8,16},{12,20},{16,8},{20,12},{24,0},{28,4},{1,25},{... | collective-permute-start | bytes 307208 | tf_op jit(solution)/shard_map/ppermute | solution.py:421
  9.1 0.5 %shard_map.81 = (f32[200,128]{1,0:T(8,128)S(1)}, f32[200,128]{1,0:T(8,128)S(1)}, f32[200,128]{1,0:T(8,128)S(1)}) custom-call(f32[4,264,128]{2,1,0:T(8,128)S(1)} %shard_map.78.keep_ref, f32[4,264,128]{2,1,0:T(8,128)S(1)} %collective-permute-done.got_ref, f32[200,128]{1,0:T(8,128)S(1)} %shard_map.80.rest_0_), custom_call_target="tpu_custom_call" | custom-call | flops 150994944 | bytes 1216512 | tf_op jit(solution)/shard_map/pallas_call | solution.py:527
  9.6 0.6 %collective-permute-start.3 = (f32[200,128]{1,0:T(8,128)S(1)}, f32[200,128]{1,0:T(8,128)S(1)}, u32[]{:S(2)}, u32[]{:S(2)}) collective-permute-start(f32[200,128]{1,0:T(8,128)S(1)} %get-tuple-element.18), channel_id=1, source_target_pairs={{0,16},{4,20},{8,24},{12,28},{16,0},{20,4},{24,8},{28,12},{1,17},{... | collective-permute-start | bytes 307208 | tf_op jit(solution)/shard_map/ppermute | solution.py:421
  10.2 0.1 collective-permute-start.4
  10.3 0.0 collective-permute-done.1.gain_ref
  10.3 2.6 %shard_map.79 = (f32[4,8,256,128]{3,2,1,0:T(8,128)S(1)}, f32[4,8,8,128]{3,2,1,0:T(8,128)S(1)}) custom-call(f32[10,8,128]{2,1,0:T(8,128)S(1)} %get-tuple-element.14.coef_ref, f32[4,264,128]{2,1,0:T(8,128)S(1)} %shard_map.78.keep_ref, f32[4,264,128]{2,1,0:T(8,128)S(1)} %collective-permute-done.got_ref, f32[4,264,128]{2,1,0:T(8,128)S(1)} %get-tuple-element.16.give_ref, ...), custom_call_target="tpu_custom_call" | custom-call | flops 3221225472 | bytes 8388608 | tf_op jit(solution)/shard_map/pallas_call | solution.py:512
  12.9 1.6 %collective-permute-done.3.refs_2_ = f32[200,128]{1,0:T(8,128)S(1)} collective-permute-done((f32[200,128]{1,0:T(8,128)S(1)}, f32[200,128]{1,0:T(8,128)S(1)}, u32[]{:S(2)}, u32[]{:S(2)}) %collective-permute-start.3) | collective-permute-done | bytes 102432 | tf_op jit(solution)/shard_map/ppermute | solution.py:421
  14.5 0.4 %collective-permute-done.4.refs_3_ = f32[200,128]{1,0:T(8,128)S(1)} collective-permute-done((f32[200,128]{1,0:T(8,128)S(1)}, f32[200,128]{1,0:T(8,128)S(1)}, u32[]{:S(2)}, u32[]{:S(2)}) %collective-permute-start.4) | collective-permute-done | bytes 102432 | tf_op jit(solution)/shard_map/ppermute | solution.py:421
  14.9 0.0 collective-permute-done.2.refs_1_
  14.9 0.5 %shard_map.82 = (f32[8,128]{1,0:T(8,128)S(1)}, f32[8,128]{1,0:T(8,128)S(1)}, f32[8,128]{1,0:T(8,128)S(1)}, f32[8,128]{1,0:T(8,128)S(1)}) custom-call(f32[4,8,8,128]{3,2,1,0:T(8,128)S(1)} %get-tuple-element.17.refs_0_.const_ref, f32[200,128]{1,0:T(8,128)S(1)} %collective-permute-done.2.refs_1_, f32[200,128]{1,0:T(8,128)S(1)} %collective-permute-done.3.refs_2_, ...), custom_call_target="tpu_custom_call" | custom-call | flops 524288 | bytes 540672 | tf_op jit(solution)/shard_map/pallas_call | solution.py:547
  15.4 2.1 %collective-permute-start.5 = (f32[8,128]{1,0:T(8,128)S(1)}, f32[8,128]{1,0:T(8,128)S(1)}, u32[]{:S(2)}, u32[]{:S(2)}) collective-permute-start(f32[8,128]{1,0:T(8,128)S(1)} %get-tuple-element.21), channel_id=1, source_target_pairs={{0,24},{4,28},{8,16},{12,20},{16,8},{20,12},{24,0},{28,4},{1,25},{... | collective-permute-start | bytes 12296 | tf_op jit(solution)/shard_map/ppermute | solution.py:421
  17.5 0.9 %collective-permute-start.6 = (f32[8,128]{1,0:T(8,128)S(1)}, f32[8,128]{1,0:T(8,128)S(1)}, u32[]{:S(2)}, u32[]{:S(2)}) collective-permute-start(f32[8,128]{1,0:T(8,128)S(1)} %get-tuple-element.22), channel_id=1, source_target_pairs={{0,16},{4,20},{8,24},{12,28},{16,0},{20,4},{24,8},{28,12},{1,17},{... | collective-permute-start | bytes 12296 | tf_op jit(solution)/shard_map/ppermute | solution.py:421
  18.3 0.6 %collective-permute-start.7 = (f32[8,128]{1,0:T(8,128)S(1)}, f32[8,128]{1,0:T(8,128)S(1)}, u32[]{:S(2)}, u32[]{:S(2)}) collective-permute-start(f32[8,128]{1,0:T(8,128)S(1)} %get-tuple-element.23), channel_id=1, source_target_pairs={{0,8},{4,12},{8,0},{12,4},{16,24},{20,28},{24,16},{28,20},{1,9},{5... | collective-permute-start | bytes 12296 | tf_op jit(solution)/shard_map/ppermute | solution.py:421
  19.0 1.0 %collective-permute-done.5.refs_0_ = f32[8,128]{1,0:T(8,128)S(1)} collective-permute-done((f32[8,128]{1,0:T(8,128)S(1)}, f32[8,128]{1,0:T(8,128)S(1)}, u32[]{:S(2)}, u32[]{:S(2)}) %collective-permute-start.5) | collective-permute-done | bytes 4128 | tf_op jit(solution)/shard_map/ppermute | solution.py:421
  20.0 1.1 %collective-permute-done.6.refs_1_ = f32[8,128]{1,0:T(8,128)S(1)} collective-permute-done((f32[8,128]{1,0:T(8,128)S(1)}, f32[8,128]{1,0:T(8,128)S(1)}, u32[]{:S(2)}, u32[]{:S(2)}) %collective-permute-start.6) | collective-permute-done | bytes 4128 | tf_op jit(solution)/shard_map/ppermute | solution.py:421
  21.1 0.9 %collective-permute-done.7.refs_2_ = f32[8,128]{1,0:T(8,128)S(1)} collective-permute-done((f32[8,128]{1,0:T(8,128)S(1)}, f32[8,128]{1,0:T(8,128)S(1)}, u32[]{:S(2)}, u32[]{:S(2)}) %collective-permute-start.7) | collective-permute-done | bytes 4128 | tf_op jit(solution)/shard_map/ppermute | solution.py:421
  22.0 0.0 collective-permute-start.8
  22.0 0.0 copy-start
  22.0 0.3 %shard_map.84.done_ref = f32[4,4,128]{2,1,0:T(4,128)S(1)} custom-call(f32[4,8,128]{2,1,0:T(8,128)S(1)} %shard_map.83.mine_ref, f32[4,8,256,128]{3,2,1,0:T(8,128)S(1)} %get-tuple-element.25.out_ref, f32[4,8,8,128]{3,2,1,0:T(8,128)S(1)} %get-tuple-element.17.refs_0_.const_ref), custom_call_target="tpu_custom_call" | custom-call | flops 1048576 | bytes 2097152 | tf_op jit(solution)/shard_map/pallas_call | solution.py:567
  22.2 0.9 %collective-permute-done.8.theirs_ref = f32[4,8,128]{2,1,0:T(8,128)S(1)} collective-permute-done((f32[4,8,128]{2,1,0:T(8,128)S(1)}, f32[4,8,128]{2,1,0:T(8,128)S(1)}, u32[]{:S(2)}, u32[]{:S(2)}) %collective-permute-start.8) | collective-permute-done | bytes 16416 | tf_op jit(solution)/shard_map/ppermute | solution.py:421
  23.1 0.0 copy-done
  23.1 0.9 %shard_map.85 = (f32[4,8,128]{2,1,0:T(8,128)}, f32[4,8,128]{2,1,0:T(8,128)}) custom-call(f32[4,8,128]{2,1,0:T(8,128)S(1)} %collective-permute-done.8.theirs_ref, f32[4,4,128]{2,1,0:T(4,128)S(1)} %shard_map.84.done_ref, s32[4,8,128]{2,1,0:T(8,128)S(1)} %copy-done, f32[4,8,256,128]{3,2,1,0:T(8,128)S(1)} %get-tuple-element.25.out_ref, ...), custom_call_target="tpu_custom_call" | custom-call | flops 1048576 | bytes 2097152 | tf_op jit(solution)/shard_map/pallas_call | solution.py:576
  (1 shorter events, 0.0 us)
Async XLA Ops:
  2.8 2.1 %collective-permute-start = (f32[4,264,128]{2,1,0:T(8,128)S(1)}, f32[4,264,128]{2,1,0:T(8,128)S(1)}, u32[]{:S(2)}, u32[]{:S(2)}) collective-permute-start(f32[4,264,128]{2,1,0:T(8,128)S(1)} %get-tuple-element.16.give_ref), channel_id=1, source_target_pairs={{0,4},{4,0},{8,12},{12,8},{16,20},{20,16},{24,28},{28,24},{1,5},{5... | collective-permute-start | bytes 1622024 | tf_op jit(solution)/shard_map/ppermute | solution.py:421
  4.1 6.2 %collective-permute-start.1 = (f32[4,264,128]{2,1,0:T(8,128)S(1)}, f32[4,264,128]{2,1,0:T(8,128)S(1)}, u32[]{:S(2)}, u32[]{:S(2)}) collective-permute-start(f32[4,264,128]{2,1,0:T(8,128)S(1)} %shard_map.78.keep_ref), channel_id=1, source_target_pairs={{0,4},{4,0},{8,12},{12,8},{16,20},{20,16},{24,28},{28,24},{1,5},{5... | collective-permute-start | bytes 1622024 | tf_op jit(solution)/shard_map/ppermute | solution.py:421
  5.2 9.6 %collective-permute-start.2 = (f32[200,128]{1,0:T(8,128)S(1)}, f32[200,128]{1,0:T(8,128)S(1)}, u32[]{:S(2)}, u32[]{:S(2)}) collective-permute-start(f32[200,128]{1,0:T(8,128)S(1)} %shard_map.80.rest_0_), channel_id=1, source_target_pairs={{0,24},{4,28},{8,16},{12,20},{16,8},{20,12},{24,0},{28,4},{1,25},{... | collective-permute-start | bytes 307208 | tf_op jit(solution)/shard_map/ppermute | solution.py:421
  9.6 4.9 %collective-permute-start.3 = (f32[200,128]{1,0:T(8,128)S(1)}, f32[200,128]{1,0:T(8,128)S(1)}, u32[]{:S(2)}, u32[]{:S(2)}) collective-permute-start(f32[200,128]{1,0:T(8,128)S(1)} %get-tuple-element.18), channel_id=1, source_target_pairs={{0,16},{4,20},{8,24},{12,28},{16,0},{20,4},{24,8},{28,12},{1,17},{... | collective-permute-start | bytes 307208 | tf_op jit(solution)/shard_map/ppermute | solution.py:421
  10.2 4.7 %collective-permute-start.4 = (f32[200,128]{1,0:T(8,128)S(1)}, f32[200,128]{1,0:T(8,128)S(1)}, u32[]{:S(2)}, u32[]{:S(2)}) collective-permute-start(f32[200,128]{1,0:T(8,128)S(1)} %get-tuple-element.19), channel_id=1, source_target_pairs={{0,8},{4,12},{8,0},{12,4},{16,24},{20,28},{24,16},{28,20},{1,9},{5... | collective-permute-start | bytes 307208 | tf_op jit(solution)/shard_map/ppermute | solution.py:421
  15.4 4.6 %collective-permute-start.5 = (f32[8,128]{1,0:T(8,128)S(1)}, f32[8,128]{1,0:T(8,128)S(1)}, u32[]{:S(2)}, u32[]{:S(2)}) collective-permute-start(f32[8,128]{1,0:T(8,128)S(1)} %get-tuple-element.21), channel_id=1, source_target_pairs={{0,24},{4,28},{8,16},{12,20},{16,8},{20,12},{24,0},{28,4},{1,25},{... | collective-permute-start | bytes 12296 | tf_op jit(solution)/shard_map/ppermute | solution.py:421
  17.5 3.6 %collective-permute-start.6 = (f32[8,128]{1,0:T(8,128)S(1)}, f32[8,128]{1,0:T(8,128)S(1)}, u32[]{:S(2)}, u32[]{:S(2)}) collective-permute-start(f32[8,128]{1,0:T(8,128)S(1)} %get-tuple-element.22), channel_id=1, source_target_pairs={{0,16},{4,20},{8,24},{12,28},{16,0},{20,4},{24,8},{28,12},{1,17},{... | collective-permute-start | bytes 12296 | tf_op jit(solution)/shard_map/ppermute | solution.py:421
  18.3 3.6 %collective-permute-start.7 = (f32[8,128]{1,0:T(8,128)S(1)}, f32[8,128]{1,0:T(8,128)S(1)}, u32[]{:S(2)}, u32[]{:S(2)}) collective-permute-start(f32[8,128]{1,0:T(8,128)S(1)} %get-tuple-element.23), channel_id=1, source_target_pairs={{0,8},{4,12},{8,0},{12,4},{16,24},{20,28},{24,16},{28,20},{1,9},{5... | collective-permute-start | bytes 12296 | tf_op jit(solution)/shard_map/ppermute | solution.py:421
  22.0 1.2 %collective-permute-start.8 = (f32[4,8,128]{2,1,0:T(8,128)S(1)}, f32[4,8,128]{2,1,0:T(8,128)S(1)}, u32[]{:S(2)}, u32[]{:S(2)}) collective-permute-start(f32[4,8,128]{2,1,0:T(8,128)S(1)} %shard_map.83.mine_ref), channel_id=1, source_target_pairs={{0,4},{4,0},{8,12},{12,8},{16,20},{20,16},{24,28},{28,24},{1,5},{5... | collective-permute-start | bytes 49160 | tf_op jit(solution)/shard_map/ppermute | solution.py:421
  22.0 1.2 %copy-start = (s32[4,8,128]{2,1,0:T(8,128)S(1)}, s32[4,8,128]{2,1,0:T(8,128)}, u32[]{:S(2)}) copy-start(s32[4,8,128]{2,1,0:T(8,128)} %phase_ref.1) | copy-start | bytes 49156

commit v8 on v7

--- a/solution.py
+++ b/solution.py
@@ -533,9 +533,9 @@
             cost_estimate=cost(24 * len(order) * cells**3, 3 * len(order) * map_bytes),
         )(keep, got, *after)
 
-    near = list(reversed(range(half - 1)))
     far = join([half - 1])
-    joined = [*far, *join(near, *far)][::-1]
+    near = join(list(reversed(range(1, half - 1))), *far)
+    joined = [*join([0], *near[:1]), *near[::-1], *far]
     arrived = send_all(joined)
     grouped = lax.axis_size(AXIS) > tiles
     edge = []

time: 24.2 us -> 24.2 us (level)
  waiting for transfers between devices: 6.49 us -> 6.11 us
  Pallas kernels: 8.07 us -> 8.42 us
    ppermute x9, waiting for transfers between devices: 6.49 us -> 6.11 us  [send(): lax.ppermute(x, AXIS, [(i, i ^ distance) for i in range(lax.axis_size(AXI...]
    pallas_call x2 -> x3, Pallas kernels: 0.89 us -> 1.25 us  [join(): pl.pallas_call(functools.partial(merge_kernel, order), out_shape=(node,)...]
  transfers between devices with their start and end apart: 9 -> 9, of which waited for: 7 -> 7; matrix products, arithmetic and copies ran while one was open for 0% -> 0% of each run, Pallas kernels for 19% -> 20%
where the time goes in v8:
time: 24.2 us; the launch traced here: 24 us
  starting transfers between devices  8.77 us (36%)
  Pallas kernels  8.42 us (35%)
  waiting for transfers between devices  6.11 us (25%)
  between operations  0.71 us (3%)
    ppermute x9, starting transfers between devices, send(): lax.ppermute(x, AXIS, [(i, i ^ distance) for i in range(lax.axis_size(AXI...  8.77 us
    ppermute x9, waiting for transfers between devices, send(): lax.ppermute(x, AXIS, [(i, i ^ distance) for i in range(lax.axis_size(AXI...  6.11 us
    pallas_call x1, Pallas kernels, on_device(): pl.pallas_call(response_kernel, out_shape=(jax.ShapeDtypeStruct((blocks,...  2.59 us
    pallas_call x1, Pallas kernels, on_device(): pl.pallas_call(first_kernel, out_shape=(pltpu.VMEM(map_shape, F32), pltpu...  2.12 us
    pallas_call x3, Pallas kernels, join(): pl.pallas_call(functools.partial(merge_kernel, order), out_shape=(node,)...  1.25 us
    pallas_call x1, Pallas kernels, on_device(): pl.pallas_call(finish_kernel, out_shape=(shape, shape), in_specs=[VMEM] *...  0.88 us
    pallas_call x1, Pallas kernels, on_device(): pl.pallas_call(second_kernel, out_shape=jax.ShapeDtypeStruct(map_shape, F...  0.79 us
    pallas_call x1, Pallas kernels, on_device(): pl.pallas_call(functools.partial(chain_kernel, grouped, half), out_shape=...  0.52 us
  transfers between devices with their start and end apart: 9, of which 7 were waited for; matrix products, arithmetic and copies ran while one was open for 0% of the time, Pallas kernels for 20%

profile of v8, /device:TPU:0, one launch (start us, length us, event | category | flops | bytes accessed | tf_op | source)
XLA Modules:
  0.0 24.0 jit_solution(1692455767051260063)
XLA Ops:
  0.6 2.1 %shard_map.77 = (f32[4,264,128]{2,1,0:T(8,128)S(1)}, f32[10,8,128]{2,1,0:T(8,128)S(1)}, f32[4,8,128,128]{3,2,1,0:T(8,128)S(1)}) custom-call(f32[4]{0:T(128)} %k_hbm.1, s32[4,8,128]{2,1,0:T(8,128)} %mat_hbm.1, s32[4,8,128]{2,1,0:T(8,128)} %fin_hbm.1, f32[4,8,128]{2,1,0:T(8,128)} %res_hbm.1, f32[4,8,128,128]{3,2,1,0:T(8,128)} %g_hbm.1), custom_call_target="tpu_custom_call" | custom-call | flops 805306368 | bytes 2097152 | tf_op jit(solution)/shard_map/pallas_call | solution.py:485
  2.8 0.5 %collective-permute-start = (f32[4,264,128]{2,1,0:T(8,128)S(1)}, f32[4,264,128]{2,1,0:T(8,128)S(1)}, u32[]{:S(2)}, u32[]{:S(2)}) collective-permute-start(f32[4,264,128]{2,1,0:T(8,128)S(1)} %get-tuple-element.15.give_ref), channel_id=1, source_target_pairs={{0,4},{4,0},{8,12},{12,8},{16,20},{20,16},{24,28},{28,24},{1,5},{5... | collective-permute-start | bytes 1622024 | tf_op jit(solution)/shard_map/ppermute | solution.py:421
  3.3 0.8 %shard_map.78.keep_ref = f32[4,264,128]{2,1,0:T(8,128)S(1)} custom-call(f32[10,8,128]{2,1,0:T(8,128)S(1)} %get-tuple-element.13.coef_ref, f32[4,8,128,128]{3,2,1,0:T(8,128)S(1)} %get-tuple-element.14.g_ref), custom_call_target="tpu_custom_call" | custom-call | flops 805306368 | bytes 2097152 | tf_op jit(solution)/shard_map/pallas_call | solution.py:503
  4.1 0.1 collective-permute-start.1
  4.2 0.6 %collective-permute-done.got_ref = f32[4,264,128]{2,1,0:T(8,128)S(1)} collective-permute-done((f32[4,264,128]{2,1,0:T(8,128)S(1)}, f32[4,264,128]{2,1,0:T(8,128)S(1)}, u32[]{:S(2)}, u32[]{:S(2)}) %collective-permute-start) | collective-permute-done | bytes 540704 | tf_op jit(solution)/shard_map/ppermute | solution.py:421
  4.8 0.4 %shard_map.80.rest_0_ = f32[200,128]{1,0:T(8,128)S(1)} custom-call(f32[4,264,128]{2,1,0:T(8,128)S(1)} %shard_map.78.keep_ref, f32[4,264,128]{2,1,0:T(8,128)S(1)} %collective-permute-done.got_ref), custom_call_target="tpu_custom_call" | custom-call | flops 50331648 | bytes 405504 | tf_op jit(solution)/shard_map/pallas_call | solution.py:527
  5.2 3.9 %collective-permute-start.2 = (f32[200,128]{1,0:T(8,128)S(1)}, f32[200,128]{1,0:T(8,128)S(1)}, u32[]{:S(2)}, u32[]{:S(2)}) collective-permute-start(f32[200,128]{1,0:T(8,128)S(1)} %shard_map.80.rest_0_), channel_id=1, source_target_pairs={{0,24},{4,28},{8,16},{12,20},{16,8},{20,12},{24,0},{28,4},{1,25},{... | collective-permute-start | bytes 307208 | tf_op jit(solution)/shard_map/ppermute | solution.py:421
  9.1 0.5 %shard_map.81 = (f32[200,128]{1,0:T(8,128)S(1)}, f32[200,128]{1,0:T(8,128)S(1)}) custom-call(f32[4,264,128]{2,1,0:T(8,128)S(1)} %shard_map.78.keep_ref, f32[4,264,128]{2,1,0:T(8,128)S(1)} %collective-permute-done.got_ref, f32[200,128]{1,0:T(8,128)S(1)} %shard_map.80.rest_0_), custom_call_target="tpu_custom_call" | custom-call | flops 100663296 | bytes 811008 | tf_op jit(solution)/shard_map/pallas_call | solution.py:527
  9.6 0.6 %collective-permute-start.3 = (f32[200,128]{1,0:T(8,128)S(1)}, f32[200,128]{1,0:T(8,128)S(1)}, u32[]{:S(2)}, u32[]{:S(2)}) collective-permute-start(f32[200,128]{1,0:T(8,128)S(1)} %get-tuple-element.17.rest_0_), channel_id=1, source_target_pairs={{0,16},{4,20},{8,24},{12,28},{16,0},{20,4},{24,8},{28,12},{1,17},{... | collective-permute-start | bytes 307208 | tf_op jit(solution)/shard_map/ppermute | solution.py:421
  10.1 0.1 collective-permute-start.4
  10.3 0.0 collective-permute-done.1.gain_ref
  10.3 2.6 %shard_map.79 = (f32[4,8,256,128]{3,2,1,0:T(8,128)S(1)}, f32[4,8,8,128]{3,2,1,0:T(8,128)S(1)}) custom-call(f32[10,8,128]{2,1,0:T(8,128)S(1)} %get-tuple-element.13.coef_ref, f32[4,264,128]{2,1,0:T(8,128)S(1)} %shard_map.78.keep_ref, f32[4,264,128]{2,1,0:T(8,128)S(1)} %collective-permute-done.got_ref, f32[4,264,128]{2,1,0:T(8,128)S(1)} %get-tuple-element.15.give_ref, ...), custom_call_target="tpu_custom_call" | custom-call | flops 3221225472 | bytes 8388608 | tf_op jit(solution)/shard_map/pallas_call | solution.py:512
  12.9 0.4 %shard_map.82.refs_4_ = f32[200,128]{1,0:T(8,128)S(1)} custom-call(f32[4,264,128]{2,1,0:T(8,128)S(1)} %shard_map.78.keep_ref, f32[4,264,128]{2,1,0:T(8,128)S(1)} %collective-permute-done.got_ref, f32[200,128]{1,0:T(8,128)S(1)} %get-tuple-element.17.rest_0_), custom_call_target="tpu_custom_call" | custom-call | flops 50331648 | bytes 405504 | tf_op jit(solution)/shard_map/pallas_call | solution.py:527
  13.3 0.0 collective-permute-done.2.refs_1_
  13.3 1.2 %collective-permute-done.3.refs_2_ = f32[200,128]{1,0:T(8,128)S(1)} collective-permute-done((f32[200,128]{1,0:T(8,128)S(1)}, f32[200,128]{1,0:T(8,128)S(1)}, u32[]{:S(2)}, u32[]{:S(2)}) %collective-permute-start.3) | collective-permute-done | bytes 102432 | tf_op jit(solution)/shard_map/ppermute | solution.py:421
  14.5 0.3 %collective-permute-done.4.refs_3_ = f32[200,128]{1,0:T(8,128)S(1)} collective-permute-done((f32[200,128]{1,0:T(8,128)S(1)}, f32[200,128]{1,0:T(8,128)S(1)}, u32[]{:S(2)}, u32[]{:S(2)}) %collective-permute-start.4) | collective-permute-done | bytes 102432 | tf_op jit(solution)/shard_map/ppermute | solution.py:421
  14.8 0.5 %shard_map.83 = (f32[8,128]{1,0:T(8,128)S(1)}, f32[8,128]{1,0:T(8,128)S(1)}, f32[8,128]{1,0:T(8,128)S(1)}, f32[8,128]{1,0:T(8,128)S(1)}) custom-call(f32[4,8,8,128]{3,2,1,0:T(8,128)S(1)} %get-tuple-element.16.refs_0_.const_ref, f32[200,128]{1,0:T(8,128)S(1)} %collective-permute-done.2.refs_1_, f32[200,128]{1,0:T(8,128)S(1)} %collective-permute-done.3.refs_2_, ...), custom_call_target="tpu_custom_call" | custom-call | flops 524288 | bytes 540672 | tf_op jit(solution)/shard_map/pallas_call | solution.py:547
  15.3 2.1 %collective-permute-start.5 = (f32[8,128]{1,0:T(8,128)S(1)}, f32[8,128]{1,0:T(8,128)S(1)}, u32[]{:S(2)}, u32[]{:S(2)}) collective-permute-start(f32[8,128]{1,0:T(8,128)S(1)} %get-tuple-element.19), channel_id=1, source_target_pairs={{0,24},{4,28},{8,16},{12,20},{16,8},{20,12},{24,0},{28,4},{1,25},{... | collective-permute-start | bytes 12296 | tf_op jit(solution)/shard_map/ppermute | solution.py:421
  17.4 0.9 %collective-permute-start.6 = (f32[8,128]{1,0:T(8,128)S(1)}, f32[8,128]{1,0:T(8,128)S(1)}, u32[]{:S(2)}, u32[]{:S(2)}) collective-permute-start(f32[8,128]{1,0:T(8,128)S(1)} %get-tuple-element.20), channel_id=1, source_target_pairs={{0,16},{4,20},{8,24},{12,28},{16,0},{20,4},{24,8},{28,12},{1,17},{... | collective-permute-start | bytes 12296 | tf_op jit(solution)/shard_map/ppermute | solution.py:421
  18.3 0.6 %collective-permute-start.7 = (f32[8,128]{1,0:T(8,128)S(1)}, f32[8,128]{1,0:T(8,128)S(1)}, u32[]{:S(2)}, u32[]{:S(2)}) collective-permute-start(f32[8,128]{1,0:T(8,128)S(1)} %get-tuple-element.21), channel_id=1, source_target_pairs={{0,8},{4,12},{8,0},{12,4},{16,24},{20,28},{24,16},{28,20},{1,9},{5... | collective-permute-start | bytes 12296 | tf_op jit(solution)/shard_map/ppermute | solution.py:421
  18.9 1.0 %collective-permute-done.5.refs_0_ = f32[8,128]{1,0:T(8,128)S(1)} collective-permute-done((f32[8,128]{1,0:T(8,128)S(1)}, f32[8,128]{1,0:T(8,128)S(1)}, u32[]{:S(2)}, u32[]{:S(2)}) %collective-permute-start.5) | collective-permute-done | bytes 4128 | tf_op jit(solution)/shard_map/ppermute | solution.py:421
  19.9 1.1 %collective-permute-done.6.refs_1_ = f32[8,128]{1,0:T(8,128)S(1)} collective-permute-done((f32[8,128]{1,0:T(8,128)S(1)}, f32[8,128]{1,0:T(8,128)S(1)}, u32[]{:S(2)}, u32[]{:S(2)}) %collective-permute-start.6) | collective-permute-done | bytes 4128 | tf_op jit(solution)/shard_map/ppermute | solution.py:421
  21.0 0.9 %collective-permute-done.7.refs_2_ = f32[8,128]{1,0:T(8,128)S(1)} collective-permute-done((f32[8,128]{1,0:T(8,128)S(1)}, f32[8,128]{1,0:T(8,128)S(1)}, u32[]{:S(2)}, u32[]{:S(2)}) %collective-permute-start.7) | collective-permute-done | bytes 4128 | tf_op jit(solution)/shard_map/ppermute | solution.py:421
  21.9 0.0 collective-permute-start.8
  22.0 0.0 copy-start
  22.0 0.3 %shard_map.85.done_ref = f32[4,4,128]{2,1,0:T(4,128)S(1)} custom-call(f32[4,8,128]{2,1,0:T(8,128)S(1)} %shard_map.84.mine_ref, f32[4,8,256,128]{3,2,1,0:T(8,128)S(1)} %get-tuple-element.23.out_ref, f32[4,8,8,128]{3,2,1,0:T(8,128)S(1)} %get-tuple-element.16.refs_0_.const_ref), custom_call_target="tpu_custom_call" | custom-call | flops 1048576 | bytes 2097152 | tf_op jit(solution)/shard_map/pallas_call | solution.py:567
  22.2 0.9 %collective-permute-done.8.theirs_ref = f32[4,8,128]{2,1,0:T(8,128)S(1)} collective-permute-done((f32[4,8,128]{2,1,0:T(8,128)S(1)}, f32[4,8,128]{2,1,0:T(8,128)S(1)}, u32[]{:S(2)}, u32[]{:S(2)}) %collective-permute-start.8) | collective-permute-done | bytes 16416 | tf_op jit(solution)/shard_map/ppermute | solution.py:421
  23.1 0.0 copy-done
  23.1 0.9 %shard_map.86 = (f32[4,8,128]{2,1,0:T(8,128)}, f32[4,8,128]{2,1,0:T(8,128)}) custom-call(f32[4,8,128]{2,1,0:T(8,128)S(1)} %collective-permute-done.8.theirs_ref, f32[4,4,128]{2,1,0:T(4,128)S(1)} %shard_map.85.done_ref, s32[4,8,128]{2,1,0:T(8,128)S(1)} %copy-done, f32[4,8,256,128]{3,2,1,0:T(8,128)S(1)} %get-tuple-element.23.out_ref, ...), custom_call_target="tpu_custom_call" | custom-call | flops 1048576 | bytes 2097152 | tf_op jit(solution)/shard_map/pallas_call | solution.py:576
  (1 shorter events, 0.0 us)
Async XLA Ops:
  2.8 2.1 %collective-permute-start = (f32[4,264,128]{2,1,0:T(8,128)S(1)}, f32[4,264,128]{2,1,0:T(8,128)S(1)}, u32[]{:S(2)}, u32[]{:S(2)}) collective-permute-start(f32[4,264,128]{2,1,0:T(8,128)S(1)} %get-tuple-element.15.give_ref), channel_id=1, source_target_pairs={{0,4},{4,0},{8,12},{12,8},{16,20},{20,16},{24,28},{28,24},{1,5},{5... | collective-permute-start | bytes 1622024 | tf_op jit(solution)/shard_map/ppermute | solution.py:421
  4.1 6.2 %collective-permute-start.1 = (f32[4,264,128]{2,1,0:T(8,128)S(1)}, f32[4,264,128]{2,1,0:T(8,128)S(1)}, u32[]{:S(2)}, u32[]{:S(2)}) collective-permute-start(f32[4,264,128]{2,1,0:T(8,128)S(1)} %shard_map.78.keep_ref), channel_id=1, source_target_pairs={{0,4},{4,0},{8,12},{12,8},{16,20},{20,16},{24,28},{28,24},{1,5},{5... | collective-permute-start | bytes 1622024 | tf_op jit(solution)/shard_map/ppermute | solution.py:421
  5.2 8.1 %collective-permute-start.2 = (f32[200,128]{1,0:T(8,128)S(1)}, f32[200,128]{1,0:T(8,128)S(1)}, u32[]{:S(2)}, u32[]{:S(2)}) collective-permute-start(f32[200,128]{1,0:T(8,128)S(1)} %shard_map.80.rest_0_), channel_id=1, source_target_pairs={{0,24},{4,28},{8,16},{12,20},{16,8},{20,12},{24,0},{28,4},{1,25},{... | collective-permute-start | bytes 307208 | tf_op jit(solution)/shard_map/ppermute | solution.py:421
  9.6 4.9 %collective-permute-start.3 = (f32[200,128]{1,0:T(8,128)S(1)}, f32[200,128]{1,0:T(8,128)S(1)}, u32[]{:S(2)}, u32[]{:S(2)}) collective-permute-start(f32[200,128]{1,0:T(8,128)S(1)} %get-tuple-element.17.rest_0_), channel_id=1, source_target_pairs={{0,16},{4,20},{8,24},{12,28},{16,0},{20,4},{24,8},{28,12},{1,17},{... | collective-permute-start | bytes 307208 | tf_op jit(solution)/shard_map/ppermute | solution.py:421
  10.1 4.7 %collective-permute-start.4 = (f32[200,128]{1,0:T(8,128)S(1)}, f32[200,128]{1,0:T(8,128)S(1)}, u32[]{:S(2)}, u32[]{:S(2)}) collective-permute-start(f32[200,128]{1,0:T(8,128)S(1)} %get-tuple-element.18), channel_id=1, source_target_pairs={{0,8},{4,12},{8,0},{12,4},{16,24},{20,28},{24,16},{28,20},{1,9},{5... | collective-permute-start | bytes 307208 | tf_op jit(solution)/shard_map/ppermute | solution.py:421
  15.3 4.6 %collective-permute-start.5 = (f32[8,128]{1,0:T(8,128)S(1)}, f32[8,128]{1,0:T(8,128)S(1)}, u32[]{:S(2)}, u32[]{:S(2)}) collective-permute-start(f32[8,128]{1,0:T(8,128)S(1)} %get-tuple-element.19), channel_id=1, source_target_pairs={{0,24},{4,28},{8,16},{12,20},{16,8},{20,12},{24,0},{28,4},{1,25},{... | collective-permute-start | bytes 12296 | tf_op jit(solution)/shard_map/ppermute | solution.py:421
  17.4 3.6 %collective-permute-start.6 = (f32[8,128]{1,0:T(8,128)S(1)}, f32[8,128]{1,0:T(8,128)S(1)}, u32[]{:S(2)}, u32[]{:S(2)}) collective-permute-start(f32[8,128]{1,0:T(8,128)S(1)} %get-tuple-element.20), channel_id=1, source_target_pairs={{0,16},{4,20},{8,24},{12,28},{16,0},{20,4},{24,8},{28,12},{1,17},{... | collective-permute-start | bytes 12296 | tf_op jit(solution)/shard_map/ppermute | solution.py:421
  18.3 3.6 %collective-permute-start.7 = (f32[8,128]{1,0:T(8,128)S(1)}, f32[8,128]{1,0:T(8,128)S(1)}, u32[]{:S(2)}, u32[]{:S(2)}) collective-permute-start(f32[8,128]{1,0:T(8,128)S(1)} %get-tuple-element.21), channel_id=1, source_target_pairs={{0,8},{4,12},{8,0},{12,4},{16,24},{20,28},{24,16},{28,20},{1,9},{5... | collective-permute-start | bytes 12296 | tf_op jit(solution)/shard_map/ppermute | solution.py:421
  21.9 1.2 %collective-permute-start.8 = (f32[4,8,128]{2,1,0:T(8,128)S(1)}, f32[4,8,128]{2,1,0:T(8,128)S(1)}, u32[]{:S(2)}, u32[]{:S(2)}) collective-permute-start(f32[4,8,128]{2,1,0:T(8,128)S(1)} %shard_map.84.mine_ref), channel_id=1, source_target_pairs={{0,4},{4,0},{8,12},{12,8},{16,20},{20,16},{24,28},{28,24},{1,5},{5... | collective-permute-start | bytes 49160 | tf_op jit(solution)/shard_map/ppermute | solution.py:421
  22.0 1.2 %copy-start = (s32[4,8,128]{2,1,0:T(8,128)S(1)}, s32[4,8,128]{2,1,0:T(8,128)}, u32[]{:S(2)}) copy-start(s32[4,8,128]{2,1,0:T(8,128)} %phase_ref.1) | copy-start | bytes 49156

commit v9 on v8

--- a/solution.py
+++ b/solution.py
@@ -359,7 +359,7 @@
             arriving[k - 1] = carried
     ends = by_place([stack_rows([entering[k], arriving[k]], cells) for k in range(count)], chip)
     for d in range(count):
-        out_refs[d][...] = ends[d]
+        out_refs[d][...] = ends[d][0:2]
 
 
 def order_kernel(*refs):
@@ -543,7 +543,7 @@
         chip = (lax.axis_index(AXIS) % tiles) // 2
         ordered = jnp.stack(arrived)[jnp.arange(half) ^ chip]
         edge = [outer_edge(ordered, tiles)]
-    end = jax.ShapeDtypeStruct((ROWS, cells), F32)
+    end = jax.ShapeDtypeStruct((2, cells), F32)
     ends = pl.pallas_call(
         functools.partial(chain_kernel, grouped, half),
         out_shape=(end,) * half,
@@ -555,7 +555,7 @@
     ends = send_all(ends)
     mine = pl.pallas_call(
         order_kernel,
-        out_shape=jax.ShapeDtypeStruct((half, ROWS, cells), F32),
+        out_shape=jax.ShapeDtypeStruct((half, 2, cells), F32),
         in_specs=[VMEM] * half,
         out_specs=VMEM,
         compiler_params=LIMIT,

time: 24.2 us -> 24.1 us (level)
  no operation moved by 1% of the time
where the time goes in v9:
time: 24.1 us; the launch traced here: 24 us
  starting transfers between devices  8.77 us (36%)
  Pallas kernels  8.42 us (35%)
  waiting for transfers between devices  6.05 us (25%)
  between operations  0.71 us (3%)
    ppermute x9, starting transfers between devices, send(): lax.ppermute(x, AXIS, [(i, i ^ distance) for i in range(lax.axis_size(AXI...  8.77 us
    ppermute x9, waiting for transfers between devices, send(): lax.ppermute(x, AXIS, [(i, i ^ distance) for i in range(lax.axis_size(AXI...  6.05 us
    pallas_call x1, Pallas kernels, on_device(): pl.pallas_call(response_kernel, out_shape=(jax.ShapeDtypeStruct((blocks,...  2.59 us
    pallas_call x1, Pallas kernels, on_device(): pl.pallas_call(first_kernel, out_shape=(pltpu.VMEM(map_shape, F32), pltpu...  2.12 us
    pallas_call x3, Pallas kernels, join(): pl.pallas_call(functools.partial(merge_kernel, order), out_shape=(node,)...  1.25 us
    pallas_call x1, Pallas kernels, on_device(): pl.pallas_call(finish_kernel, out_shape=(shape, shape), in_specs=[VMEM] *...  0.88 us
    pallas_call x1, Pallas kernels, on_device(): pl.pallas_call(second_kernel, out_shape=jax.ShapeDtypeStruct(map_shape, F...  0.79 us
    pallas_call x1, Pallas kernels, on_device(): pl.pallas_call(functools.partial(chain_kernel, grouped, half), out_shape=...  0.52 us
  transfers between devices with their start and end apart: 9, of which 7 were waited for; matrix products, arithmetic and copies ran while one was open for 0% of the time, Pallas kernels for 20%

profile of v9, /device:TPU:0, one launch (start us, length us, event | category | flops | bytes accessed | tf_op | source)
XLA Modules:
  0.0 24.0 jit_solution(17457141455927647021)
XLA Ops:
  0.6 2.1 %shard_map.77 = (f32[4,264,128]{2,1,0:T(8,128)S(1)}, f32[10,8,128]{2,1,0:T(8,128)S(1)}, f32[4,8,128,128]{3,2,1,0:T(8,128)S(1)}) custom-call(f32[4]{0:T(128)} %k_hbm.1, s32[4,8,128]{2,1,0:T(8,128)} %mat_hbm.1, s32[4,8,128]{2,1,0:T(8,128)} %fin_hbm.1, f32[4,8,128]{2,1,0:T(8,128)} %res_hbm.1, f32[4,8,128,128]{3,2,1,0:T(8,128)} %g_hbm.1), custom_call_target="tpu_custom_call" | custom-call | flops 805306368 | bytes 2097152 | tf_op jit(solution)/shard_map/pallas_call | solution.py:485
  2.8 0.5 %collective-permute-start = (f32[4,264,128]{2,1,0:T(8,128)S(1)}, f32[4,264,128]{2,1,0:T(8,128)S(1)}, u32[]{:S(2)}, u32[]{:S(2)}) collective-permute-start(f32[4,264,128]{2,1,0:T(8,128)S(1)} %get-tuple-element.15.give_ref), channel_id=1, source_target_pairs={{0,4},{4,0},{8,12},{12,8},{16,20},{20,16},{24,28},{28,24},{1,5},{5... | collective-permute-start | bytes 1622024 | tf_op jit(solution)/shard_map/ppermute | solution.py:421
  3.3 0.8 %shard_map.78.keep_ref = f32[4,264,128]{2,1,0:T(8,128)S(1)} custom-call(f32[10,8,128]{2,1,0:T(8,128)S(1)} %get-tuple-element.13.coef_ref, f32[4,8,128,128]{3,2,1,0:T(8,128)S(1)} %get-tuple-element.14.g_ref), custom_call_target="tpu_custom_call" | custom-call | flops 805306368 | bytes 2097152 | tf_op jit(solution)/shard_map/pallas_call | solution.py:503
  4.1 0.1 collective-permute-start.1
  4.2 0.6 %collective-permute-done.got_ref = f32[4,264,128]{2,1,0:T(8,128)S(1)} collective-permute-done((f32[4,264,128]{2,1,0:T(8,128)S(1)}, f32[4,264,128]{2,1,0:T(8,128)S(1)}, u32[]{:S(2)}, u32[]{:S(2)}) %collective-permute-start) | collective-permute-done | bytes 540704 | tf_op jit(solution)/shard_map/ppermute | solution.py:421
  4.8 0.4 %shard_map.80.rest_0_ = f32[200,128]{1,0:T(8,128)S(1)} custom-call(f32[4,264,128]{2,1,0:T(8,128)S(1)} %shard_map.78.keep_ref, f32[4,264,128]{2,1,0:T(8,128)S(1)} %collective-permute-done.got_ref), custom_call_target="tpu_custom_call" | custom-call | flops 50331648 | bytes 405504 | tf_op jit(solution)/shard_map/pallas_call | solution.py:527
  5.2 3.9 %collective-permute-start.2 = (f32[200,128]{1,0:T(8,128)S(1)}, f32[200,128]{1,0:T(8,128)S(1)}, u32[]{:S(2)}, u32[]{:S(2)}) collective-permute-start(f32[200,128]{1,0:T(8,128)S(1)} %shard_map.80.rest_0_), channel_id=1, source_target_pairs={{0,24},{4,28},{8,16},{12,20},{16,8},{20,12},{24,0},{28,4},{1,25},{... | collective-permute-start | bytes 307208 | tf_op jit(solution)/shard_map/ppermute | solution.py:421
  9.1 0.5 %shard_map.81 = (f32[200,128]{1,0:T(8,128)S(1)}, f32[200,128]{1,0:T(8,128)S(1)}) custom-call(f32[4,264,128]{2,1,0:T(8,128)S(1)} %shard_map.78.keep_ref, f32[4,264,128]{2,1,0:T(8,128)S(1)} %collective-permute-done.got_ref, f32[200,128]{1,0:T(8,128)S(1)} %shard_map.80.rest_0_), custom_call_target="tpu_custom_call" | custom-call | flops 100663296 | bytes 811008 | tf_op jit(solution)/shard_map/pallas_call | solution.py:527
  9.6 0.6 %collective-permute-start.3 = (f32[200,128]{1,0:T(8,128)S(1)}, f32[200,128]{1,0:T(8,128)S(1)}, u32[]{:S(2)}, u32[]{:S(2)}) collective-permute-start(f32[200,128]{1,0:T(8,128)S(1)} %get-tuple-element.17.rest_0_), channel_id=1, source_target_pairs={{0,16},{4,20},{8,24},{12,28},{16,0},{20,4},{24,8},{28,12},{1,17},{... | collective-permute-start | bytes 307208 | tf_op jit(solution)/shard_map/ppermute | solution.py:421
  10.1 0.1 collective-permute-start.4
  10.3 0.0 collective-permute-done.1.gain_ref
  10.3 2.6 %shard_map.79 = (f32[4,8,256,128]{3,2,1,0:T(8,128)S(1)}, f32[4,8,8,128]{3,2,1,0:T(8,128)S(1)}) custom-call(f32[10,8,128]{2,1,0:T(8,128)S(1)} %get-tuple-element.13.coef_ref, f32[4,264,128]{2,1,0:T(8,128)S(1)} %shard_map.78.keep_ref, f32[4,264,128]{2,1,0:T(8,128)S(1)} %collective-permute-done.got_ref, f32[4,264,128]{2,1,0:T(8,128)S(1)} %get-tuple-element.15.give_ref, ...), custom_call_target="tpu_custom_call" | custom-call | flops 3221225472 | bytes 8388608 | tf_op jit(solution)/shard_map/pallas_call | solution.py:512
  12.9 0.4 %shard_map.82.refs_4_ = f32[200,128]{1,0:T(8,128)S(1)} custom-call(f32[4,264,128]{2,1,0:T(8,128)S(1)} %shard_map.78.keep_ref, f32[4,264,128]{2,1,0:T(8,128)S(1)} %collective-permute-done.got_ref, f32[200,128]{1,0:T(8,128)S(1)} %get-tuple-element.17.rest_0_), custom_call_target="tpu_custom_call" | custom-call | flops 50331648 | bytes 405504 | tf_op jit(solution)/shard_map/pallas_call | solution.py:527
  13.3 0.0 collective-permute-done.2.refs_1_
  13.3 1.2 %collective-permute-done.3.refs_2_ = f32[200,128]{1,0:T(8,128)S(1)} collective-permute-done((f32[200,128]{1,0:T(8,128)S(1)}, f32[200,128]{1,0:T(8,128)S(1)}, u32[]{:S(2)}, u32[]{:S(2)}) %collective-permute-start.3) | collective-permute-done | bytes 102432 | tf_op jit(solution)/shard_map/ppermute | solution.py:421
  14.5 0.3 %collective-permute-done.4.refs_3_ = f32[200,128]{1,0:T(8,128)S(1)} collective-permute-done((f32[200,128]{1,0:T(8,128)S(1)}, f32[200,128]{1,0:T(8,128)S(1)}, u32[]{:S(2)}, u32[]{:S(2)}) %collective-permute-start.4) | collective-permute-done | bytes 102432 | tf_op jit(solution)/shard_map/ppermute | solution.py:421
  14.8 0.5 %shard_map.83 = (f32[2,128]{1,0:T(2,128)S(1)}, f32[2,128]{1,0:T(2,128)S(1)}, f32[2,128]{1,0:T(2,128)S(1)}, f32[2,128]{1,0:T(2,128)S(1)}) custom-call(f32[4,8,8,128]{3,2,1,0:T(8,128)S(1)} %get-tuple-element.16.refs_0_.const_ref, f32[200,128]{1,0:T(8,128)S(1)} %collective-permute-done.2.refs_1_, f32[200,128]{1,0:T(8,128)S(1)} %collective-permute-done.3.refs_2_, ...), custom_call_target="tpu_custom_call" | custom-call | flops 524288 | bytes 540672 | tf_op jit(solution)/shard_map/pallas_call | solution.py:547
  15.3 2.1 %collective-permute-start.5 = (f32[2,128]{1,0:T(2,128)S(1)}, f32[2,128]{1,0:T(2,128)S(1)}, u32[]{:S(2)}, u32[]{:S(2)}) collective-permute-start(f32[2,128]{1,0:T(2,128)S(1)} %get-tuple-element.19), channel_id=1, source_target_pairs={{0,24},{4,28},{8,16},{12,20},{16,8},{20,12},{24,0},{28,4},{1,25},{... | collective-permute-start | bytes 3080 | tf_op jit(solution)/shard_map/ppermute | solution.py:421
  17.4 0.9 %collective-permute-start.6 = (f32[2,128]{1,0:T(2,128)S(1)}, f32[2,128]{1,0:T(2,128)S(1)}, u32[]{:S(2)}, u32[]{:S(2)}) collective-permute-start(f32[2,128]{1,0:T(2,128)S(1)} %get-tuple-element.20), channel_id=1, source_target_pairs={{0,16},{4,20},{8,24},{12,28},{16,0},{20,4},{24,8},{28,12},{1,17},{... | collective-permute-start | bytes 3080 | tf_op jit(solution)/shard_map/ppermute | solution.py:421
  18.3 0.6 %collective-permute-start.7 = (f32[2,128]{1,0:T(2,128)S(1)}, f32[2,128]{1,0:T(2,128)S(1)}, u32[]{:S(2)}, u32[]{:S(2)}) collective-permute-start(f32[2,128]{1,0:T(2,128)S(1)} %get-tuple-element.21), channel_id=1, source_target_pairs={{0,8},{4,12},{8,0},{12,4},{16,24},{20,28},{24,16},{28,20},{1,9},{5... | collective-permute-start | bytes 3080 | tf_op jit(solution)/shard_map/ppermute | solution.py:421
  18.9 1.0 %collective-permute-done.5.refs_0_ = f32[2,128]{1,0:T(2,128)S(1)} collective-permute-done((f32[2,128]{1,0:T(2,128)S(1)}, f32[2,128]{1,0:T(2,128)S(1)}, u32[]{:S(2)}, u32[]{:S(2)}) %collective-permute-start.5) | collective-permute-done | bytes 1056 | tf_op jit(solution)/shard_map/ppermute | solution.py:421
  19.9 1.1 %collective-permute-done.6.refs_1_ = f32[2,128]{1,0:T(2,128)S(1)} collective-permute-done((f32[2,128]{1,0:T(2,128)S(1)}, f32[2,128]{1,0:T(2,128)S(1)}, u32[]{:S(2)}, u32[]{:S(2)}) %collective-permute-start.6) | collective-permute-done | bytes 1056 | tf_op jit(solution)/shard_map/ppermute | solution.py:421
  21.0 0.9 %collective-permute-done.7.refs_2_ = f32[2,128]{1,0:T(2,128)S(1)} collective-permute-done((f32[2,128]{1,0:T(2,128)S(1)}, f32[2,128]{1,0:T(2,128)S(1)}, u32[]{:S(2)}, u32[]{:S(2)}) %collective-permute-start.7) | collective-permute-done | bytes 1056 | tf_op jit(solution)/shard_map/ppermute | solution.py:421
  21.9 0.0 collective-permute-start.8
  21.9 0.0 copy-start
  21.9 0.3 %shard_map.85.done_ref = f32[4,4,128]{2,1,0:T(4,128)S(1)} custom-call(f32[4,2,128]{2,1,0:T(2,128)S(1)} %shard_map.84.mine_ref, f32[4,8,256,128]{3,2,1,0:T(8,128)S(1)} %get-tuple-element.23.out_ref, f32[4,8,8,128]{3,2,1,0:T(8,128)S(1)} %get-tuple-element.16.refs_0_.const_ref), custom_call_target="tpu_custom_call" | custom-call | flops 1048576 | bytes 2097152 | tf_op jit(solution)/shard_map/pallas_call | solution.py:567
  22.2 0.9 %collective-permute-done.8.theirs_ref = f32[4,2,128]{2,1,0:T(2,128)S(1)} collective-permute-done((f32[4,2,128]{2,1,0:T(2,128)S(1)}, f32[4,2,128]{2,1,0:T(2,128)S(1)}, u32[]{:S(2)}, u32[]{:S(2)}) %collective-permute-start.8) | collective-permute-done | bytes 4128 | tf_op jit(solution)/shard_map/ppermute | solution.py:421
  23.1 0.0 copy-done
  23.1 0.9 %shard_map.86 = (f32[4,8,128]{2,1,0:T(8,128)}, f32[4,8,128]{2,1,0:T(8,128)}) custom-call(f32[4,2,128]{2,1,0:T(2,128)S(1)} %collective-permute-done.8.theirs_ref, f32[4,4,128]{2,1,0:T(4,128)S(1)} %shard_map.85.done_ref, s32[4,8,128]{2,1,0:T(8,128)S(1)} %copy-done, f32[4,8,256,128]{3,2,1,0:T(8,128)S(1)} %get-tuple-element.23.out_ref, ...), custom_call_target="tpu_custom_call" | custom-call | flops 1048576 | bytes 2097152 | tf_op jit(solution)/shard_map/pallas_call | solution.py:576
  (1 shorter events, 0.0 us)
Async XLA Ops:
  2.8 2.1 %collective-permute-start = (f32[4,264,128]{2,1,0:T(8,128)S(1)}, f32[4,264,128]{2,1,0:T(8,128)S(1)}, u32[]{:S(2)}, u32[]{:S(2)}) collective-permute-start(f32[4,264,128]{2,1,0:T(8,128)S(1)} %get-tuple-element.15.give_ref), channel_id=1, source_target_pairs={{0,4},{4,0},{8,12},{12,8},{16,20},{20,16},{24,28},{28,24},{1,5},{5... | collective-permute-start | bytes 1622024 | tf_op jit(solution)/shard_map/ppermute | solution.py:421
  4.1 6.2 %collective-permute-start.1 = (f32[4,264,128]{2,1,0:T(8,128)S(1)}, f32[4,264,128]{2,1,0:T(8,128)S(1)}, u32[]{:S(2)}, u32[]{:S(2)}) collective-permute-start(f32[4,264,128]{2,1,0:T(8,128)S(1)} %shard_map.78.keep_ref), channel_id=1, source_target_pairs={{0,4},{4,0},{8,12},{12,8},{16,20},{20,16},{24,28},{28,24},{1,5},{5... | collective-permute-start | bytes 1622024 | tf_op jit(solution)/shard_map/ppermute | solution.py:421
  5.2 8.1 %collective-permute-start.2 = (f32[200,128]{1,0:T(8,128)S(1)}, f32[200,128]{1,0:T(8,128)S(1)}, u32[]{:S(2)}, u32[]{:S(2)}) collective-permute-start(f32[200,128]{1,0:T(8,128)S(1)} %shard_map.80.rest_0_), channel_id=1, source_target_pairs={{0,24},{4,28},{8,16},{12,20},{16,8},{20,12},{24,0},{28,4},{1,25},{... | collective-permute-start | bytes 307208 | tf_op jit(solution)/shard_map/ppermute | solution.py:421
  9.6 4.9 %collective-permute-start.3 = (f32[200,128]{1,0:T(8,128)S(1)}, f32[200,128]{1,0:T(8,128)S(1)}, u32[]{:S(2)}, u32[]{:S(2)}) collective-permute-start(f32[200,128]{1,0:T(8,128)S(1)} %get-tuple-element.17.rest_0_), channel_id=1, source_target_pairs={{0,16},{4,20},{8,24},{12,28},{16,0},{20,4},{24,8},{28,12},{1,17},{... | collective-permute-start | bytes 307208 | tf_op jit(solution)/shard_map/ppermute | solution.py:421
  10.1 4.7 %collective-permute-start.4 = (f32[200,128]{1,0:T(8,128)S(1)}, f32[200,128]{1,0:T(8,128)S(1)}, u32[]{:S(2)}, u32[]{:S(2)}) collective-permute-start(f32[200,128]{1,0:T(8,128)S(1)} %get-tuple-element.18), channel_id=1, source_target_pairs={{0,8},{4,12},{8,0},{12,4},{16,24},{20,28},{24,16},{28,20},{1,9},{5... | collective-permute-start | bytes 307208 | tf_op jit(solution)/shard_map/ppermute | solution.py:421
  15.3 4.5 %collective-permute-start.5 = (f32[2,128]{1,0:T(2,128)S(1)}, f32[2,128]{1,0:T(2,128)S(1)}, u32[]{:S(2)}, u32[]{:S(2)}) collective-permute-start(f32[2,128]{1,0:T(2,128)S(1)} %get-tuple-element.19), channel_id=1, source_target_pairs={{0,24},{4,28},{8,16},{12,20},{16,8},{20,12},{24,0},{28,4},{1,25},{... | collective-permute-start | bytes 3080 | tf_op jit(solution)/shard_map/ppermute | solution.py:421
  17.4 3.6 %collective-permute-start.6 = (f32[2,128]{1,0:T(2,128)S(1)}, f32[2,128]{1,0:T(2,128)S(1)}, u32[]{:S(2)}, u32[]{:S(2)}) collective-permute-start(f32[2,128]{1,0:T(2,128)S(1)} %get-tuple-element.20), channel_id=1, source_target_pairs={{0,16},{4,20},{8,24},{12,28},{16,0},{20,4},{24,8},{28,12},{1,17},{... | collective-permute-start | bytes 3080 | tf_op jit(solution)/shard_map/ppermute | solution.py:421
  18.3 3.6 %collective-permute-start.7 = (f32[2,128]{1,0:T(2,128)S(1)}, f32[2,128]{1,0:T(2,128)S(1)}, u32[]{:S(2)}, u32[]{:S(2)}) collective-permute-start(f32[2,128]{1,0:T(2,128)S(1)} %get-tuple-element.21), channel_id=1, source_target_pairs={{0,8},{4,12},{8,0},{12,4},{16,24},{20,28},{24,16},{28,20},{1,9},{5... | collective-permute-start | bytes 3080 | tf_op jit(solution)/shard_map/ppermute | solution.py:421
  21.9 1.2 %collective-permute-start.8 = (f32[4,2,128]{2,1,0:T(2,128)S(1)}, f32[4,2,128]{2,1,0:T(2,128)S(1)}, u32[]{:S(2)}, u32[]{:S(2)}) collective-permute-start(f32[4,2,128]{2,1,0:T(2,128)S(1)} %shard_map.84.mine_ref), channel_id=1, source_target_pairs={{0,4},{4,0},{8,12},{12,8},{16,20},{20,16},{24,28},{28,24},{1,5},{5... | collective-permute-start | bytes 12296 | tf_op jit(solution)/shard_map/ppermute | solution.py:421
  21.9 1.2 %copy-start = (s32[4,8,128]{2,1,0:T(8,128)S(1)}, s32[4,8,128]{2,1,0:T(8,128)}, u32[]{:S(2)}) copy-start(s32[4,8,128]{2,1,0:T(8,128)} %phase_ref.1) | copy-start | bytes 49156
